TPU v7x, 32 devices: a whole 2x2x4 slice. The times are simulated.
32 devices in a mesh: ctx: 4 (over z), tp: 8 (over y, x, core).
Axes of the slice: x: 2, y: 2, z: 4, core: 2. Of those that a mesh axis runs over, the one named last changes fastest.
Arguments:
- tokens: bfloat16 [512, 8192], P('ctx', 'tp'), may hold values from -6 to 6
- inner_weight: bfloat16 [8192, 8192], P(None, 'tp'), may hold values from -0.0625 to 0.0625
- gate_weight: bfloat16 [8192, 8192], P(None, 'tp'), may hold values from -0.0625 to 0.0625
- conv_weight: float32 [4, 8192], P(None, 'tp'), may hold values from -3 to 3
- conv_bias: float32 [8192], P('tp'), may hold values from -3 to 3
- proj_weight: bfloat16 [8192, 544], P('tp'), may hold values from -0.0625 to 0.0625
- step_weight: bfloat16 [512, 8192], P(None, 'tp'), may hold values from -0.25 to 0.25
- step_bias: float32 [8192], P('tp'), may hold values from -4 to -0.5
- decay_rate: float32 [8192, 16], P('tp'), may hold values from 1e-05 to 2
- skip_gain: float32 [8192], P('tp'), may hold values from -1 to 2
- out_weight: bfloat16 [8192, 8192], P('tp'), may hold values from -0.09375 to 0.09375
- carried_state: float32 [8192, 16], P('tp'), may hold values from -6 to 6
Outputs:
- mixed: bfloat16 [512, 8192], P('ctx', 'tp')
- boundary_states: float32 [4, 8192, 16], P('ctx', 'tp')
All inputs are finite; a program needn't handle non-finite values.
Results may differ from a plain program's by a relative error of at most 0.025.
Values may be sent and summed in bfloat16 or wider, within the bound.
No kernel may reach another device: no remote copies, remote signals or barrier semaphores. Data moves between devices by JAX's collectives and lax.ppermute only.
A program may use at most 192 MiB of HBM per device.

v0:
```python
import functools
import math

import jax
import jax.numpy as jnp
from jax import lax
from jax.experimental import pallas as pl
from jax.experimental.pallas import tpu as pltpu
from jax.sharding import PartitionSpec as P


STATE = 16
DT_RANK = 512
LANES = 128
EDGE = 8
LOG2E = math.log2(math.e)
F32 = jnp.float32
BF16 = jnp.bfloat16
VMEM = pltpu.VMEM


def flip(value, axis, mask):
    peers = lax.axis_size(axis)
    return lax.ppermute(value, axis, [(i, i ^ mask) for i in range(peers)])


def cost(flops, nbytes, trans=0):
    return pl.CostEstimate(flops=flops, bytes_accessed=nbytes, transcendentals=trans)


PIECES = 2


def params(mib):
    return pltpu.CompilerParams(vmem_limit_bytes=mib << 20)


def far(value):
    return pltpu.with_memory_space_constraint(value, pltpu.HBM)


def tie(value, *others):
    return lax.optimization_barrier((value, *others))[0]


def peer(role):
    me = lax.axis_index("tp")
    core = me % 2
    if role >= 20:
        return me ^ (4 - 2 * core) ^ (role - 20)
    if role >= 10:
        return me ^ (2 + 2 * core) ^ (role - 10)
    return me ^ role


def row_copies(masks, weights, bufs, sem, feat):
    copies = []
    piece = feat // PIECES
    for q, (w, buf) in enumerate(zip(weights, bufs)):
        for i, mask in enumerate(masks):
            for p in range(PIECES):
                at = pl.multiple_of((peer(mask)) * feat + p * piece, piece)
                copies.append(
                    pltpu.make_async_copy(
                        w.at[pl.ds(at, piece), :],
                        buf.at[pl.ds(i * feat + p * piece, piece), :],
                        sem.at[(q * len(masks) + i) * PIECES + p],
                    )
                )
    return copies


def mm_kernel(masks, n_w, has_acc, *refs):
    n_b = len(masks)
    lhs = refs[:n_b]
    w = refs[n_b : n_b + n_w]
    refs = refs[n_b + n_w :]
    acc_in = refs[:n_w] if has_acc else None
    refs = refs[n_w:] if has_acc else refs
    outs = refs[:n_w]
    bufs = refs[n_w : 2 * n_w]
    sem = refs[2 * n_w]
    feat = lhs[0].shape[1]
    piece = feat // PIECES
    copies = row_copies(masks, w, bufs, sem, feat)
    for c in copies:
        c.start()
    step = 0
    for q in range(n_w):
        total = acc_in[q][...] if has_acc else None
        for i in range(n_b):
            for p in range(PIECES):
                copies[step].wait()
                step += 1
                part = jnp.dot(
                    lhs[i][:, p * piece : (p + 1) * piece],
                    bufs[q][i * feat + p * piece : i * feat + (p + 1) * piece, :],
                    preferred_element_type=F32,
                )
                total = part if total is None else total + part
        outs[q][...] = total


def mm(blocks, masks, weights, accs):
    rows, feat = blocks[0].shape
    ch = weights[0].shape[1]
    n_w = len(weights)
    has_acc = accs is not None
    vm = pl.BlockSpec(memory_space=VMEM)
    depth = feat * len(blocks)
    return pl.pallas_call(
        functools.partial(mm_kernel, masks, n_w, has_acc),
        in_specs=[vm] * len(blocks)
        + [pl.BlockSpec(memory_space=pltpu.HBM)] * n_w
        + [vm] * (n_w if has_acc else 0),
        out_specs=[vm] * n_w,
        out_shape=[jax.ShapeDtypeStruct((rows, ch), F32)] * n_w,
        scratch_shapes=[VMEM((depth, ch), BF16)] * n_w
        + [pltpu.SemaphoreType.DMA((n_w * len(blocks) * PIECES,))],
        compiler_params=params(12),
        cost_estimate=cost(2 * rows * depth * ch * n_w, 2 * depth * ch * n_w),
    )(*blocks, *map(far, weights), *(accs or ()))


def fetch_kernel(masks, n_w, *refs):
    w = refs[:n_w]
    outs = refs[n_w + 1 : 2 * n_w + 1]
    sem = refs[2 * n_w + 1]
    copies = row_copies(masks, w, outs, sem, outs[0].shape[0] // len(masks))
    for c in copies:
        c.start()
    for c in copies:
        c.wait()


def fetch(masks, weights, feat, dep):
    ch = weights[0].shape[1]
    n_w = len(weights)
    depth = feat * len(masks)
    return pl.pallas_call(
        functools.partial(fetch_kernel, masks, n_w),
        in_specs=[pl.BlockSpec(memory_space=pltpu.HBM)] * n_w + [pl.BlockSpec(memory_space=VMEM)],
        out_specs=[pl.BlockSpec(memory_space=VMEM)] * n_w,
        out_shape=[VMEM((depth, ch), BF16)] * n_w,
        scratch_shapes=[pltpu.SemaphoreType.DMA((n_w * len(masks) * PIECES,))],
        compiler_params=params(1),
        cost_estimate=cost(0, 2 * depth * ch * n_w),
    )(*map(far, weights), dep)


def last_kernel(edge, a_ref, b_ref, w_ref, acc_ref, out_ref, edge_ref=None):
    feat = a_ref.shape[1]
    total = acc_ref[...] + jnp.dot(a_ref[...], w_ref[:feat, :], preferred_element_type=F32)
    total = total + jnp.dot(b_ref[...], w_ref[feat:, :], preferred_element_type=F32)
    out_ref[...] = total.astype(BF16)
    if edge:
        edge_ref[...] = total[total.shape[0] - edge :].astype(BF16)


def finish(a, b, w, acc, edge=0):
    rows, feat = a.shape
    ch = w.shape[1]
    vm = pl.BlockSpec(memory_space=VMEM)
    shapes = [jax.ShapeDtypeStruct((rows, ch), BF16)]
    if edge:
        shapes.append(jax.ShapeDtypeStruct((edge, ch), BF16))
    return pl.pallas_call(
        functools.partial(last_kernel, edge),
        in_specs=[vm] * 4,
        out_specs=[vm] * len(shapes),
        out_shape=shapes,
        compiler_params=params(4),
        cost_estimate=cost(4 * rows * feat * ch, 4 * feat * ch),
    )(a, b, pltpu.with_memory_space_constraint(w, VMEM), acc)


def conv_kernel(split, x_ref, tail_ref, w_ref, b_ref, pw_ref, conv_ref, send_ref, keep_ref, pad, acc):
    rows, ch = x_ref.shape
    taps = w_ref.shape[0]
    edge = tail_ref.shape[0]
    pad[0:edge, :] = tail_ref[...].astype(F32)
    pad[edge : edge + rows, :] = x_ref[...].astype(F32)
    total = jnp.broadcast_to(b_ref[...], (rows, ch))
    for k in range(taps):
        total = total + w_ref[k : k + 1, :] * pad[edge - taps + 1 + k : edge - taps + 1 + k + rows, :]
    conv = (total * jax.nn.sigmoid(total)).astype(BF16)
    conv_ref[...] = conv
    proj = lax.dot_general(conv, pw_ref[...], (((1,), (1,)), ((), ())), preferred_element_type=F32)
    if split:
        half = rows // 2
        core = lax.axis_index("tp") % 2
        acc[...] = proj
        send_ref[...] = acc[pl.ds(pl.multiple_of((1 - core) * half, half), half), :].astype(BF16)
        keep_ref[...] = acc[pl.ds(pl.multiple_of(core * half, half), half), :]
    else:
        keep_ref[...] = proj.astype(keep_ref.dtype)
        send_ref[...] = jnp.zeros(send_ref.shape, send_ref.dtype)


def conv_proj(x, tail, conv_w, conv_b, proj_wt, split):
    rows, ch = x.shape
    wide = proj_wt.shape[0]
    half = rows // 2 if split else rows
    shalf = half if split else 8
    return pl.pallas_call(
        functools.partial(conv_kernel, split),
        in_specs=[pl.BlockSpec(memory_space=VMEM)] * 5,
        out_specs=[pl.BlockSpec(memory_space=VMEM)] * 3,
        out_shape=[
            jax.ShapeDtypeStruct((rows, ch), BF16),
            jax.ShapeDtypeStruct((shalf, wide), BF16),
            jax.ShapeDtypeStruct((half, wide), F32 if split else BF16),
        ],
        scratch_shapes=[VMEM((tail.shape[0] + rows, ch), F32), VMEM((rows, wide), F32)],
        compiler_params=params(6),
        cost_estimate=cost(2 * rows * ch * wide, 2 * ch * wide),
    )(x, tail, conv_w, conv_b, proj_wt)


def spread(ref, value, groups):
    count = value.shape[0]
    for j in range(groups):
        ref[pl.ds(j, count, stride=groups), :] = value[:, j * LANES : (j + 1) * LANES]


def collect(ref, count, groups):
    return jnp.concatenate([ref[pl.ds(j, count, stride=groups), :] for j in range(groups)], axis=1)


def line(ref, at, groups):
    return jnp.broadcast_to(ref[pl.ds(at, 1), :], (groups, LANES))


def scan_kernel(
    split, *refs,
):
    n_p = 2 if split else 1
    parts = refs[:n_p]
    (conv_ref, sw_ref, sb_ref, decay_ref, carried_ref,
     end_ref, y_ref, cum_ref, c_ref,
     proj_s, step_s, drive_s, nd_s, h_s, b_ref) = refs[n_p:]
    rows, ch = conv_ref.shape
    groups = ch // LANES
    if split:
        half = rows // 2
        core = lax.axis_index("tp") % 2
        proj_s[pl.ds(pl.multiple_of(core * half, half), half), :] = parts[0][...].astype(F32)
        proj_s[pl.ds(pl.multiple_of((1 - core) * half, half), half), :] = parts[1][...].astype(F32)
    else:
        proj_s[...] = parts[0][...].astype(F32)
    for n in range(STATE):
        for ref, at in ((b_ref, DT_RANK + n), (c_ref, DT_RANK + STATE + n)):
            ref[pl.ds(n, rows, stride=STATE), :] = jnp.broadcast_to(
                proj_s[:, at : at + 1], (rows, LANES)
            )
    low = proj_s[:, :DT_RANK].astype(BF16)
    pre = jnp.dot(low, sw_ref[...], preferred_element_type=F32) + sb_ref[...]
    step = jnp.maximum(pre, 0.0) + jnp.log1p(jnp.exp(-jnp.abs(pre)))
    spread(step_s, step, groups)
    spread(drive_s, step * conv_ref[...].astype(F32), groups)
    spread(nd_s, decay_ref[...] * -LOG2E, groups)
    lead = jnp.where(lax.axis_index("ctx") == 0, 1.0, 0.0)
    spread(h_s, carried_ref[...] * lead, groups)
    nd = [nd_s[n * groups : (n + 1) * groups, :] for n in range(STATE)]
    h0 = tuple(h_s[n * groups : (n + 1) * groups, :] for n in range(STATE))

    def body(t, carry):
        h, total = carry
        at = pl.ds(pl.multiple_of(t * groups, groups), groups)
        dt = step_s[at, :]
        u = drive_s[at, :]
        total = total + dt
        cum_ref[at, :] = total
        y = None
        new = []
        for n in range(STATE):
            a = jnp.exp2(dt * nd[n])
            v = a * h[n] + u * line(b_ref, t * STATE + n, groups)
            new.append(v)
            term = v * line(c_ref, t * STATE + n, groups)
            y = term if y is None else y + term
        y_ref[at, :] = y
        return tuple(new), total

    h, total = lax.fori_loop(0, rows, body, (h0, jnp.zeros((groups, LANES), F32)), unroll=8)
    for n in range(STATE):
        h_s[n * groups : (n + 1) * groups, :] = h[n]
    end_ref[0:STATE, :] = collect(h_s, STATE, groups)
    nd_s[0:groups, :] = total
    end_ref[STATE : STATE + 1, :] = collect(nd_s, 1, groups)


def scan(parts, conv_x, step_w, step_b, decay_t, carried_t):
    rows, ch = conv_x.shape
    groups = ch // LANES
    vm = pl.BlockSpec(memory_space=VMEM)
    return pl.pallas_call(
        functools.partial(scan_kernel, len(parts) == 2),
        in_specs=[vm] * (5 + len(parts)),
        out_specs=[vm] * 4,
        out_shape=[
            jax.ShapeDtypeStruct((STATE + 1, ch), F32),
            jax.ShapeDtypeStruct((rows * groups, LANES), F32),
            jax.ShapeDtypeStruct((rows * groups, LANES), F32),
            jax.ShapeDtypeStruct((rows * STATE, LANES), F32),
        ],
        scratch_shapes=[
            VMEM((rows, parts[0].shape[1]), F32),
            VMEM((rows * groups, LANES), F32),
            VMEM((rows * groups, LANES), F32),
            VMEM((STATE * groups, LANES), F32),
            VMEM((STATE * groups, LANES), F32),
            VMEM((rows * STATE, LANES), F32),
        ],
        compiler_params=params(8),
        cost_estimate=cost(rows * ch * STATE * 8, rows * ch * 8, rows * ch * STATE),
    )(*parts, conv_x, step_w, step_b, decay_t, carried_t)


def add_kernel(*refs):
    total = refs[0][...].astype(F32)
    for r in refs[1:-1]:
        total = total + r[...].astype(F32)
    refs[-1][...] = total.astype(BF16)


def add(*values):
    vm = pl.BlockSpec(memory_space=VMEM)
    shape = values[0].shape
    size = shape[0] * shape[1]
    return pl.pallas_call(
        add_kernel,
        in_specs=[vm] * len(values),
        out_specs=vm,
        out_shape=jax.ShapeDtypeStruct(shape, BF16),
        compiler_params=params(3),
        cost_estimate=cost(size * len(values), 2 * size * len(values)),
    )(*values)


def add_pair_kernel(a_ref, b_ref, *outs):
    for i, o in enumerate(outs):
        o[...] = (a_ref[i].astype(F32) + b_ref[i].astype(F32)).astype(BF16)


def add_pair(a, b):
    vm = pl.BlockSpec(memory_space=VMEM)
    n, rows, feat = a.shape
    return pl.pallas_call(
        add_pair_kernel,
        in_specs=[vm, vm],
        out_specs=[vm] * n,
        out_shape=[jax.ShapeDtypeStruct((rows, feat), BF16)] * n,
        compiler_params=params(3),
        cost_estimate=cost(a.size, 6 * a.size),
    )(a, b)


def merge_kernel(bit, first, decay_ref, group_ref, got_ref, *refs):
    ent_ref = None if first else refs[0]
    new_ref, out_ref = refs[-2:]
    upper = (lax.axis_index("ctx") // bit) % 2 == 1
    decay = decay_ref[...]
    gh, gs = got_ref[:STATE, :], got_ref[STATE:, :]
    mh, ms = group_ref[:STATE, :], group_ref[STATE:, :]
    entering = gh if first else jnp.exp(-decay * ent_ref[STATE:, :]) * gh + ent_ref[:STATE, :]
    before = gs if first else ent_ref[STATE:, :] + gs
    keep_h = jnp.zeros_like(gh) if first else ent_ref[:STATE, :]
    keep_s = jnp.zeros_like(gs) if first else ent_ref[STATE:, :]
    out_ref[:STATE, :] = jnp.where(upper, entering, keep_h)
    out_ref[STATE:, :] = jnp.where(upper, before, keep_s)
    low = jnp.where(upper, gh, mh)
    high = jnp.where(upper, mh, gh)
    high_s = jnp.where(upper, ms, gs)
    new_ref[:STATE, :] = jnp.exp(-decay * high_s) * low + high
    new_ref[STATE:, :] = ms + gs


def merge(bit, decay_t, group, got, ent):
    vm = pl.BlockSpec(memory_space=VMEM)
    first = ent is None
    extra = () if first else (ent,)
    return pl.pallas_call(
        functools.partial(merge_kernel, bit, first),
        in_specs=[vm] * (3 + len(extra)),
        out_specs=[vm, vm],
        out_shape=[jax.ShapeDtypeStruct(group.shape, F32)] * 2,
        compiler_params=params(3),
        cost_estimate=cost(group.size * 8, group.size * 16),
    )(decay_t, group, got, *extra)


def gate_kernel(bit, first, y_ref, cum_ref, c_ref, end_ref, got_ref, decay_ref, conv_ref, skip_ref, gate_ref, *refs):
    ent_ref = None if first else refs[0]
    out_ref, bound_ref, nd_s, e_s, y_s = refs[-5:]
    rows, ch = conv_ref.shape
    groups = ch // LANES
    decay = decay_ref[...]
    upper = (lax.axis_index("ctx") // bit) % 2 == 1
    got = got_ref[:STATE, :]
    if first:
        entering = jnp.where(upper, got, jnp.zeros_like(got))
    else:
        kept = ent_ref[:STATE, :]
        entering = jnp.where(upper, jnp.exp(-decay * ent_ref[STATE:, :]) * got + kept, kept)
    bound_ref[...] = jnp.exp(-decay * end_ref[STATE:, :]) * entering + end_ref[:STATE, :]
    spread(nd_s, decay * -LOG2E, groups)
    spread(e_s, entering, groups)
    nd = [nd_s[n * groups : (n + 1) * groups, :] for n in range(STATE)]
    ent = [e_s[n * groups : (n + 1) * groups, :] for n in range(STATE)]

    def body(t, carry):
        at = pl.ds(pl.multiple_of(t * groups, groups), groups)
        total = cum_ref[at, :]
        y = y_ref[at, :]
        for n in range(STATE):
            y = y + jnp.exp2(total * nd[n]) * ent[n] * line(c_ref, t * STATE + n, groups)
        y_s[at, :] = y
        return carry

    lax.fori_loop(0, rows, body, 0, unroll=8)
    y = collect(y_s, rows, groups)
    gate = gate_ref[...].astype(BF16).astype(F32)
    out = (y + skip_ref[...] * conv_ref[...].astype(F32)) * (gate * jax.nn.sigmoid(gate))
    out_ref[...] = out.astype(BF16)


def gating(bit, y, cum, bc, end, got, ent, decay_t, conv_x, skip, gate):
    rows, ch = conv_x.shape
    groups = ch // LANES
    vm = pl.BlockSpec(memory_space=VMEM)
    first = ent is None
    extra = () if first else (ent,)
    return pl.pallas_call(
        functools.partial(gate_kernel, bit, first),
        in_specs=[vm] * (9 + len(extra)),
        out_specs=[vm, vm],
        out_shape=[
            jax.ShapeDtypeStruct((rows, ch), BF16),
            jax.ShapeDtypeStruct((STATE, ch), F32),
        ],
        scratch_shapes=[
            VMEM((STATE * groups, LANES), F32),
            VMEM((STATE * groups, LANES), F32),
            VMEM((rows * groups, LANES), F32),
        ],
        compiler_params=params(8),
        cost_estimate=cost(rows * ch * STATE * 6, rows * ch * 8, rows * ch * STATE),
    )(y, cum, bc, end, got, decay_t, conv_x, skip, gate, *extra)


def col_copies(masks, w, buf, sem, feat):
    copies = []
    for i, mask in enumerate(masks):
        at = pl.multiple_of((peer(mask)) * feat, feat)
        copies.append(
            pltpu.make_async_copy(w.at[:, pl.ds(at, feat)], buf.at[i], sem.at[i])
        )
    return copies


def cols_kernel(masks, w_ref, dep_ref, out_ref, sem):
    copies = col_copies(masks, w_ref, out_ref, sem, out_ref.shape[2])
    for c in copies:
        c.start()
    for c in copies:
        c.wait()


def fetch_cols(masks, weight, feat, dep):
    ch = weight.shape[0]
    return pl.pallas_call(
        functools.partial(cols_kernel, masks),
        in_specs=[
            pl.BlockSpec(memory_space=pltpu.HBM),
            pl.BlockSpec(memory_space=VMEM),
        ],
        out_specs=pl.BlockSpec(memory_space=VMEM),
        out_shape=VMEM((len(masks), ch, feat), BF16),
        scratch_shapes=[pltpu.SemaphoreType.DMA((len(masks),))],
        compiler_params=params(1),
        cost_estimate=cost(0, 2 * ch * feat * len(masks)),
    )(far(weight), dep)


def out_held_kernel(g_ref, w_ref, o_ref):
    for i in range(w_ref.shape[0]):
        o_ref[i] = jnp.dot(g_ref[...], w_ref[i], preferred_element_type=F32).astype(o_ref.dtype)


def out_held(gated, cols):
    rows, ch = gated.shape
    n, _, feat = cols.shape
    vm = pl.BlockSpec(memory_space=VMEM)
    return pl.pallas_call(
        out_held_kernel,
        in_specs=[vm, vm],
        out_specs=vm,
        out_shape=jax.ShapeDtypeStruct((n, rows, feat), BF16),
        compiler_params=params(4),
        cost_estimate=cost(2 * rows * ch * feat * n, 2 * ch * feat * n),
    )(gated, pltpu.with_memory_space_constraint(cols, VMEM))


def out_kernel(masks, g_ref, w_ref, o_ref, buf, sem):
    copies = col_copies(masks, w_ref, buf, sem, o_ref.shape[2])
    for c in copies:
        c.start()
    for i, c in enumerate(copies):
        c.wait()
        o_ref[i] = jnp.dot(g_ref[...], buf[i], preferred_element_type=F32).astype(o_ref.dtype)


def out_blocks(gated, weight, masks, feat):
    rows, ch = gated.shape
    n = len(masks)
    vm = pl.BlockSpec(memory_space=VMEM)
    return pl.pallas_call(
        functools.partial(out_kernel, masks),
        in_specs=[vm, pl.BlockSpec(memory_space=pltpu.HBM)],
        out_specs=vm,
        out_shape=jax.ShapeDtypeStruct((n, rows, feat), BF16),
        scratch_shapes=[VMEM((n, ch, feat), BF16), pltpu.SemaphoreType.DMA((n,))],
        compiler_params=params(12),
        cost_estimate=cost(2 * rows * ch * feat * n, 2 * ch * feat * n),
    )(gated, far(weight))


def on_device(
    tokens, inner_weight, gate_weight, conv_weight, conv_bias, proj_weight, step_weight,
    step_bias, decay_rate, skip_gain, out_weight, carried_state,
):
    rows, feat = tokens.shape
    n_tp = lax.axis_size("tp")
    n_ctx = lax.axis_size("ctx")
    square = n_tp == 8
    shift = [(i, i + 1) for i in range(n_ctx - 1)]
    proj_wt = proj_weight.T
    decay_t = decay_rate.T
    carried_t = carried_state.T

    if square:
        p1 = flip(tokens, "tp", 1)
        px = flip(tokens, "tp", 2)
        py = flip(tokens, "tp", 4)
        pd = flip(tokens, "tp", 6)
        inner, gate_acc = mm([tokens, p1], [0, 1], [inner_weight, gate_weight], None)
        px = tie(px, inner)
        py = tie(py, inner)
        qx = flip(px, "tp", 1)
        qy = flip(py, "tp", 1)
        inner, = mm([px, qx, py, qy], [2, 3, 4, 5], [inner_weight], [inner])
        pd = tie(pd, inner)
        qd = flip(pd, "tp", 1)
        inner_d, = fetch([6, 7], [inner_weight], feat, pd)
        qd = tie(qd, inner_d)
        inner_x, edge_x = finish(pd, qd, inner_d, inner, EDGE)
    else:
        piece = lax.all_gather(tokens, "tp", axis=1, tiled=True)
        inner_x = jnp.dot(piece, inner_weight, preferred_element_type=F32).astype(BF16)
        gate_acc = jnp.dot(piece, gate_weight, preferred_element_type=F32)
        edge_x = inner_x[rows - EDGE :]

    tail = lax.ppermute(edge_x, "ctx", shift)
    if square:
        gate_acc, = mm([px], [2], [gate_weight], [tie(gate_acc, edge_x)])
        tail = tie(tail, gate_acc)
    conv_x, send, keep = conv_proj(
        inner_x, tail, conv_weight, conv_bias[None, :], proj_wt, square
    )
    if square:
        part = add(keep, flip(send, "tp", 1))
        quarter = [flip(part, "tp", m) for m in (2, 4, 6)]
        cols_away = fetch_cols([7, 21, 11, 1], out_weight, feat, part)
        quarter = [tie(v, cols_away) for v in quarter]
        mine = add(part, *quarter)
        parts = (mine, flip(mine, "tp", 1))
    else:
        parts = (lax.psum(keep, "tp"),)
    end, y, cum, bc = scan(
        parts, conv_x, step_weight, step_bias[None, :], decay_t, carried_t
    )

    group, ent, bit = end, None, 1
    while bit * 2 < n_ctx:
        got = flip(group, "ctx", bit)
        if square and bit == 1:
            gate_acc, = mm([qx, py, qy], [3, 4, 5], [gate_weight], [tie(gate_acc, group)])
            got = tie(got, gate_acc)
        group, ent = merge(bit, decay_t, group, got, ent)
        bit *= 2
    pairs = [(i, i ^ bit) for i in range(n_ctx) if (i // bit) % 2 == 0]
    got = lax.ppermute(group, "ctx", pairs)
    if square:
        gate_acc, = mm([pd, qd], [6, 7], [gate_weight], [tie(gate_acc, group)])
        got = tie(got, gate_acc)
    gated, bound = gating(
        bit, y, cum, bc, end, got, ent, decay_t, conv_x, skip_gain[None, :], gate_acc
    )
    if square:
        away = out_held(gated, cols_away)
        got = flip(away, "tp", 1)
        near = out_blocks(gated, out_weight, [6, 10, 20, 0], feat)
        sd, sf, ss, so = add_pair(near, got)
        to_first = [(i, i ^ (2 + 2 * (i % 2))) for i in range(n_tp)]
        to_second = [(i, i ^ (4 - 2 * (i % 2))) for i in range(n_tp)]
        rd = lax.ppermute(sd, "tp", to_first)
        rf = lax.ppermute(sf, "tp", to_first)
        rs = lax.ppermute(add(ss, rd), "tp", to_second)
        mixed = add(so, rf, rs)
    else:
        partial = jnp.dot(gated, out_weight, preferred_element_type=F32).astype(BF16)
        mixed = lax.psum_scatter(partial, "tp", scatter_dimension=1, tiled=True)
    return (mixed, bound.T[None])


def solution(mesh):
    in_specs = (
        P("ctx", "tp"), P(None, "tp"), P(None, "tp"), P(None, "tp"), P("tp"), P("tp", None),
        P(None, "tp"), P("tp"), P("tp", None), P("tp"), P("tp", None), P("tp", None),
    )
    out_specs = (P("ctx", "tp"), P("ctx", "tp", None))
    return jax.shard_map(
        on_device, mesh=mesh, in_specs=in_specs, out_specs=out_specs, check_vma=False
    )
```

profile of v0, /device:TPU:0, one launch (start us, length us, event | category | flops | bytes accessed | tf_op | source)
XLA Modules:
  0.0 79.1 jit_solution(14447537743010999980)
XLA Ops:
  0.6 0.6 collective-permute-start.2
  1.2 2.6 %collective-permute-start.4 = (bf16[128,1024]{1,0:T(8,128)(2,1)}, bf16[128,1024]{1,0:T(8,128)(2,1)S(1)}, u32[]{:S(2)}, u32[]{:S(2)}) collective-permute-start(bf16[128,1024]{1,0:T(8,128)(2,1)} %refs_0_.2), channel_id=1, source_target_pairs={{0,4},{1,5},{2,6},{3,7},{4,0},{5,1},{6,2},{7,3},{8,12},{9,13},{10,... | collective-permute-start | bytes 786440 | tf_op jit(solution)/shard_map/ppermute | solution.py:24
  3.8 1.5 %collective-permute-start.1 = (bf16[128,1024]{1,0:T(8,128)(2,1)}, bf16[128,1024]{1,0:T(8,128)(2,1)S(1)}, u32[]{:S(2)}, u32[]{:S(2)}) collective-permute-start(bf16[128,1024]{1,0:T(8,128)(2,1)} %refs_0_.2), channel_id=1, source_target_pairs={{0,2},{1,3},{2,0},{3,1},{4,6},{5,7},{6,4},{7,5},{8,10},{9,11},{10,... | collective-permute-start | bytes 786440 | tf_op jit(solution)/shard_map/ppermute | solution.py:24
  5.3 1.0 %copy-done.1 = bf16[128,1024]{1,0:T(8,128)(2,1)S(1)} copy-done((bf16[128,1024]{1,0:T(8,128)(2,1)S(1)}, bf16[128,1024]{1,0:T(8,128)(2,1)}, u32[]{:S(2)}) %copy-start.1) | copy-done | bytes 262168
  6.2 3.8 %shard_map.131 = (f32[128,1024]{1,0:T(8,128)S(1)}, f32[128,1024]{1,0:T(8,128)S(1)}) custom-call(bf16[128,1024]{1,0:T(8,128)(2,1)S(1)} %copy-done.1, bf16[128,1024]{1,0:T(8,128)(2,1)S(1)} %collective-permute-done.2.refs_1_, bf16[8192,1024]{1,0:T(8,128)(2,1)} %refs_0_.3, bf16[8192,1024]{1,0:T(8,128)(2,1)} %refs_2_.3), custom_call_target="tpu_custom_call" | custom-call | flops 1073741824 | bytes 8388608 | tf_op jit(solution)/shard_map/pallas_call | solution.py:111
  10.1 0.8 %collective-permute-done.4.refs_2_.refs_1_ = bf16[128,1024]{1,0:T(8,128)(2,1)S(1)} collective-permute-done((bf16[128,1024]{1,0:T(8,128)(2,1)}, bf16[128,1024]{1,0:T(8,128)(2,1)S(1)}, u32[]{:S(2)}, u32[]{:S(2)}) %collective-permute-start.4) | collective-permute-done | bytes 262176 | tf_op jit(solution)/shard_map/ppermute | solution.py:24
  10.9 1.5 %collective-permute-done.1.refs_0_ = bf16[128,1024]{1,0:T(8,128)(2,1)S(1)} collective-permute-done((bf16[128,1024]{1,0:T(8,128)(2,1)}, bf16[128,1024]{1,0:T(8,128)(2,1)S(1)}, u32[]{:S(2)}, u32[]{:S(2)}) %collective-permute-start.1) | collective-permute-done | bytes 262176 | tf_op jit(solution)/shard_map/ppermute | solution.py:24
  12.3 0.5 collective-permute-start.5
  12.9 1.4 %collective-permute-start = (bf16[128,1024]{1,0:T(8,128)(2,1)S(1)}, bf16[128,1024]{1,0:T(8,128)(2,1)S(1)}, u32[]{:S(2)}, u32[]{:S(2)}) collective-permute-start(bf16[128,1024]{1,0:T(8,128)(2,1)S(1)} %copy-done.1), channel_id=1, source_target_pairs={{0,6},{1,7},{2,4},{3,5},{4,2},{5,3},{6,0},{7,1},{8,14},{9,15},{10,... | collective-permute-start | bytes 786440 | tf_op jit(solution)/shard_map/ppermute | solution.py:24
  14.3 3.8 %shard_map.132.acc_ref = f32[128,1024]{1,0:T(8,128)S(1)} custom-call(bf16[128,1024]{1,0:T(8,128)(2,1)S(1)} %collective-permute-done.1.refs_0_, bf16[128,1024]{1,0:T(8,128)(2,1)S(1)} %collective-permute-done.3.refs_1_.refs_0_, bf16[128,1024]{1,0:T(8,128)(2,1)S(1)} %collective-permute-done.4.refs_2_.refs_1_, ...), custom_call_target="tpu_custom_call" | custom-call | flops 1073741824 | bytes 8388608 | tf_op jit(solution)/shard_map/pallas_call | solution.py:111
  18.1 3.9 %collective-permute-done.refs_1_.a_ref.refs_0_ = bf16[128,1024]{1,0:T(8,128)(2,1)S(1)} collective-permute-done((bf16[128,1024]{1,0:T(8,128)(2,1)S(1)}, bf16[128,1024]{1,0:T(8,128)(2,1)S(1)}, u32[]{:S(2)}, u32[]{:S(2)}) %collective-permute-start) | collective-permute-done | bytes 262176 | tf_op jit(solution)/shard_map/ppermute | solution.py:24
  22.0 2.2 %shard_map.133.w_ref = bf16[2048,1024]{1,0:T(8,128)(2,1)S(1)} custom-call(bf16[8192,1024]{1,0:T(8,128)(2,1)} %refs_0_.3, bf16[128,1024]{1,0:T(8,128)(2,1)S(1)} %collective-permute-done.refs_1_.a_ref.refs_0_), custom_call_target="tpu_custom_call" | custom-call | bytes 4194304 | tf_op jit(solution)/shard_map/pallas_call | solution.py:140
  24.2 0.0 copy-start
  24.2 0.7 shard_map.134
  25.0 3.5 %collective-permute-start.7 = (bf16[8,1024]{1,0:T(8,128)(2,1)S(1)}, bf16[8,1024]{1,0:T(8,128)(2,1)S(1)}, u32[]{:S(2)}, u32[]{:S(2)}) collective-permute-start(bf16[8,1024]{1,0:T(8,128)(2,1)S(1)} %get-tuple-element.40), channel_id=1, source_target_pairs={{0,8},{8,16},{16,24},{1,9},{9,17},{17,25},{2,10},{10,18},{18,26},{... | collective-permute-start | bytes 49160 | tf_op jit(solution)/shard_map/ppermute | solution.py:564
  28.4 1.9 %shard_map.135.refs_4_ = f32[128,1024]{1,0:T(8,128)S(1)} custom-call(bf16[128,1024]{1,0:T(8,128)(2,1)S(1)} %collective-permute-done.1.refs_0_, bf16[8192,1024]{1,0:T(8,128)(2,1)} %refs_2_.3, f32[128,1024]{1,0:T(8,128)S(1)} %get-tuple-element.42.refs_2_), custom_call_target="tpu_custom_call" | custom-call | flops 268435456 | bytes 2097152 | tf_op jit(solution)/shard_map/pallas_call | solution.py:111
  30.3 0.0 copy-start.2
  30.3 0.0 copy-start.5
  30.4 0.0 copy-start.7
  30.4 0.9 %shard_map.136 = (bf16[128,1024]{1,0:T(8,128)(2,1)S(1)}, bf16[64,544]{1,0:T(8,128)(2,1)S(1)}, f32[64,544]{1,0:T(8,128)S(1)}) custom-call(bf16[128,1024]{1,0:T(8,128)(2,1)S(1)} %get-tuple-element.39.x_ref, bf16[8,1024]{1,0:T(8,128)(2,1)S(1)} %collective-permute-done.7.tail_ref, f32[4,1024]{1,0:T(4,128)S(1)} %copy-done.3, f32[1,1024]{1,0:T(1,128)S(1)} %bitcast.13, ...), custom_call_target="tpu_custom_call" | custom-call | flops 142606336 | bytes 1114112 | tf_op jit(solution)/shard_map/pallas_call | solution.py:205
  31.3 0.3 collective-permute-start.8
  31.6 1.0 %collective-permute-done.8.refs_1_ = bf16[64,544]{1,0:T(8,128)(2,1)S(1)} collective-permute-done((bf16[64,544]{1,0:T(8,128)(2,1)S(1)}, bf16[64,544]{1,0:T(8,128)(2,1)S(1)}, u32[]{:S(2)}, u32[]{:S(2)}) %collective-permute-start.8) | collective-permute-done | bytes 69664 | tf_op jit(solution)/shard_map/ppermute | solution.py:24
  32.7 1.5 %collective-permute-start.11 = (bf16[64,544]{1,0:T(8,128)(2,1)S(1)}, bf16[64,544]{1,0:T(8,128)(2,1)S(1)}, u32[]{:S(2)}, u32[]{:S(2)}) collective-permute-start(bf16[64,544]{1,0:T(8,128)(2,1)S(1)} %shard_map.137.dep_ref.refs_0_), channel_id=1, source_target_pairs={{0,6},{1,7},{2,4},{3,5},{4,2},{5,3},{6,0},{7,1},{8,14},{9,15},{10,... | collective-permute-start | bytes 208904 | tf_op jit(solution)/shard_map/ppermute | solution.py:24
  34.2 1.5 %collective-permute-start.10 = (bf16[64,544]{1,0:T(8,128)(2,1)S(1)}, bf16[64,544]{1,0:T(8,128)(2,1)S(1)}, u32[]{:S(2)}, u32[]{:S(2)}) collective-permute-start(bf16[64,544]{1,0:T(8,128)(2,1)S(1)} %shard_map.137.dep_ref.refs_0_), channel_id=1, source_target_pairs={{0,4},{1,5},{2,6},{3,7},{4,0},{5,1},{6,2},{7,3},{8,12},{9,13},{10,... | collective-permute-start | bytes 208904 | tf_op jit(solution)/shard_map/ppermute | solution.py:24
  35.7 0.5 collective-permute-start.9
  36.2 3.5 %shard_map.138.w_ref = bf16[4,1024,1024]{2,1,0:T(8,128)(2,1)S(1)} custom-call(bf16[1024,8192]{1,0:T(8,128)(2,1)} %w_ref.5, bf16[64,544]{1,0:T(8,128)(2,1)S(1)} %shard_map.137.dep_ref.refs_0_), custom_call_target="tpu_custom_call" | custom-call | bytes 8388608 | tf_op jit(solution)/shard_map/pallas_call | solution.py:472
  39.8 0.2 collective-permute-done.10.refs_2_
  40.0 0.2 collective-permute-done.9.refs_1_
  40.2 0.1 collective-permute-start.12
  40.3 1.3 %collective-permute-done.12.refs_1_ = bf16[64,544]{1,0:T(8,128)(2,1)S(1)} collective-permute-done((bf16[64,544]{1,0:T(8,128)(2,1)S(1)}, bf16[64,544]{1,0:T(8,128)(2,1)S(1)}, u32[]{:S(2)}, u32[]{:S(2)}) %collective-permute-start.12) | collective-permute-done | bytes 69664 | tf_op jit(solution)/shard_map/ppermute | solution.py:24
  41.5 3.5 %shard_map.140 = (f32[17,1024]{1,0:T(8,128)S(1)}, f32[1024,128]{1,0:T(8,128)S(1)}, f32[1024,128]{1,0:T(8,128)S(1)}, f32[2048,128]{1,0:T(8,128)S(1)}) custom-call(bf16[64,544]{1,0:T(8,128)(2,1)S(1)} %shard_map.139.refs_0_, bf16[64,544]{1,0:T(8,128)(2,1)S(1)} %collective-permute-done.12.refs_1_, bf16[128,1024]{1,0:T(8,128)(2,1)S(1)} %get-tuple-element.49.refs_2_.conv_ref, ...), custom_call_target="tpu_custom_call" | custom-call | flops 16777216 | bytes 1048576 | tf_op jit(solution)/shard_map/pallas_call | solution.py:297
  45.1 1.8 %collective-permute-start.13 = (f32[17,1024]{1,0:T(8,128)S(1)}, f32[17,1024]{1,0:T(8,128)S(1)}, u32[]{:S(2)}, u32[]{:S(2)}) collective-permute-start(f32[17,1024]{1,0:T(8,128)S(1)} %get-tuple-element.53.group_ref.end_ref), channel_id=1, source_target_pairs={{0,8},{8,0},{16,24},{24,16},{1,9},{9,1},{17,25},{25,17},{2,10},{10... | collective-permute-start | bytes 208904 | tf_op jit(solution)/shard_map/ppermute | solution.py:24
  46.9 3.2 %shard_map.141.refs_3_ = f32[128,1024]{1,0:T(8,128)S(1)} custom-call(bf16[128,1024]{1,0:T(8,128)(2,1)S(1)} %collective-permute-done.3.refs_1_.refs_0_, bf16[128,1024]{1,0:T(8,128)(2,1)S(1)} %collective-permute-done.4.refs_2_.refs_1_, bf16[128,1024]{1,0:T(8,128)(2,1)S(1)} %collective-permute-done.5.refs_3_.refs_2_, bf16[8192,1024]{1,0:T(8,128)(2,1)} %refs_2_.3, ...), custom_call_target="tpu_custom_call" | custom-call | flops 805306368 | bytes 6291456 | tf_op jit(solution)/shard_map/pallas_call | solution.py:111
  50.1 4.8 %collective-permute-start.14 = (f32[17,1024]{1,0:T(8,128)S(1)}, f32[17,1024]{1,0:T(8,128)S(1)}, u32[]{:S(2)}, u32[]{:S(2)}) collective-permute-start(f32[17,1024]{1,0:T(8,128)S(1)} %get-tuple-element.56), channel_id=1, source_target_pairs={{0,16},{8,24},{1,17},{9,25},{2,18},{10,26},{3,19},{11,27},{4,20},{... | collective-permute-start | bytes 208904 | tf_op jit(solution)/shard_map/ppermute | solution.py:593
  54.9 2.5 %shard_map.143.gate_ref = f32[128,1024]{1,0:T(8,128)S(1)} custom-call(bf16[128,1024]{1,0:T(8,128)(2,1)S(1)} %collective-permute-done.refs_1_.a_ref.refs_0_, bf16[128,1024]{1,0:T(8,128)(2,1)S(1)} %collective-permute-done.6.b_ref.refs_1_, bf16[8192,1024]{1,0:T(8,128)(2,1)} %refs_2_.3, f32[128,1024]{1,0:T(8,128)S(1)} %shard_map.141.refs_3_), custom_call_target="tpu_custom_call" | custom-call | flops 536870912 | bytes 4194304 | tf_op jit(solution)/shard_map/pallas_call | solution.py:111
  57.5 2.3 %shard_map.144 = (bf16[128,1024]{1,0:T(8,128)(2,1)S(1)}, f32[16,1024]{1,0:T(8,128)}) custom-call(f32[1024,128]{1,0:T(8,128)S(1)} %get-tuple-element.50.y_ref, f32[1024,128]{1,0:T(8,128)S(1)} %get-tuple-element.51.cum_ref, f32[2048,128]{1,0:T(8,128)S(1)} %get-tuple-element.52.c_ref, f32[17,1024]{1,0:T(8,128)S(1)} %get-tuple-element.53.group_ref.end_ref, ...), custom_call_target="tpu_custom_call" | custom-call | flops 12582912 | bytes 1048576 | tf_op jit(solution)/shard_map/pallas_call | solution.py:434
  59.7 1.3 %shard_map.146 = bf16[4,128,1024]{2,1,0:T(8,128)(2,1)S(1)} custom-call(bf16[128,1024]{1,0:T(8,128)(2,1)S(1)} %get-tuple-element.60.g_ref, bf16[4,1024,1024]{2,1,0:T(8,128)(2,1)S(1)} %shard_map.138.w_ref), custom_call_target="tpu_custom_call" | custom-call | flops 1073741824 | bytes 8388608 | tf_op jit(solution)/shard_map/pallas_call | solution.py:495
  61.0 0.1 collective-permute-start.15
  61.1 4.0 %shard_map.145.a_ref = bf16[4,128,1024]{2,1,0:T(8,128)(2,1)S(1)} custom-call(bf16[128,1024]{1,0:T(8,128)(2,1)S(1)} %get-tuple-element.60.g_ref, bf16[1024,8192]{1,0:T(8,128)(2,1)} %w_ref.5), custom_call_target="tpu_custom_call" | custom-call | flops 1073741824 | bytes 8388608 | tf_op jit(solution)/shard_map/pallas_call | solution.py:518
  65.1 0.2 shard_map.147
  65.3 1.2 %collective-permute-start.17 = (bf16[128,1024]{1,0:T(8,128)(2,1)S(1)}, bf16[128,1024]{1,0:T(8,128)(2,1)S(1)}, u32[]{:S(2)}, u32[]{:S(2)}) collective-permute-start(bf16[128,1024]{1,0:T(8,128)(2,1)S(1)} %get-tuple-element.64), channel_id=1, source_target_pairs={{0,2},{1,5},{2,0},{3,7},{4,6},{5,1},{6,4},{7,3},{8,10},{9,13},{10,... | collective-permute-start | bytes 786440 | tf_op jit(solution)/shard_map/ppermute | solution.py:607
  66.5 0.9 %collective-permute-start.16 = (bf16[128,1024]{1,0:T(8,128)(2,1)S(1)}, bf16[128,1024]{1,0:T(8,128)(2,1)S(1)}, u32[]{:S(2)}, u32[]{:S(2)}) collective-permute-start(bf16[128,1024]{1,0:T(8,128)(2,1)S(1)} %get-tuple-element.62), channel_id=1, source_target_pairs={{0,2},{1,5},{2,0},{3,7},{4,6},{5,1},{6,4},{7,3},{8,10},{9,13},{10,... | collective-permute-start | bytes 786440 | tf_op jit(solution)/shard_map/ppermute | solution.py:608
  67.4 4.3 %collective-permute-done.17.refs_1_ = bf16[128,1024]{1,0:T(8,128)(2,1)S(1)} collective-permute-done((bf16[128,1024]{1,0:T(8,128)(2,1)S(1)}, bf16[128,1024]{1,0:T(8,128)(2,1)S(1)}, u32[]{:S(2)}, u32[]{:S(2)}) %collective-permute-start.17) | collective-permute-done | bytes 262176 | tf_op jit(solution)/shard_map/ppermute | solution.py:607
  71.8 0.1 shard_map.148
  71.8 0.6 collective-permute-start.18
  72.4 2.6 %collective-permute-done.16.refs_1_ = bf16[128,1024]{1,0:T(8,128)(2,1)S(1)} collective-permute-done((bf16[128,1024]{1,0:T(8,128)(2,1)S(1)}, bf16[128,1024]{1,0:T(8,128)(2,1)S(1)}, u32[]{:S(2)}, u32[]{:S(2)}) %collective-permute-start.16) | collective-permute-done | bytes 262176 | tf_op jit(solution)/shard_map/ppermute | solution.py:608
  75.0 3.2 %collective-permute-done.18.refs_2_ = bf16[128,1024]{1,0:T(8,128)(2,1)S(1)} collective-permute-done((bf16[128,1024]{1,0:T(8,128)(2,1)S(1)}, bf16[128,1024]{1,0:T(8,128)(2,1)S(1)}, u32[]{:S(2)}, u32[]{:S(2)}) %collective-permute-start.18) | collective-permute-done | bytes 262176 | tf_op jit(solution)/shard_map/ppermute | solution.py:609
  78.3 0.8 %shard_map.149 = bf16[128,1024]{1,0:T(8,128)(2,1)} custom-call(bf16[128,1024]{1,0:T(8,128)(2,1)S(1)} %get-tuple-element.61.refs_0_, bf16[128,1024]{1,0:T(8,128)(2,1)S(1)} %collective-permute-done.16.refs_1_, bf16[128,1024]{1,0:T(8,128)(2,1)S(1)} %collective-permute-done.18.refs_2_), custom_call_target="tpu_custom_call" | custom-call | flops 393216 | bytes 786432 | tf_op jit(solution)/shard_map/pallas_call | solution.py:331
  (27 shorter events, 0.2 us)
Async XLA Ops:
  0.6 4.6 %collective-permute-start.2 = (bf16[128,1024]{1,0:T(8,128)(2,1)}, bf16[128,1024]{1,0:T(8,128)(2,1)S(1)}, u32[]{:S(2)}, u32[]{:S(2)}) collective-permute-start(bf16[128,1024]{1,0:T(8,128)(2,1)} %refs_0_.2), channel_id=1, source_target_pairs={{0,1},{1,0},{2,3},{3,2},{4,5},{5,4},{6,7},{7,6},{8,9},{9,8},{10,11... | collective-permute-start | bytes 786440 | tf_op jit(solution)/shard_map/ppermute | solution.py:24
  1.2 9.7 %collective-permute-start.4 = (bf16[128,1024]{1,0:T(8,128)(2,1)}, bf16[128,1024]{1,0:T(8,128)(2,1)S(1)}, u32[]{:S(2)}, u32[]{:S(2)}) collective-permute-start(bf16[128,1024]{1,0:T(8,128)(2,1)} %refs_0_.2), channel_id=1, source_target_pairs={{0,4},{1,5},{2,6},{3,7},{4,0},{5,1},{6,2},{7,3},{8,12},{9,13},{10,... | collective-permute-start | bytes 786440 | tf_op jit(solution)/shard_map/ppermute | solution.py:24
  3.8 8.6 %collective-permute-start.1 = (bf16[128,1024]{1,0:T(8,128)(2,1)}, bf16[128,1024]{1,0:T(8,128)(2,1)S(1)}, u32[]{:S(2)}, u32[]{:S(2)}) collective-permute-start(bf16[128,1024]{1,0:T(8,128)(2,1)} %refs_0_.2), channel_id=1, source_target_pairs={{0,2},{1,3},{2,0},{3,1},{4,6},{5,7},{6,4},{7,5},{8,10},{9,11},{10,... | collective-permute-start | bytes 786440 | tf_op jit(solution)/shard_map/ppermute | solution.py:24
  5.3 1.0 %copy-start.1 = (bf16[128,1024]{1,0:T(8,128)(2,1)S(1)}, bf16[128,1024]{1,0:T(8,128)(2,1)}, u32[]{:S(2)}) copy-start(bf16[128,1024]{1,0:T(8,128)(2,1)} %refs_0_.2) | copy-start | bytes 786436
  12.3 1.9 %collective-permute-start.3 = (bf16[128,1024]{1,0:T(8,128)(2,1)S(1)}, bf16[128,1024]{1,0:T(8,128)(2,1)S(1)}, u32[]{:S(2)}, u32[]{:S(2)}) collective-permute-start(bf16[128,1024]{1,0:T(8,128)(2,1)S(1)} %collective-permute-done.1.refs_0_), channel_id=1, source_target_pairs={{0,1},{1,0},{2,3},{3,2},{4,5},{5,4},{6,7},{7,6},{8,9},{9,8},{10,11... | collective-permute-start | bytes 786440 | tf_op jit(solution)/shard_map/ppermute | solution.py:24
  12.3 1.9 %collective-permute-start.5 = (bf16[128,1024]{1,0:T(8,128)(2,1)S(1)}, bf16[128,1024]{1,0:T(8,128)(2,1)S(1)}, u32[]{:S(2)}, u32[]{:S(2)}) collective-permute-start(bf16[128,1024]{1,0:T(8,128)(2,1)S(1)} %collective-permute-done.4.refs_2_.refs_1_), channel_id=1, source_target_pairs={{0,1},{1,0},{2,3},{3,2},{4,5},{5,4},{6,7},{7,6},{8,9},{9,8},{10,11... | collective-permute-start | bytes 786440 | tf_op jit(solution)/shard_map/ppermute | solution.py:24
  12.9 9.1 %collective-permute-start = (bf16[128,1024]{1,0:T(8,128)(2,1)S(1)}, bf16[128,1024]{1,0:T(8,128)(2,1)S(1)}, u32[]{:S(2)}, u32[]{:S(2)}) collective-permute-start(bf16[128,1024]{1,0:T(8,128)(2,1)S(1)} %copy-done.1), channel_id=1, source_target_pairs={{0,6},{1,7},{2,4},{3,5},{4,2},{5,3},{6,0},{7,1},{8,14},{9,15},{10,... | collective-permute-start | bytes 786440 | tf_op jit(solution)/shard_map/ppermute | solution.py:24
  22.0 2.3 %collective-permute-start.6 = (bf16[128,1024]{1,0:T(8,128)(2,1)S(1)}, bf16[128,1024]{1,0:T(8,128)(2,1)S(1)}, u32[]{:S(2)}, u32[]{:S(2)}) collective-permute-start(bf16[128,1024]{1,0:T(8,128)(2,1)S(1)} %collective-permute-done.refs_1_.a_ref.refs_0_), channel_id=1, source_target_pairs={{0,1},{1,0},{2,3},{3,2},{4,5},{5,4},{6,7},{7,6},{8,9},{9,8},{10,11... | collective-permute-start | bytes 786440 | tf_op jit(solution)/shard_map/ppermute | solution.py:24
  24.2 6.2 %copy-start = (bf16[1024,544]{0,1:T(8,128)(2,1)S(1)}, bf16[1024,544]{0,1:T(8,128)(2,1)}, u32[]{:S(2)}) copy-start(bf16[1024,544]{0,1:T(8,128)(2,1)} %param.17) | copy-start | bytes 3342340
  24.2 6.2 %copy-start.3 = (f32[4,1024]{1,0:T(4,128)S(1)}, f32[4,1024]{1,0:T(4,128)}, u32[]{:S(2)}) copy-start(f32[4,1024]{1,0:T(4,128)} %w_ref.3) | copy-start | bytes 49156
  24.2 6.2 %copy-start.4 = (f32[1024]{0:T(1024)S(1)}, f32[1024]{0:T(1024)}, u32[]{:S(2)}) copy-start(f32[1024]{0:T(1024)} %param.16) | copy-start | bytes 12292
  25.0 5.4 %collective-permute-start.7 = (bf16[8,1024]{1,0:T(8,128)(2,1)S(1)}, bf16[8,1024]{1,0:T(8,128)(2,1)S(1)}, u32[]{:S(2)}, u32[]{:S(2)}) collective-permute-start(bf16[8,1024]{1,0:T(8,128)(2,1)S(1)} %get-tuple-element.40), channel_id=1, source_target_pairs={{0,8},{8,16},{16,24},{1,9},{9,17},{17,25},{2,10},{10,18},{18,26},{... | collective-permute-start | bytes 49160 | tf_op jit(solution)/shard_map/ppermute | solution.py:564
  30.3 11.2 %copy-start.2 = (f32[1024,16]{0,1:T(8,128)S(1)}, f32[1024,16]{0,1:T(8,128)}, u32[]{:S(2)}) copy-start(f32[1024,16]{0,1:T(8,128)} %param.20) | copy-start | bytes 196612
  30.3 11.2 %copy-start.5 = (bf16[512,1024]{1,0:T(8,128)(2,1)S(1)}, bf16[512,1024]{1,0:T(8,128)(2,1)}, u32[]{:S(2)}) copy-start(bf16[512,1024]{1,0:T(8,128)(2,1)} %refs_3_.4) | copy-start | bytes 3145732
  30.4 11.2 %copy-start.6 = (f32[1024,16]{0,1:T(8,128)S(1)}, f32[1024,16]{0,1:T(8,128)}, u32[]{:S(2)}) copy-start(f32[1024,16]{0,1:T(8,128)} %param.23) | copy-start | bytes 196612
  30.4 11.2 %copy-start.7 = (f32[1024]{0:T(1024)S(1)}, f32[1024]{0:T(1024)}, u32[]{:S(2)}) copy-start(f32[1024]{0:T(1024)} %param.19) | copy-start | bytes 12292
  31.3 1.3 %collective-permute-start.8 = (bf16[64,544]{1,0:T(8,128)(2,1)S(1)}, bf16[64,544]{1,0:T(8,128)(2,1)S(1)}, u32[]{:S(2)}, u32[]{:S(2)}) collective-permute-start(bf16[64,544]{1,0:T(8,128)(2,1)S(1)} %get-tuple-element.45), channel_id=1, source_target_pairs={{0,1},{1,0},{2,3},{3,2},{4,5},{5,4},{6,7},{7,6},{8,9},{9,8},{10,11... | collective-permute-start | bytes 208904 | tf_op jit(solution)/shard_map/ppermute | solution.py:24
  32.7 7.1 %collective-permute-start.11 = (bf16[64,544]{1,0:T(8,128)(2,1)S(1)}, bf16[64,544]{1,0:T(8,128)(2,1)S(1)}, u32[]{:S(2)}, u32[]{:S(2)}) collective-permute-start(bf16[64,544]{1,0:T(8,128)(2,1)S(1)} %shard_map.137.dep_ref.refs_0_), channel_id=1, source_target_pairs={{0,6},{1,7},{2,4},{3,5},{4,2},{5,3},{6,0},{7,1},{8,14},{9,15},{10,... | collective-permute-start | bytes 208904 | tf_op jit(solution)/shard_map/ppermute | solution.py:24
  34.2 5.8 %collective-permute-start.10 = (bf16[64,544]{1,0:T(8,128)(2,1)S(1)}, bf16[64,544]{1,0:T(8,128)(2,1)S(1)}, u32[]{:S(2)}, u32[]{:S(2)}) collective-permute-start(bf16[64,544]{1,0:T(8,128)(2,1)S(1)} %shard_map.137.dep_ref.refs_0_), channel_id=1, source_target_pairs={{0,4},{1,5},{2,6},{3,7},{4,0},{5,1},{6,2},{7,3},{8,12},{9,13},{10,... | collective-permute-start | bytes 208904 | tf_op jit(solution)/shard_map/ppermute | solution.py:24
  35.7 4.4 %collective-permute-start.9 = (bf16[64,544]{1,0:T(8,128)(2,1)S(1)}, bf16[64,544]{1,0:T(8,128)(2,1)S(1)}, u32[]{:S(2)}, u32[]{:S(2)}) collective-permute-start(bf16[64,544]{1,0:T(8,128)(2,1)S(1)} %shard_map.137.dep_ref.refs_0_), channel_id=1, source_target_pairs={{0,2},{1,3},{2,0},{3,1},{4,6},{5,7},{6,4},{7,5},{8,10},{9,11},{10,... | collective-permute-start | bytes 208904 | tf_op jit(solution)/shard_map/ppermute | solution.py:24
  40.2 1.3 %collective-permute-start.12 = (bf16[64,544]{1,0:T(8,128)(2,1)S(1)}, bf16[64,544]{1,0:T(8,128)(2,1)S(1)}, u32[]{:S(2)}, u32[]{:S(2)}) collective-permute-start(bf16[64,544]{1,0:T(8,128)(2,1)S(1)} %shard_map.139.refs_0_), channel_id=1, source_target_pairs={{0,1},{1,0},{2,3},{3,2},{4,5},{5,4},{6,7},{7,6},{8,9},{9,8},{10,11... | collective-permute-start | bytes 208904 | tf_op jit(solution)/shard_map/ppermute | solution.py:24
  45.1 12.4 %copy-start.8 = (f32[1024]{0:T(1024)S(1)}, f32[1024]{0:T(1024)}, u32[]{:S(2)}) copy-start(f32[1024]{0:T(1024)} %param.21) | copy-start | bytes 12292
  45.1 5.0 %collective-permute-start.13 = (f32[17,1024]{1,0:T(8,128)S(1)}, f32[17,1024]{1,0:T(8,128)S(1)}, u32[]{:S(2)}, u32[]{:S(2)}) collective-permute-start(f32[17,1024]{1,0:T(8,128)S(1)} %get-tuple-element.53.group_ref.end_ref), channel_id=1, source_target_pairs={{0,8},{8,0},{16,24},{24,16},{1,9},{9,1},{17,25},{25,17},{2,10},{10... | collective-permute-start | bytes 208904 | tf_op jit(solution)/shard_map/ppermute | solution.py:24
  50.1 7.3 %collective-permute-start.14 = (f32[17,1024]{1,0:T(8,128)S(1)}, f32[17,1024]{1,0:T(8,128)S(1)}, u32[]{:S(2)}, u32[]{:S(2)}) collective-permute-start(f32[17,1024]{1,0:T(8,128)S(1)} %get-tuple-element.56), channel_id=1, source_target_pairs={{0,16},{8,24},{1,17},{9,25},{2,18},{10,26},{3,19},{11,27},{4,20},{... | collective-permute-start | bytes 208904 | tf_op jit(solution)/shard_map/ppermute | solution.py:593
  61.0 4.1 %collective-permute-start.15 = (bf16[4,128,1024]{2,1,0:T(8,128)(2,1)S(1)}, bf16[4,128,1024]{2,1,0:T(8,128)(2,1)S(1)}, u32[]{:S(2)}, u32[]{:S(2)}) collective-permute-start(bf16[4,128,1024]{2,1,0:T(8,128)(2,1)S(1)} %shard_map.146), channel_id=1, source_target_pairs={{0,1},{1,0},{2,3},{3,2},{4,5},{5,4},{6,7},{7,6},{8,9},{9,8},{10,11... | collective-permute-start | bytes 3145736 | tf_op jit(solution)/shard_map/ppermute | solution.py:24
  65.3 6.4 %collective-permute-start.17 = (bf16[128,1024]{1,0:T(8,128)(2,1)S(1)}, bf16[128,1024]{1,0:T(8,128)(2,1)S(1)}, u32[]{:S(2)}, u32[]{:S(2)}) collective-permute-start(bf16[128,1024]{1,0:T(8,128)(2,1)S(1)} %get-tuple-element.64), channel_id=1, source_target_pairs={{0,2},{1,5},{2,0},{3,7},{4,6},{5,1},{6,4},{7,3},{8,10},{9,13},{10,... | collective-permute-start | bytes 786440 | tf_op jit(solution)/shard_map/ppermute | solution.py:607
  66.5 8.5 %collective-permute-start.16 = (bf16[128,1024]{1,0:T(8,128)(2,1)S(1)}, bf16[128,1024]{1,0:T(8,128)(2,1)S(1)}, u32[]{:S(2)}, u32[]{:S(2)}) collective-permute-start(bf16[128,1024]{1,0:T(8,128)(2,1)S(1)} %get-tuple-element.62), channel_id=1, source_target_pairs={{0,2},{1,5},{2,0},{3,7},{4,6},{5,1},{6,4},{7,3},{8,10},{9,13},{10,... | collective-permute-start | bytes 786440 | tf_op jit(solution)/shard_map/ppermute | solution.py:608
  71.8 6.4 %collective-permute-start.18 = (bf16[128,1024]{1,0:T(8,128)(2,1)S(1)}, bf16[128,1024]{1,0:T(8,128)(2,1)S(1)}, u32[]{:S(2)}, u32[]{:S(2)}) collective-permute-start(bf16[128,1024]{1,0:T(8,128)(2,1)S(1)} %shard_map.148), channel_id=1, source_target_pairs={{0,4},{1,3},{2,6},{3,1},{4,0},{5,7},{6,2},{7,5},{8,12},{9,11},{10,... | collective-permute-start | bytes 786440 | tf_op jit(solution)/shard_map/ppermute | solution.py:609
where the time goes:
time: 79.5 us; the launch traced here: 79.1 us
  Pallas kernels  34.8 us (44%)
  starting transfers between devices  23.3 us (29%)
  waiting for transfers between devices  19.1 us (24%)
  local copies, waits for them, and re-layouts  1.03 us (1%)
  between operations  0.94 us (1%)
    pallas_call x5, Pallas kernels, mm(): pl.pallas_call(functools.partial(mm_kernel, masks, n_w, has_acc), in_spec...  15.2 us
    ppermute x14, starting transfers between devices, flip(): return lax.ppermute(value, axis, [(i, i ^ mask) for i in range(peers)])  12.4 us
    ppermute x14, waiting for transfers between devices, flip(): return lax.ppermute(value, axis, [(i, i ^ mask) for i in range(peers)])  8.84 us
    ppermute x1, starting transfers between devices, on_device(): got = lax.ppermute(group, 'ctx', pairs)  4.75 us
    ppermute x1, waiting for transfers between devices, on_device(): rd = lax.ppermute(sd, 'tp', to_first)  4.35 us
    pallas_call x1, Pallas kernels, out_blocks(): pl.pallas_call(functools.partial(out_kernel, masks), in_specs=[vm, pl.Blo...  3.99 us
    pallas_call x1, Pallas kernels, fetch_cols(): pl.pallas_call(functools.partial(cols_kernel, masks), in_specs=[pl.BlockS...  3.52 us
    pallas_call x1, Pallas kernels, scan(): pl.pallas_call(functools.partial(scan_kernel, len(parts) == 2), in_specs=...  3.52 us
  transfers between devices with their start and end apart: 19, of which 10 were waited for; matrix products, arithmetic and copies ran while one was open for 0% of the time, Pallas kernels for 32%

commit v1 on v0

--- a/solution.py
+++ b/solution.py
@@ -70,7 +70,7 @@
     return copies
 
 
-def mm_kernel(masks, n_w, has_acc, *refs):
+def stream_kernel(masks, n_w, has_acc, *refs):
     n_b = len(masks)
     lhs = refs[:n_b]
     w = refs[n_b : n_b + n_w]
@@ -83,12 +83,18 @@
     feat = lhs[0].shape[1]
     piece = feat // PIECES
     copies = row_copies(masks, w, bufs, sem, feat)
+    own, own_sem = refs[2 * n_w + 1 :]
+    load = pltpu.make_async_copy(lhs[-1], own, own_sem)
+    load.start()
     for c in copies:
         c.start()
+    lhs = tuple(lhs[:-1]) + (own,)
     step = 0
     for q in range(n_w):
         total = acc_in[q][...] if has_acc else None
         for i in range(n_b):
+            if i == n_b - 1 and q == 0:
+                load.wait()
             for p in range(PIECES):
                 copies[step].wait()
                 step += 1
@@ -101,7 +107,7 @@
         outs[q][...] = total
 
 
-def mm(blocks, masks, weights, accs):
+def stream_mm(blocks, masks, weights, accs):
     rows, feat = blocks[0].shape
     ch = weights[0].shape[1]
     n_w = len(weights)
@@ -109,69 +115,58 @@
     vm = pl.BlockSpec(memory_space=VMEM)
     depth = feat * len(blocks)
     return pl.pallas_call(
-        functools.partial(mm_kernel, masks, n_w, has_acc),
-        in_specs=[vm] * len(blocks)
+        functools.partial(stream_kernel, masks, n_w, has_acc),
+        in_specs=[vm] * (len(blocks) - 1)
+        + [pl.BlockSpec(memory_space=pltpu.HBM)]
         + [pl.BlockSpec(memory_space=pltpu.HBM)] * n_w
         + [vm] * (n_w if has_acc else 0),
         out_specs=[vm] * n_w,
         out_shape=[jax.ShapeDtypeStruct((rows, ch), F32)] * n_w,
         scratch_shapes=[VMEM((depth, ch), BF16)] * n_w
-        + [pltpu.SemaphoreType.DMA((n_w * len(blocks) * PIECES,))],
+        + [pltpu.SemaphoreType.DMA((n_w * len(blocks) * PIECES,))]
+        + [VMEM((rows, feat), BF16), pltpu.SemaphoreType.DMA],
         compiler_params=params(12),
         cost_estimate=cost(2 * rows * depth * ch * n_w, 2 * depth * ch * n_w),
-    )(*blocks, *map(far, weights), *(accs or ()))
-
-
-def fetch_kernel(masks, n_w, *refs):
-    w = refs[:n_w]
-    outs = refs[n_w + 1 : 2 * n_w + 1]
-    sem = refs[2 * n_w + 1]
-    copies = row_copies(masks, w, outs, sem, outs[0].shape[0] // len(masks))
-    for c in copies:
-        c.start()
-    for c in copies:
-        c.wait()
-
-
-def fetch(masks, weights, feat, dep):
-    ch = weights[0].shape[1]
-    n_w = len(weights)
-    depth = feat * len(masks)
-    return pl.pallas_call(
-        functools.partial(fetch_kernel, masks, n_w),
-        in_specs=[pl.BlockSpec(memory_space=pltpu.HBM)] * n_w + [pl.BlockSpec(memory_space=VMEM)],
-        out_specs=[pl.BlockSpec(memory_space=VMEM)] * n_w,
-        out_shape=[VMEM((depth, ch), BF16)] * n_w,
-        scratch_shapes=[pltpu.SemaphoreType.DMA((n_w * len(masks) * PIECES,))],
-        compiler_params=params(1),
-        cost_estimate=cost(0, 2 * depth * ch * n_w),
-    )(*map(far, weights), dep)
-
-
-def last_kernel(edge, a_ref, b_ref, w_ref, acc_ref, out_ref, edge_ref=None):
-    feat = a_ref.shape[1]
-    total = acc_ref[...] + jnp.dot(a_ref[...], w_ref[:feat, :], preferred_element_type=F32)
-    total = total + jnp.dot(b_ref[...], w_ref[feat:, :], preferred_element_type=F32)
-    out_ref[...] = total.astype(BF16)
+    )(*blocks[:-1], far(blocks[-1]), *map(far, weights), *(accs or ()))
+
+
+def held(value):
+    return pltpu.with_memory_space_constraint(value, VMEM)
+
+
+def mm_kernel(roles, has_acc, edge, *refs):
+    n_b = len(roles)
+    lhs = refs[:n_b]
+    w_ref = refs[n_b]
+    total = refs[n_b + 1][...] if has_acc else None
+    outs = refs[n_b + 1 + has_acc :]
+    feat = lhs[0].shape[1]
+    for x, role in zip(lhs, roles):
+        at = pl.ds(pl.multiple_of(peer(role) * feat, feat), feat)
+        part = jnp.dot(x[...], w_ref[at, :], preferred_element_type=F32)
+        total = part if total is None else total + part
+    outs[0][...] = total.astype(outs[0].dtype)
     if edge:
-        edge_ref[...] = total[total.shape[0] - edge :].astype(BF16)
-
-
-def finish(a, b, w, acc, edge=0):
-    rows, feat = a.shape
-    ch = w.shape[1]
-    vm = pl.BlockSpec(memory_space=VMEM)
-    shapes = [jax.ShapeDtypeStruct((rows, ch), BF16)]
+        outs[1][...] = total[total.shape[0] - edge :].astype(BF16)
+
+
+def mm(blocks, roles, weight, acc, edge=0):
+    rows, feat = blocks[0].shape
+    ch = weight.shape[1]
+    vm = pl.BlockSpec(memory_space=VMEM)
+    shapes = [jax.ShapeDtypeStruct((rows, ch), BF16 if edge else F32)]
     if edge:
         shapes.append(jax.ShapeDtypeStruct((edge, ch), BF16))
-    return pl.pallas_call(
-        functools.partial(last_kernel, edge),
-        in_specs=[vm] * 4,
+    extra = () if acc is None else (acc,)
+    n = len(blocks)
+    return pl.pallas_call(
+        functools.partial(mm_kernel, roles, len(extra), edge),
+        in_specs=[vm] * (n + 1 + len(extra)),
         out_specs=[vm] * len(shapes),
         out_shape=shapes,
-        compiler_params=params(4),
-        cost_estimate=cost(4 * rows * feat * ch, 4 * feat * ch),
-    )(a, b, pltpu.with_memory_space_constraint(w, VMEM), acc)
+        compiler_params=params(5 if n > 5 else 4),
+        cost_estimate=cost(2 * n * rows * feat * ch, 2 * n * feat * ch),
+    )(*blocks, weight, *extra)
 
 
 def conv_kernel(split, x_ref, tail_ref, w_ref, b_ref, pw_ref, conv_ref, send_ref, keep_ref, pad, acc):
@@ -237,7 +232,7 @@
     n_p = 2 if split else 1
     parts = refs[:n_p]
     (conv_ref, sw_ref, sb_ref, decay_ref, carried_ref,
-     end_ref, y_ref, cum_ref, c_ref,
+     end_ref, pack_ref, y_ref, cum_ref, c_ref,
      proj_s, step_s, drive_s, nd_s, h_s, b_ref) = refs[n_p:]
     rows, ch = conv_ref.shape
     groups = ch // LANES
@@ -288,6 +283,7 @@
     end_ref[0:STATE, :] = collect(h_s, STATE, groups)
     nd_s[0:groups, :] = total
     end_ref[STATE : STATE + 1, :] = collect(nd_s, 1, groups)
+    pack_ref[...] = end_ref[...].astype(BF16)
 
 
 def scan(parts, conv_x, step_w, step_b, decay_t, carried_t):
@@ -297,9 +293,10 @@
     return pl.pallas_call(
         functools.partial(scan_kernel, len(parts) == 2),
         in_specs=[vm] * (5 + len(parts)),
-        out_specs=[vm] * 4,
+        out_specs=[vm] * 5,
         out_shape=[
             jax.ShapeDtypeStruct((STATE + 1, ch), F32),
+            jax.ShapeDtypeStruct((STATE + 1, ch), BF16),
             jax.ShapeDtypeStruct((rows * groups, LANES), F32),
             jax.ShapeDtypeStruct((rows * groups, LANES), F32),
             jax.ShapeDtypeStruct((rows * STATE, LANES), F32),
@@ -358,10 +355,11 @@
 
 def merge_kernel(bit, first, decay_ref, group_ref, got_ref, *refs):
     ent_ref = None if first else refs[0]
-    new_ref, out_ref = refs[-2:]
+    new_ref, pack_ref, out_ref = refs[-3:]
     upper = (lax.axis_index("ctx") // bit) % 2 == 1
     decay = decay_ref[...]
-    gh, gs = got_ref[:STATE, :], got_ref[STATE:, :]
+    got = got_ref[...].astype(F32)
+    gh, gs = got[:STATE], got[STATE:]
     mh, ms = group_ref[:STATE, :], group_ref[STATE:, :]
     entering = gh if first else jnp.exp(-decay * ent_ref[STATE:, :]) * gh + ent_ref[:STATE, :]
     before = gs if first else ent_ref[STATE:, :] + gs
@@ -374,6 +372,7 @@
     high_s = jnp.where(upper, ms, gs)
     new_ref[:STATE, :] = jnp.exp(-decay * high_s) * low + high
     new_ref[STATE:, :] = ms + gs
+    pack_ref[...] = new_ref[...].astype(BF16)
 
 
 def merge(bit, decay_t, group, got, ent):
@@ -383,8 +382,12 @@
     return pl.pallas_call(
         functools.partial(merge_kernel, bit, first),
         in_specs=[vm] * (3 + len(extra)),
-        out_specs=[vm, vm],
-        out_shape=[jax.ShapeDtypeStruct(group.shape, F32)] * 2,
+        out_specs=[vm] * 3,
+        out_shape=[
+            jax.ShapeDtypeStruct(group.shape, F32),
+            jax.ShapeDtypeStruct(group.shape, BF16),
+            jax.ShapeDtypeStruct(group.shape, F32),
+        ],
         compiler_params=params(3),
         cost_estimate=cost(group.size * 8, group.size * 16),
     )(decay_t, group, got, *extra)
@@ -397,7 +400,7 @@
     groups = ch // LANES
     decay = decay_ref[...]
     upper = (lax.axis_index("ctx") // bit) % 2 == 1
-    got = got_ref[:STATE, :]
+    got = got_ref[...].astype(F32)[:STATE]
     if first:
         entering = jnp.where(upper, got, jnp.zeros_like(got))
     else:
@@ -449,81 +452,25 @@
     )(y, cum, bc, end, got, decay_t, conv_x, skip, gate, *extra)
 
 
-def col_copies(masks, w, buf, sem, feat):
-    copies = []
+def out_stack_kernel(masks, g_ref, w_ref, out):
+    feat = out.shape[2]
     for i, mask in enumerate(masks):
-        at = pl.multiple_of((peer(mask)) * feat, feat)
-        copies.append(
-            pltpu.make_async_copy(w.at[:, pl.ds(at, feat)], buf.at[i], sem.at[i])
-        )
-    return copies
-
-
-def cols_kernel(masks, w_ref, dep_ref, out_ref, sem):
-    copies = col_copies(masks, w_ref, out_ref, sem, out_ref.shape[2])
-    for c in copies:
-        c.start()
-    for c in copies:
-        c.wait()
-
-
-def fetch_cols(masks, weight, feat, dep):
-    ch = weight.shape[0]
-    return pl.pallas_call(
-        functools.partial(cols_kernel, masks),
-        in_specs=[
-            pl.BlockSpec(memory_space=pltpu.HBM),
-            pl.BlockSpec(memory_space=VMEM),
-        ],
-        out_specs=pl.BlockSpec(memory_space=VMEM),
-        out_shape=VMEM((len(masks), ch, feat), BF16),
-        scratch_shapes=[pltpu.SemaphoreType.DMA((len(masks),))],
-        compiler_params=params(1),
-        cost_estimate=cost(0, 2 * ch * feat * len(masks)),
-    )(far(weight), dep)
-
-
-def out_held_kernel(g_ref, w_ref, o_ref):
-    for i in range(w_ref.shape[0]):
-        o_ref[i] = jnp.dot(g_ref[...], w_ref[i], preferred_element_type=F32).astype(o_ref.dtype)
-
-
-def out_held(gated, cols):
+        at = pl.ds(pl.multiple_of(peer(mask) * feat, feat), feat)
+        out[i] = jnp.dot(g_ref[...], w_ref[:, at], preferred_element_type=F32).astype(BF16)
+
+
+def out_blocks(gated, weight, masks, feat):
     rows, ch = gated.shape
-    n, _, feat = cols.shape
-    vm = pl.BlockSpec(memory_space=VMEM)
-    return pl.pallas_call(
-        out_held_kernel,
+    n = len(masks)
+    vm = pl.BlockSpec(memory_space=VMEM)
+    return pl.pallas_call(
+        functools.partial(out_stack_kernel, masks),
         in_specs=[vm, vm],
         out_specs=vm,
         out_shape=jax.ShapeDtypeStruct((n, rows, feat), BF16),
         compiler_params=params(4),
         cost_estimate=cost(2 * rows * ch * feat * n, 2 * ch * feat * n),
-    )(gated, pltpu.with_memory_space_constraint(cols, VMEM))
-
-
-def out_kernel(masks, g_ref, w_ref, o_ref, buf, sem):
-    copies = col_copies(masks, w_ref, buf, sem, o_ref.shape[2])
-    for c in copies:
-        c.start()
-    for i, c in enumerate(copies):
-        c.wait()
-        o_ref[i] = jnp.dot(g_ref[...], buf[i], preferred_element_type=F32).astype(o_ref.dtype)
-
-
-def out_blocks(gated, weight, masks, feat):
-    rows, ch = gated.shape
-    n = len(masks)
-    vm = pl.BlockSpec(memory_space=VMEM)
-    return pl.pallas_call(
-        functools.partial(out_kernel, masks),
-        in_specs=[vm, pl.BlockSpec(memory_space=pltpu.HBM)],
-        out_specs=vm,
-        out_shape=jax.ShapeDtypeStruct((n, rows, feat), BF16),
-        scratch_shapes=[VMEM((n, ch, feat), BF16), pltpu.SemaphoreType.DMA((n,))],
-        compiler_params=params(12),
-        cost_estimate=cost(2 * rows * ch * feat * n, 2 * ch * feat * n),
-    )(gated, far(weight))
+    )(gated, weight)
 
 
 def on_device(
@@ -540,21 +487,21 @@
     carried_t = carried_state.T
 
     if square:
+        to_first = [(i, i ^ (2 + 2 * (i % 2))) for i in range(n_tp)]
+        to_second = [(i, i ^ (4 - 2 * (i % 2))) for i in range(n_tp)]
         p1 = flip(tokens, "tp", 1)
-        px = flip(tokens, "tp", 2)
-        py = flip(tokens, "tp", 4)
-        pd = flip(tokens, "tp", 6)
-        inner, gate_acc = mm([tokens, p1], [0, 1], [inner_weight, gate_weight], None)
-        px = tie(px, inner)
-        py = tie(py, inner)
-        qx = flip(px, "tp", 1)
-        qy = flip(py, "tp", 1)
-        inner, = mm([px, qx, py, qy], [2, 3, 4, 5], [inner_weight], [inner])
-        pd = tie(pd, inner)
-        qd = flip(pd, "tp", 1)
-        inner_d, = fetch([6, 7], [inner_weight], feat, pd)
-        qd = tie(qd, inner_d)
-        inner_x, edge_x = finish(pd, qd, inner_d, inner, EDGE)
+        vs = lax.ppermute(tokens, "tp", to_second)
+        inner, = stream_mm([tokens], [0], [inner_weight], None)
+        vf = lax.ppermute(tie(tokens, inner), "tp", to_first)
+        vs = tie(vs, inner)
+        vd = lax.ppermute(vs, "tp", to_first)
+        qs = flip(vs, "tp", 1)
+        qf = flip(vf, "tp", 1)
+        inner_w, gate_w = held(inner_weight), held(gate_weight)
+        inner, = mm([p1, vs, qs, vf, qf], [1, 20, 11, 10, 21], inner_w, inner)
+        vd = tie(vd, inner)
+        qd = flip(vd, "tp", 1)
+        inner_x, edge_x = mm([vd, qd], [6, 7], inner_w, inner, EDGE)
     else:
         piece = lax.all_gather(tokens, "tp", axis=1, tiled=True)
         inner_x = jnp.dot(piece, inner_weight, preferred_element_type=F32).astype(BF16)
@@ -562,48 +509,45 @@
         edge_x = inner_x[rows - EDGE :]
 
     tail = lax.ppermute(edge_x, "ctx", shift)
-    if square:
-        gate_acc, = mm([px], [2], [gate_weight], [tie(gate_acc, edge_x)])
-        tail = tie(tail, gate_acc)
     conv_x, send, keep = conv_proj(
         inner_x, tail, conv_weight, conv_bias[None, :], proj_wt, square
     )
     if square:
         part = add(keep, flip(send, "tp", 1))
         quarter = [flip(part, "tp", m) for m in (2, 4, 6)]
-        cols_away = fetch_cols([7, 21, 11, 1], out_weight, feat, part)
-        quarter = [tie(v, cols_away) for v in quarter]
+        blocks = [tokens, p1, vs, qs, vf, qf, vd, qd]
+        gate_acc, = mm(
+            [tie(tokens, part), *blocks[1:]], [0, 1, 20, 11, 10, 21, 6, 7], gate_w, None
+        )
+        quarter = [tie(v, gate_acc) for v in quarter]
         mine = add(part, *quarter)
         parts = (mine, flip(mine, "tp", 1))
     else:
         parts = (lax.psum(keep, "tp"),)
-    end, y, cum, bc = scan(
+    end, packet, y, cum, bc = scan(
         parts, conv_x, step_weight, step_bias[None, :], decay_t, carried_t
     )
 
     group, ent, bit = end, None, 1
     while bit * 2 < n_ctx:
-        got = flip(group, "ctx", bit)
-        if square and bit == 1:
-            gate_acc, = mm([qx, py, qy], [3, 4, 5], [gate_weight], [tie(gate_acc, group)])
-            got = tie(got, gate_acc)
-        group, ent = merge(bit, decay_t, group, got, ent)
+        got = flip(packet, "ctx", bit)
+        group, packet, ent = merge(bit, decay_t, group, got, ent)
         bit *= 2
     pairs = [(i, i ^ bit) for i in range(n_ctx) if (i // bit) % 2 == 0]
-    got = lax.ppermute(group, "ctx", pairs)
-    if square:
-        gate_acc, = mm([pd, qd], [6, 7], [gate_weight], [tie(gate_acc, group)])
-        got = tie(got, gate_acc)
+    got = lax.ppermute(packet, "ctx", pairs)
     gated, bound = gating(
         bit, y, cum, bc, end, got, ent, decay_t, conv_x, skip_gain[None, :], gate_acc
     )
     if square:
-        away = out_held(gated, cols_away)
+        out_weight = pltpu.with_memory_space_constraint(out_weight, VMEM)
+        away = out_blocks(gated, out_weight, [7, 21], feat)
         got = flip(away, "tp", 1)
-        near = out_blocks(gated, out_weight, [6, 10, 20, 0], feat)
-        sd, sf, ss, so = add_pair(near, got)
-        to_first = [(i, i ^ (2 + 2 * (i % 2))) for i in range(n_tp)]
-        to_second = [(i, i ^ (4 - 2 * (i % 2))) for i in range(n_tp)]
+        away_b = out_blocks(gated, out_weight, [11, 1], feat)
+        got_b = flip(away_b, "tp", 1)
+        near = out_blocks(gated, out_weight, [6, 10], feat)
+        sd, sf = add_pair(near, tie(got, away_b))
+        near_b = out_blocks(gated, out_weight, [20, 0], feat)
+        ss, so = add_pair(near_b, got_b)
         rd = lax.ppermute(sd, "tp", to_first)
         rf = lax.ppermute(sf, "tp", to_first)
         rs = lax.ppermute(add(ss, rd), "tp", to_second)

time: 79.5 us -> 72.5 us (0.912)
  Pallas kernels: 34.8 us -> 18.9 us
  waiting for transfers between devices: 19.1 us -> 28.3 us
  local copies, waits for them, and re-layouts: 1.03 us -> 0.1 us
  starting transfers between devices: 23.3 us -> 24.1 us
    pallas_call x10 -> x8, Pallas kernels: 26.9 us -> 10.4 us  [the longest x3 4.62 us: mm(): pl.pallas_call(functools.partial(mm_kernel, roles, len(extra), edge), in_...]
    ppermute x1 -> x4, waiting for transfers between devices: 0.01 us -> 9.57 us  [the longest x1 4.46 us: on_device(): vf = lax.ppermute(tie(tokens, inner), 'tp', to_first)]
    ppermute x1 -> x4, starting transfers between devices: 4.75 us -> 10.9 us  [the longest x1 4.93 us: on_device(): got = lax.ppermute(packet, 'ctx', pairs)]
    ppermute x14 -> x12, starting transfers between devices: 12.4 us -> 7.03 us  [flip(): return lax.ppermute(value, axis, [(i, i ^ mask) for i in range(peers)])]
    ppermute x1, waiting for transfers between devices: 0.01 us -> 1.43 us  [on_device(): tail = lax.ppermute(edge_x, 'ctx', shift)]
    ppermute x14 -> x12, waiting for transfers between devices: 8.84 us -> 7.78 us  [flip(): return lax.ppermute(value, axis, [(i, i ^ mask) for i in range(peers)])]
    unnamed x18 -> x36, local copies, waits for them, and re-layouts: 1.03 us -> 0.1 us
    ppermute x1, waiting for transfers between devices: 4.35 us -> 3.42 us  [on_device(): rd = lax.ppermute(sd, 'tp', to_first)]
  transfers between devices with their start and end apart: 19 -> 20, of which waited for: 10 -> 16; matrix products, arithmetic and copies ran while one was open for 0% -> 0% of each run, Pallas kernels for 32% -> 13%
where the time goes in v1:
time: 72.5 us; the launch traced here: 72.3 us
  waiting for transfers between devices  28.3 us (39%)
  starting transfers between devices  24.1 us (33%)
  Pallas kernels  18.9 us (26%)
  between operations  0.95 us (1%)
    ppermute x12, waiting for transfers between devices, flip(): return lax.ppermute(value, axis, [(i, i ^ mask) for i in range(peers)])  7.78 us
    ppermute x12, starting transfers between devices, flip(): return lax.ppermute(value, axis, [(i, i ^ mask) for i in range(peers)])  7.03 us
    ppermute x1, starting transfers between devices, on_device(): got = lax.ppermute(packet, 'ctx', pairs)  4.93 us
    pallas_call x3, Pallas kernels, mm(): pl.pallas_call(functools.partial(mm_kernel, roles, len(extra), edge), in_...  4.62 us
    ppermute x1, waiting for transfers between devices, on_device(): vf = lax.ppermute(tie(tokens, inner), 'tp', to_first)  4.46 us
    ppermute x1, starting transfers between devices, on_device(): tail = lax.ppermute(edge_x, 'ctx', shift)  3.65 us
    pallas_call x1, Pallas kernels, scan(): pl.pallas_call(functools.partial(scan_kernel, len(parts) == 2), in_specs=...  3.53 us
    ppermute x1, waiting for transfers between devices, on_device(): rd = lax.ppermute(sd, 'tp', to_first)  3.42 us
  transfers between devices with their start and end apart: 20, of which 16 were waited for; matrix products, arithmetic and copies ran while one was open for 0% of the time, Pallas kernels for 13%

profile of v1, /device:TPU:0, one launch (start us, length us, event | category | flops | bytes accessed | tf_op | source)
XLA Modules:
  0.0 72.3 jit_solution(14221007232329947770)
XLA Ops:
  0.6 3.1 %collective-permute-start = (bf16[128,1024]{1,0:T(8,128)(2,1)}, bf16[128,1024]{1,0:T(8,128)(2,1)S(1)}, u32[]{:S(2)}, u32[]{:S(2)}) collective-permute-start(bf16[128,1024]{1,0:T(8,128)(2,1)} %refs_0_.2), channel_id=1, source_target_pairs={{0,4},{1,3},{2,6},{3,1},{4,0},{5,7},{6,2},{7,5},{8,12},{9,11},{10,... | collective-permute-start | bytes 786440 | tf_op jit(solution)/shard_map/ppermute | solution.py:493
  3.7 2.8 %shard_map.131.refs_6_ = f32[128,1024]{1,0:T(8,128)S(1)} custom-call(bf16[128,1024]{1,0:T(8,128)(2,1)} %refs_0_.2, bf16[8192,1024]{1,0:T(8,128)(2,1)} %refs_2_.1), custom_call_target="tpu_custom_call" | custom-call | flops 268435456 | bytes 2097152 | tf_op jit(solution)/shard_map/pallas_call | solution.py:117
  6.6 1.5 %collective-permute-start.4 = (bf16[128,1024]{1,0:T(8,128)(2,1)S(1)}, bf16[128,1024]{1,0:T(8,128)(2,1)S(1)}, u32[]{:S(2)}, u32[]{:S(2)}) collective-permute-start(bf16[128,1024]{1,0:T(8,128)(2,1)S(1)} %copy-done.2), channel_id=1, source_target_pairs={{0,2},{1,5},{2,0},{3,7},{4,6},{5,1},{6,4},{7,3},{8,10},{9,13},{10,... | collective-permute-start | bytes 786440 | tf_op jit(solution)/shard_map/ppermute | solution.py:495
  8.1 0.2 collective-permute-done.refs_1_.refs_2_
  8.3 0.3 collective-permute-start.3
  8.6 4.5 %collective-permute-done.4.refs_3_.refs_4_ = bf16[128,1024]{1,0:T(8,128)(2,1)S(1)} collective-permute-done((bf16[128,1024]{1,0:T(8,128)(2,1)S(1)}, bf16[128,1024]{1,0:T(8,128)(2,1)S(1)}, u32[]{:S(2)}, u32[]{:S(2)}) %collective-permute-start.4) | collective-permute-done | bytes 262176 | tf_op jit(solution)/shard_map/ppermute | solution.py:495
  13.1 1.4 %collective-permute-start.1 = (bf16[128,1024]{1,0:T(8,128)(2,1)S(1)}, bf16[128,1024]{1,0:T(8,128)(2,1)S(1)}, u32[]{:S(2)}, u32[]{:S(2)}) collective-permute-start(bf16[128,1024]{1,0:T(8,128)(2,1)S(1)} %collective-permute-done.refs_1_.refs_2_), channel_id=1, source_target_pairs={{0,2},{1,5},{2,0},{3,7},{4,6},{5,1},{6,4},{7,3},{8,10},{9,13},{10,... | collective-permute-start | bytes 786440 | tf_op jit(solution)/shard_map/ppermute | solution.py:497
  14.5 0.1 collective-permute-done.5.refs_4_.refs_5_
  14.6 1.5 %shard_map.132.refs_3_ = f32[128,1024]{1,0:T(8,128)S(1)} custom-call(bf16[128,1024]{1,0:T(8,128)(2,1)S(1)} %collective-permute-done.2.refs_0_.refs_1_, bf16[128,1024]{1,0:T(8,128)(2,1)S(1)} %collective-permute-done.refs_1_.refs_2_, bf16[128,1024]{1,0:T(8,128)(2,1)S(1)} %collective-permute-done.3.refs_2_.refs_3_, ...), custom_call_target="tpu_custom_call" | custom-call | flops 1342177280 | bytes 10485760 | tf_op jit(solution)/shard_map/pallas_call | solution.py:162
  16.2 3.2 %collective-permute-done.1.refs_0_.refs_6_ = bf16[128,1024]{1,0:T(8,128)(2,1)S(1)} collective-permute-done((bf16[128,1024]{1,0:T(8,128)(2,1)S(1)}, bf16[128,1024]{1,0:T(8,128)(2,1)S(1)}, u32[]{:S(2)}, u32[]{:S(2)}) %collective-permute-start.1) | collective-permute-done | bytes 262176 | tf_op jit(solution)/shard_map/ppermute | solution.py:497
  19.4 1.5 %collective-permute-done.6.refs_1_.refs_7_ = bf16[128,1024]{1,0:T(8,128)(2,1)S(1)} collective-permute-done((bf16[128,1024]{1,0:T(8,128)(2,1)S(1)}, bf16[128,1024]{1,0:T(8,128)(2,1)S(1)}, u32[]{:S(2)}, u32[]{:S(2)}) %collective-permute-start.6) | collective-permute-done | bytes 262176 | tf_op jit(solution)/shard_map/ppermute | solution.py:24
  21.0 0.7 %shard_map.133 = (bf16[128,1024]{1,0:T(8,128)(2,1)S(1)}, bf16[8,1024]{1,0:T(8,128)(2,1)S(1)}) custom-call(bf16[128,1024]{1,0:T(8,128)(2,1)S(1)} %collective-permute-done.1.refs_0_.refs_6_, bf16[128,1024]{1,0:T(8,128)(2,1)S(1)} %collective-permute-done.6.refs_1_.refs_7_, bf16[8192,1024]{1,0:T(8,128)(2,1)S(1)} %copy-done, f32[128,1024]{1,0:T(8,128)S(1)} %shard_map.132.refs_3_), custom_call_target="tpu_custom_call" | custom-call | flops 536870912 | bytes 4194304 | tf_op jit(solution)/shard_map/pallas_call | solution.py:162
  21.7 3.7 %collective-permute-start.7 = (bf16[8,1024]{1,0:T(8,128)(2,1)S(1)}, bf16[8,1024]{1,0:T(8,128)(2,1)S(1)}, u32[]{:S(2)}, u32[]{:S(2)}) collective-permute-start(bf16[8,1024]{1,0:T(8,128)(2,1)S(1)} %get-tuple-element.32), channel_id=1, source_target_pairs={{0,8},{8,16},{16,24},{1,9},{9,17},{17,25},{2,10},{10,18},{18,26},{... | collective-permute-start | bytes 49160 | tf_op jit(solution)/shard_map/ppermute | solution.py:511
  25.4 1.4 %collective-permute-done.7.tail_ref = bf16[8,1024]{1,0:T(8,128)(2,1)S(1)} collective-permute-done((bf16[8,1024]{1,0:T(8,128)(2,1)S(1)}, bf16[8,1024]{1,0:T(8,128)(2,1)S(1)}, u32[]{:S(2)}, u32[]{:S(2)}) %collective-permute-start.7) | collective-permute-done | bytes 16416 | tf_op jit(solution)/shard_map/ppermute | solution.py:511
  26.8 0.9 %shard_map.134 = (bf16[128,1024]{1,0:T(8,128)(2,1)S(1)}, bf16[64,544]{1,0:T(8,128)(2,1)S(1)}, f32[64,544]{1,0:T(8,128)S(1)}) custom-call(bf16[128,1024]{1,0:T(8,128)(2,1)S(1)} %get-tuple-element.31.x_ref, bf16[8,1024]{1,0:T(8,128)(2,1)S(1)} %collective-permute-done.7.tail_ref, f32[4,1024]{1,0:T(4,128)S(1)} %copy-done.4, f32[1,1024]{1,0:T(1,128)S(1)} %bitcast.17, ...), custom_call_target="tpu_custom_call" | custom-call | flops 142606336 | bytes 1114112 | tf_op jit(solution)/shard_map/pallas_call | solution.py:200
  27.7 0.1 collective-permute-start.8
  27.8 1.3 %collective-permute-done.8.refs_1_ = bf16[64,544]{1,0:T(8,128)(2,1)S(1)} collective-permute-done((bf16[64,544]{1,0:T(8,128)(2,1)S(1)}, bf16[64,544]{1,0:T(8,128)(2,1)S(1)}, u32[]{:S(2)}, u32[]{:S(2)}) %collective-permute-start.8) | collective-permute-done | bytes 69664 | tf_op jit(solution)/shard_map/ppermute | solution.py:24
  29.1 1.2 %collective-permute-start.11 = (bf16[64,544]{1,0:T(8,128)(2,1)S(1)}, bf16[64,544]{1,0:T(8,128)(2,1)S(1)}, u32[]{:S(2)}, u32[]{:S(2)}) collective-permute-start(bf16[64,544]{1,0:T(8,128)(2,1)S(1)} %shard_map.135.refs_0_), channel_id=1, source_target_pairs={{0,6},{1,7},{2,4},{3,5},{4,2},{5,3},{6,0},{7,1},{8,14},{9,15},{10,... | collective-permute-start | bytes 208904 | tf_op jit(solution)/shard_map/ppermute | solution.py:24
  30.3 1.8 %collective-permute-start.10 = (bf16[64,544]{1,0:T(8,128)(2,1)S(1)}, bf16[64,544]{1,0:T(8,128)(2,1)S(1)}, u32[]{:S(2)}, u32[]{:S(2)}) collective-permute-start(bf16[64,544]{1,0:T(8,128)(2,1)S(1)} %shard_map.135.refs_0_), channel_id=1, source_target_pairs={{0,4},{1,5},{2,6},{3,7},{4,0},{5,1},{6,2},{7,3},{8,12},{9,13},{10,... | collective-permute-start | bytes 208904 | tf_op jit(solution)/shard_map/ppermute | solution.py:24
  32.1 0.5 collective-permute-start.9
  32.7 2.4 %shard_map.136.gate_ref = f32[128,1024]{1,0:T(8,128)S(1)} custom-call(bf16[128,1024]{1,0:T(8,128)(2,1)S(1)} %copy-done.2, bf16[128,1024]{1,0:T(8,128)(2,1)S(1)} %collective-permute-done.2.refs_0_.refs_1_, bf16[128,1024]{1,0:T(8,128)(2,1)S(1)} %collective-permute-done.refs_1_.refs_2_, bf16[128,1024]{1,0:T(8,128)(2,1)S(1)} %collective-permute-done.3.refs_2_.refs_3_, ...), custom_call_target="tpu_custom_call" | custom-call | flops 2147483648 | bytes 16777216 | tf_op jit(solution)/shard_map/pallas_call | solution.py:162
  35.0 0.1 collective-permute-done.11.refs_3_
  35.1 1.2 %collective-permute-done.10.refs_2_ = bf16[64,544]{1,0:T(8,128)(2,1)S(1)} collective-permute-done((bf16[64,544]{1,0:T(8,128)(2,1)S(1)}, bf16[64,544]{1,0:T(8,128)(2,1)S(1)}, u32[]{:S(2)}, u32[]{:S(2)}) %collective-permute-start.10) | collective-permute-done | bytes 69664 | tf_op jit(solution)/shard_map/ppermute | solution.py:24
  36.3 0.2 collective-permute-done.9.refs_1_
  36.6 0.1 collective-permute-start.12
  36.7 1.3 %collective-permute-done.12.refs_1_ = bf16[64,544]{1,0:T(8,128)(2,1)S(1)} collective-permute-done((bf16[64,544]{1,0:T(8,128)(2,1)S(1)}, bf16[64,544]{1,0:T(8,128)(2,1)S(1)}, u32[]{:S(2)}, u32[]{:S(2)}) %collective-permute-start.12) | collective-permute-done | bytes 69664 | tf_op jit(solution)/shard_map/ppermute | solution.py:24
  38.0 3.5 %shard_map.138 = (f32[17,1024]{1,0:T(8,128)S(1)}, bf16[17,1024]{1,0:T(8,128)(2,1)S(1)}, f32[1024,128]{1,0:T(8,128)S(1)}, f32[1024,128]{1,0:T(8,128)S(1)}, f32[2048,128]{1,0:T(8,128)S(1)}) custom-call(bf16[64,544]{1,0:T(8,128)(2,1)S(1)} %shard_map.137.refs_0_, bf16[64,544]{1,0:T(8,128)(2,1)S(1)} %collective-permute-done.12.refs_1_, ...), custom_call_target="tpu_custom_call" | custom-call | flops 16777216 | bytes 1048576 | tf_op jit(solution)/shard_map/pallas_call | solution.py:293
  41.5 2.4 %collective-permute-start.13 = (bf16[17,1024]{1,0:T(8,128)(2,1)S(1)}, bf16[17,1024]{1,0:T(8,128)(2,1)S(1)}, u32[]{:S(2)}, u32[]{:S(2)}) collective-permute-start(bf16[17,1024]{1,0:T(8,128)(2,1)S(1)} %get-tuple-element.44), channel_id=1, source_target_pairs={{0,8},{8,0},{16,24},{24,16},{1,9},{9,1},{17,25},{25,17},{2,10},{10... | collective-permute-start | bytes 104456 | tf_op jit(solution)/shard_map/ppermute | solution.py:24
  43.9 2.1 %collective-permute-done.13.got_ref = bf16[17,1024]{1,0:T(8,128)(2,1)S(1)} collective-permute-done((bf16[17,1024]{1,0:T(8,128)(2,1)S(1)}, bf16[17,1024]{1,0:T(8,128)(2,1)S(1)}, u32[]{:S(2)}, u32[]{:S(2)}) %collective-permute-start.13) | collective-permute-done | bytes 34848 | tf_op jit(solution)/shard_map/ppermute | solution.py:24
  45.9 0.7 shard_map.139
  46.6 4.9 %collective-permute-start.14 = (bf16[17,1024]{1,0:T(8,128)(2,1)S(1)}, bf16[17,1024]{1,0:T(8,128)(2,1)S(1)}, u32[]{:S(2)}, u32[]{:S(2)}) collective-permute-start(bf16[17,1024]{1,0:T(8,128)(2,1)S(1)} %get-tuple-element.45), channel_id=1, source_target_pairs={{0,16},{8,24},{1,17},{9,25},{2,18},{10,26},{3,19},{11,27},{4,20},{... | collective-permute-start | bytes 104456 | tf_op jit(solution)/shard_map/ppermute | solution.py:537
  51.6 1.7 %collective-permute-done.14.got_ref = bf16[17,1024]{1,0:T(8,128)(2,1)S(1)} collective-permute-done((bf16[17,1024]{1,0:T(8,128)(2,1)S(1)}, bf16[17,1024]{1,0:T(8,128)(2,1)S(1)}, u32[]{:S(2)}, u32[]{:S(2)}) %collective-permute-start.14) | collective-permute-done | bytes 34848 | tf_op jit(solution)/shard_map/ppermute | solution.py:537
  53.3 2.3 %shard_map.140 = (bf16[128,1024]{1,0:T(8,128)(2,1)S(1)}, f32[16,1024]{1,0:T(8,128)}) custom-call(f32[1024,128]{1,0:T(8,128)S(1)} %get-tuple-element.40.y_ref, f32[1024,128]{1,0:T(8,128)S(1)} %get-tuple-element.41.cum_ref, f32[2048,128]{1,0:T(8,128)S(1)} %get-tuple-element.42.c_ref, f32[17,1024]{1,0:T(8,128)S(1)} %get-tuple-element.43.group_ref.end_ref, ...), custom_call_target="tpu_custom_call" | custom-call | flops 12582912 | bytes 1048576 | tf_op jit(solution)/shard_map/pallas_call | solution.py:437
  55.6 0.7 %shard_map.145 = bf16[2,128,1024]{2,1,0:T(8,128)(2,1)S(1)} custom-call(bf16[128,1024]{1,0:T(8,128)(2,1)S(1)} %get-tuple-element.47.g_ref, bf16[1024,8192]{1,0:T(8,128)(2,1)S(1)} %bitcast.10), custom_call_target="tpu_custom_call" | custom-call | flops 536870912 | bytes 4194304 | tf_op jit(solution)/shard_map/pallas_call | solution.py:466
  56.3 0.1 collective-permute-start.16
  56.4 0.7 %shard_map.142 = bf16[2,128,1024]{2,1,0:T(8,128)(2,1)S(1)} custom-call(bf16[128,1024]{1,0:T(8,128)(2,1)S(1)} %get-tuple-element.47.g_ref, bf16[1024,8192]{1,0:T(8,128)(2,1)S(1)} %bitcast.10), custom_call_target="tpu_custom_call" | custom-call | flops 536870912 | bytes 4194304 | tf_op jit(solution)/shard_map/pallas_call | solution.py:466
  57.1 0.5 collective-permute-start.15
  57.7 0.7 shard_map.144.a_ref
  58.4 0.1 shard_map.146
  58.6 0.6 collective-permute-start.18
  59.2 0.7 shard_map.141.a_ref
  59.9 1.6 %collective-permute-start.17 = (bf16[128,1024]{1,0:T(8,128)(2,1)S(1)}, bf16[128,1024]{1,0:T(8,128)(2,1)S(1)}, u32[]{:S(2)}, u32[]{:S(2)}) collective-permute-start(bf16[128,1024]{1,0:T(8,128)(2,1)S(1)} %get-tuple-element.50), channel_id=1, source_target_pairs={{0,2},{1,5},{2,0},{3,7},{4,6},{5,1},{6,4},{7,3},{8,10},{9,13},{10,... | collective-permute-start | bytes 786440 | tf_op jit(solution)/shard_map/ppermute | solution.py:552
  61.4 0.1 shard_map.143
  61.6 3.4 %collective-permute-done.18.refs_1_ = bf16[128,1024]{1,0:T(8,128)(2,1)S(1)} collective-permute-done((bf16[128,1024]{1,0:T(8,128)(2,1)S(1)}, bf16[128,1024]{1,0:T(8,128)(2,1)S(1)}, u32[]{:S(2)}, u32[]{:S(2)}) %collective-permute-start.18) | collective-permute-done | bytes 262176 | tf_op jit(solution)/shard_map/ppermute | solution.py:551
  65.1 0.4 collective-permute-start.19
  65.4 3.3 %collective-permute-done.17.refs_1_ = bf16[128,1024]{1,0:T(8,128)(2,1)S(1)} collective-permute-done((bf16[128,1024]{1,0:T(8,128)(2,1)S(1)}, bf16[128,1024]{1,0:T(8,128)(2,1)S(1)}, u32[]{:S(2)}, u32[]{:S(2)}) %collective-permute-start.17) | collective-permute-done | bytes 262176 | tf_op jit(solution)/shard_map/ppermute | solution.py:552
  68.7 2.8 %collective-permute-done.19.refs_2_ = bf16[128,1024]{1,0:T(8,128)(2,1)S(1)} collective-permute-done((bf16[128,1024]{1,0:T(8,128)(2,1)S(1)}, bf16[128,1024]{1,0:T(8,128)(2,1)S(1)}, u32[]{:S(2)}, u32[]{:S(2)}) %collective-permute-start.19) | collective-permute-done | bytes 262176 | tf_op jit(solution)/shard_map/ppermute | solution.py:553
  71.5 0.8 %shard_map.148 = bf16[128,1024]{1,0:T(8,128)(2,1)} custom-call(bf16[128,1024]{1,0:T(8,128)(2,1)S(1)} %get-tuple-element.48.refs_0_, bf16[128,1024]{1,0:T(8,128)(2,1)S(1)} %collective-permute-done.17.refs_1_, bf16[128,1024]{1,0:T(8,128)(2,1)S(1)} %collective-permute-done.19.refs_2_), custom_call_target="tpu_custom_call" | custom-call | flops 393216 | bytes 786432 | tf_op jit(solution)/shard_map/pallas_call | solution.py:328
  (48 shorter events, 0.3 us)
Async XLA Ops:
  0.6 5.9 %copy-start.2 = (bf16[128,1024]{1,0:T(8,128)(2,1)S(1)}, bf16[128,1024]{1,0:T(8,128)(2,1)}, u32[]{:S(2)}) copy-start(bf16[128,1024]{1,0:T(8,128)(2,1)} %refs_0_.2) | copy-start | bytes 786436
  0.6 14.0 %copy-start = (bf16[8192,1024]{1,0:T(8,128)(2,1)S(1)}, bf16[8192,1024]{1,0:T(8,128)(2,1)}, u32[]{:S(2)}) copy-start(bf16[8192,1024]{1,0:T(8,128)(2,1)} %refs_2_.1) | copy-start | bytes 50331652
  0.6 7.6 %collective-permute-start = (bf16[128,1024]{1,0:T(8,128)(2,1)}, bf16[128,1024]{1,0:T(8,128)(2,1)S(1)}, u32[]{:S(2)}, u32[]{:S(2)}) collective-permute-start(bf16[128,1024]{1,0:T(8,128)(2,1)} %refs_0_.2), channel_id=1, source_target_pairs={{0,4},{1,3},{2,6},{3,1},{4,0},{5,7},{6,2},{7,5},{8,12},{9,11},{10,... | collective-permute-start | bytes 786440 | tf_op jit(solution)/shard_map/ppermute | solution.py:493
  6.6 20.2 %copy-start.1 = (bf16[1024,544]{0,1:T(8,128)(2,1)S(1)}, bf16[1024,544]{0,1:T(8,128)(2,1)}, u32[]{:S(2)}) copy-start(bf16[1024,544]{0,1:T(8,128)(2,1)} %param.17) | copy-start | bytes 3342340
  6.6 20.2 %copy-start.4 = (f32[4,1024]{1,0:T(4,128)S(1)}, f32[4,1024]{1,0:T(4,128)}, u32[]{:S(2)}) copy-start(f32[4,1024]{1,0:T(4,128)} %w_ref.5) | copy-start | bytes 49156
  6.6 20.2 %copy-start.5 = (f32[1024]{0:T(1024)S(1)}, f32[1024]{0:T(1024)}, u32[]{:S(2)}) copy-start(f32[1024]{0:T(1024)} %param.16) | copy-start | bytes 12292
  6.6 26.1 %slice-start.4 = ((s8[16777216]{0:T(1024)(128)(4,1)}), s8[4194304]{0:T(1024)(128)(4,1)S(1)}, s32[]{:S(2)}) async-start(s8[16777216]{0:T(1024)(128)(4,1)} %bitcast.11), calls=%async_computation.4 | async-start | bytes 8388608
  6.6 26.0 %slice-start.5 = ((s8[16777216]{0:T(1024)(128)(4,1)}), s8[4194304]{0:T(1024)(128)(4,1)S(1)}, s32[]{:S(2)}) async-start(s8[16777216]{0:T(1024)(128)(4,1)} %bitcast.11), calls=%async_computation.5 | async-start | bytes 8388608
  6.6 6.4 %collective-permute-start.4 = (bf16[128,1024]{1,0:T(8,128)(2,1)S(1)}, bf16[128,1024]{1,0:T(8,128)(2,1)S(1)}, u32[]{:S(2)}, u32[]{:S(2)}) collective-permute-start(bf16[128,1024]{1,0:T(8,128)(2,1)S(1)} %copy-done.2), channel_id=1, source_target_pairs={{0,2},{1,5},{2,0},{3,7},{4,6},{5,1},{6,4},{7,3},{8,10},{9,13},{10,... | collective-permute-start | bytes 786440 | tf_op jit(solution)/shard_map/ppermute | solution.py:495
  8.1 6.4 %collective-permute-start.2 = (bf16[128,1024]{1,0:T(8,128)(2,1)S(1)}, bf16[128,1024]{1,0:T(8,128)(2,1)S(1)}, u32[]{:S(2)}, u32[]{:S(2)}) collective-permute-start(bf16[128,1024]{1,0:T(8,128)(2,1)S(1)} %copy-done.2), channel_id=1, source_target_pairs={{0,1},{1,0},{2,3},{3,2},{4,5},{5,4},{6,7},{7,6},{8,9},{9,8},{10,11... | collective-permute-start | bytes 786440 | tf_op jit(solution)/shard_map/ppermute | solution.py:24
  8.3 6.2 %collective-permute-start.3 = (bf16[128,1024]{1,0:T(8,128)(2,1)S(1)}, bf16[128,1024]{1,0:T(8,128)(2,1)S(1)}, u32[]{:S(2)}, u32[]{:S(2)}) collective-permute-start(bf16[128,1024]{1,0:T(8,128)(2,1)S(1)} %collective-permute-done.refs_1_.refs_2_), channel_id=1, source_target_pairs={{0,1},{1,0},{2,3},{3,2},{4,5},{5,4},{6,7},{7,6},{8,9},{9,8},{10,11... | collective-permute-start | bytes 786440 | tf_op jit(solution)/shard_map/ppermute | solution.py:24
  13.1 1.5 %collective-permute-start.5 = (bf16[128,1024]{1,0:T(8,128)(2,1)S(1)}, bf16[128,1024]{1,0:T(8,128)(2,1)S(1)}, u32[]{:S(2)}, u32[]{:S(2)}) collective-permute-start(bf16[128,1024]{1,0:T(8,128)(2,1)S(1)} %collective-permute-done.4.refs_3_.refs_4_), channel_id=1, source_target_pairs={{0,1},{1,0},{2,3},{3,2},{4,5},{5,4},{6,7},{7,6},{8,9},{9,8},{10,11... | collective-permute-start | bytes 786440 | tf_op jit(solution)/shard_map/ppermute | solution.py:24
  13.1 6.4 %collective-permute-start.1 = (bf16[128,1024]{1,0:T(8,128)(2,1)S(1)}, bf16[128,1024]{1,0:T(8,128)(2,1)S(1)}, u32[]{:S(2)}, u32[]{:S(2)}) collective-permute-start(bf16[128,1024]{1,0:T(8,128)(2,1)S(1)} %collective-permute-done.refs_1_.refs_2_), channel_id=1, source_target_pairs={{0,2},{1,5},{2,0},{3,7},{4,6},{5,1},{6,4},{7,3},{8,10},{9,13},{10,... | collective-permute-start | bytes 786440 | tf_op jit(solution)/shard_map/ppermute | solution.py:497
  16.2 16.5 %slice-start.6 = ((s8[16777216]{0:T(1024)(128)(4,1)}), s8[4194304]{0:T(1024)(128)(4,1)S(1)}, s32[]{:S(2)}) async-start(s8[16777216]{0:T(1024)(128)(4,1)} %bitcast.11), calls=%async_computation.6 | async-start | bytes 8388608
  16.2 16.5 %slice-start.7 = ((s8[16777216]{0:T(1024)(128)(4,1)}), s8[4194304]{0:T(1024)(128)(4,1)S(1)}, s32[]{:S(2)}) async-start(s8[16777216]{0:T(1024)(128)(4,1)} %bitcast.11), calls=%async_computation.7 | async-start | bytes 8388608
  16.2 21.8 %copy-start.3 = (f32[1024,16]{0,1:T(8,128)S(1)}, f32[1024,16]{0,1:T(8,128)}, u32[]{:S(2)}) copy-start(f32[1024,16]{0,1:T(8,128)} %param.20) | copy-start | bytes 196612
  16.2 21.8 %copy-start.6 = (bf16[512,1024]{1,0:T(8,128)(2,1)S(1)}, bf16[512,1024]{1,0:T(8,128)(2,1)}, u32[]{:S(2)}) copy-start(bf16[512,1024]{1,0:T(8,128)(2,1)} %refs_3_.1) | copy-start | bytes 3145732
  16.2 21.8 %copy-start.7 = (f32[1024,16]{0,1:T(8,128)S(1)}, f32[1024,16]{0,1:T(8,128)}, u32[]{:S(2)}) copy-start(f32[1024,16]{0,1:T(8,128)} %param.23) | copy-start | bytes 196612
  16.2 21.8 %copy-start.8 = (f32[1024]{0:T(1024)S(1)}, f32[1024]{0:T(1024)}, u32[]{:S(2)}) copy-start(f32[1024]{0:T(1024)} %param.19) | copy-start | bytes 12292
  19.4 1.5 %collective-permute-start.6 = (bf16[128,1024]{1,0:T(8,128)(2,1)S(1)}, bf16[128,1024]{1,0:T(8,128)(2,1)S(1)}, u32[]{:S(2)}, u32[]{:S(2)}) collective-permute-start(bf16[128,1024]{1,0:T(8,128)(2,1)S(1)} %collective-permute-done.1.refs_0_.refs_6_), channel_id=1, source_target_pairs={{0,1},{1,0},{2,3},{3,2},{4,5},{5,4},{6,7},{7,6},{8,9},{9,8},{10,11... | collective-permute-start | bytes 786440 | tf_op jit(solution)/shard_map/ppermute | solution.py:24
  21.0 34.6 %slice-start = ((s8[16777216]{0:T(1024)(128)(4,1)}), s8[4194304]{0:T(1024)(128)(4,1)S(1)}, s32[]{:S(2)}) async-start(s8[16777216]{0:T(1024)(128)(4,1)} %bitcast.9), calls=%async_computation | async-start | bytes 8388608
  21.0 34.6 %slice-start.1 = ((s8[16777216]{0:T(1024)(128)(4,1)}), s8[4194304]{0:T(1024)(128)(4,1)S(1)}, s32[]{:S(2)}) async-start(s8[16777216]{0:T(1024)(128)(4,1)} %bitcast.9), calls=%async_computation.1 | async-start | bytes 8388608
  21.7 31.6 %copy-start.9 = (f32[1024]{0:T(1024)S(1)}, f32[1024]{0:T(1024)}, u32[]{:S(2)}) copy-start(f32[1024]{0:T(1024)} %param.21) | copy-start | bytes 12292
  21.7 5.1 %collective-permute-start.7 = (bf16[8,1024]{1,0:T(8,128)(2,1)S(1)}, bf16[8,1024]{1,0:T(8,128)(2,1)S(1)}, u32[]{:S(2)}, u32[]{:S(2)}) collective-permute-start(bf16[8,1024]{1,0:T(8,128)(2,1)S(1)} %get-tuple-element.32), channel_id=1, source_target_pairs={{0,8},{8,16},{16,24},{1,9},{9,17},{17,25},{2,10},{10,18},{18,26},{... | collective-permute-start | bytes 49160 | tf_op jit(solution)/shard_map/ppermute | solution.py:511
  27.7 1.3 %collective-permute-start.8 = (bf16[64,544]{1,0:T(8,128)(2,1)S(1)}, bf16[64,544]{1,0:T(8,128)(2,1)S(1)}, u32[]{:S(2)}, u32[]{:S(2)}) collective-permute-start(bf16[64,544]{1,0:T(8,128)(2,1)S(1)} %get-tuple-element.34), channel_id=1, source_target_pairs={{0,1},{1,0},{2,3},{3,2},{4,5},{5,4},{6,7},{7,6},{8,9},{9,8},{10,11... | collective-permute-start | bytes 208904 | tf_op jit(solution)/shard_map/ppermute | solution.py:24
  29.1 26.5 %slice-start.2 = ((s8[16777216]{0:T(1024)(128)(4,1)}), s8[4194304]{0:T(1024)(128)(4,1)S(1)}, s32[]{:S(2)}) async-start(s8[16777216]{0:T(1024)(128)(4,1)} %bitcast.9), calls=%async_computation.2 | async-start | bytes 8388608
  29.1 26.5 %slice-start.3 = ((s8[16777216]{0:T(1024)(128)(4,1)}), s8[4194304]{0:T(1024)(128)(4,1)S(1)}, s32[]{:S(2)}) async-start(s8[16777216]{0:T(1024)(128)(4,1)} %bitcast.9), calls=%async_computation.3 | async-start | bytes 8388608
  29.1 6.0 %collective-permute-start.11 = (bf16[64,544]{1,0:T(8,128)(2,1)S(1)}, bf16[64,544]{1,0:T(8,128)(2,1)S(1)}, u32[]{:S(2)}, u32[]{:S(2)}) collective-permute-start(bf16[64,544]{1,0:T(8,128)(2,1)S(1)} %shard_map.135.refs_0_), channel_id=1, source_target_pairs={{0,6},{1,7},{2,4},{3,5},{4,2},{5,3},{6,0},{7,1},{8,14},{9,15},{10,... | collective-permute-start | bytes 208904 | tf_op jit(solution)/shard_map/ppermute | solution.py:24
  30.3 6.0 %collective-permute-start.10 = (bf16[64,544]{1,0:T(8,128)(2,1)S(1)}, bf16[64,544]{1,0:T(8,128)(2,1)S(1)}, u32[]{:S(2)}, u32[]{:S(2)}) collective-permute-start(bf16[64,544]{1,0:T(8,128)(2,1)S(1)} %shard_map.135.refs_0_), channel_id=1, source_target_pairs={{0,4},{1,5},{2,6},{3,7},{4,0},{5,1},{6,2},{7,3},{8,12},{9,13},{10,... | collective-permute-start | bytes 208904 | tf_op jit(solution)/shard_map/ppermute | solution.py:24
  32.1 4.4 %collective-permute-start.9 = (bf16[64,544]{1,0:T(8,128)(2,1)S(1)}, bf16[64,544]{1,0:T(8,128)(2,1)S(1)}, u32[]{:S(2)}, u32[]{:S(2)}) collective-permute-start(bf16[64,544]{1,0:T(8,128)(2,1)S(1)} %shard_map.135.refs_0_), channel_id=1, source_target_pairs={{0,2},{1,3},{2,0},{3,1},{4,6},{5,7},{6,4},{7,5},{8,10},{9,11},{10,... | collective-permute-start | bytes 208904 | tf_op jit(solution)/shard_map/ppermute | solution.py:24
  36.6 1.3 %collective-permute-start.12 = (bf16[64,544]{1,0:T(8,128)(2,1)S(1)}, bf16[64,544]{1,0:T(8,128)(2,1)S(1)}, u32[]{:S(2)}, u32[]{:S(2)}) collective-permute-start(bf16[64,544]{1,0:T(8,128)(2,1)S(1)} %shard_map.137.refs_0_), channel_id=1, source_target_pairs={{0,1},{1,0},{2,3},{3,2},{4,5},{5,4},{6,7},{7,6},{8,9},{9,8},{10,11... | collective-permute-start | bytes 208904 | tf_op jit(solution)/shard_map/ppermute | solution.py:24
  41.5 4.4 %collective-permute-start.13 = (bf16[17,1024]{1,0:T(8,128)(2,1)S(1)}, bf16[17,1024]{1,0:T(8,128)(2,1)S(1)}, u32[]{:S(2)}, u32[]{:S(2)}) collective-permute-start(bf16[17,1024]{1,0:T(8,128)(2,1)S(1)} %get-tuple-element.44), channel_id=1, source_target_pairs={{0,8},{8,0},{16,24},{24,16},{1,9},{9,1},{17,25},{25,17},{2,10},{10... | collective-permute-start | bytes 104456 | tf_op jit(solution)/shard_map/ppermute | solution.py:24
  46.6 6.7 %collective-permute-start.14 = (bf16[17,1024]{1,0:T(8,128)(2,1)S(1)}, bf16[17,1024]{1,0:T(8,128)(2,1)S(1)}, u32[]{:S(2)}, u32[]{:S(2)}) collective-permute-start(bf16[17,1024]{1,0:T(8,128)(2,1)S(1)} %get-tuple-element.45), channel_id=1, source_target_pairs={{0,16},{8,24},{1,17},{9,25},{2,18},{10,26},{3,19},{11,27},{4,20},{... | collective-permute-start | bytes 104456 | tf_op jit(solution)/shard_map/ppermute | solution.py:537
  56.3 2.1 %collective-permute-start.16 = (bf16[2,128,1024]{2,1,0:T(8,128)(2,1)S(1)}, bf16[2,128,1024]{2,1,0:T(8,128)(2,1)S(1)}, u32[]{:S(2)}, u32[]{:S(2)}) collective-permute-start(bf16[2,128,1024]{2,1,0:T(8,128)(2,1)S(1)} %shard_map.145), channel_id=1, source_target_pairs={{0,1},{1,0},{2,3},{3,2},{4,5},{5,4},{6,7},{7,6},{8,9},{9,8},{10,11... | collective-permute-start | bytes 1572872 | tf_op jit(solution)/shard_map/ppermute | solution.py:24
  57.1 4.3 %collective-permute-start.15 = (bf16[2,128,1024]{2,1,0:T(8,128)(2,1)S(1)}, bf16[2,128,1024]{2,1,0:T(8,128)(2,1)S(1)}, u32[]{:S(2)}, u32[]{:S(2)}) collective-permute-start(bf16[2,128,1024]{2,1,0:T(8,128)(2,1)S(1)} %shard_map.142), channel_id=1, source_target_pairs={{0,1},{1,0},{2,3},{3,2},{4,5},{5,4},{6,7},{7,6},{8,9},{9,8},{10,11... | collective-permute-start | bytes 1572872 | tf_op jit(solution)/shard_map/ppermute | solution.py:24
  58.6 6.4 %collective-permute-start.18 = (bf16[128,1024]{1,0:T(8,128)(2,1)S(1)}, bf16[128,1024]{1,0:T(8,128)(2,1)S(1)}, u32[]{:S(2)}, u32[]{:S(2)}) collective-permute-start(bf16[128,1024]{1,0:T(8,128)(2,1)S(1)} %get-tuple-element.52), channel_id=1, source_target_pairs={{0,2},{1,5},{2,0},{3,7},{4,6},{5,1},{6,4},{7,3},{8,10},{9,13},{10,... | collective-permute-start | bytes 786440 | tf_op jit(solution)/shard_map/ppermute | solution.py:551
  59.9 8.8 %collective-permute-start.17 = (bf16[128,1024]{1,0:T(8,128)(2,1)S(1)}, bf16[128,1024]{1,0:T(8,128)(2,1)S(1)}, u32[]{:S(2)}, u32[]{:S(2)}) collective-permute-start(bf16[128,1024]{1,0:T(8,128)(2,1)S(1)} %get-tuple-element.50), channel_id=1, source_target_pairs={{0,2},{1,5},{2,0},{3,7},{4,6},{5,1},{6,4},{7,3},{8,10},{9,13},{10,... | collective-permute-start | bytes 786440 | tf_op jit(solution)/shard_map/ppermute | solution.py:552
  65.1 6.4 %collective-permute-start.19 = (bf16[128,1024]{1,0:T(8,128)(2,1)S(1)}, bf16[128,1024]{1,0:T(8,128)(2,1)S(1)}, u32[]{:S(2)}, u32[]{:S(2)}) collective-permute-start(bf16[128,1024]{1,0:T(8,128)(2,1)S(1)} %shard_map.147), channel_id=1, source_target_pairs={{0,4},{1,3},{2,6},{3,1},{4,0},{5,7},{6,2},{7,5},{8,12},{9,11},{10,... | collective-permute-start | bytes 786440 | tf_op jit(solution)/shard_map/ppermute | solution.py:553

commit v2 on v1

--- a/solution.py
+++ b/solution.py
@@ -353,9 +353,9 @@
     )(a, b)
 
 
-def merge_kernel(bit, first, decay_ref, group_ref, got_ref, *refs):
+def merge_kernel(bit, first, last, decay_ref, group_ref, got_ref, *refs):
     ent_ref = None if first else refs[0]
-    new_ref, pack_ref, out_ref = refs[-3:]
+    pack_ref, out_ref = refs[-2:]
     upper = (lax.axis_index("ctx") // bit) % 2 == 1
     decay = decay_ref[...]
     got = got_ref[...].astype(F32)
@@ -370,21 +370,24 @@
     low = jnp.where(upper, gh, mh)
     high = jnp.where(upper, mh, gh)
     high_s = jnp.where(upper, ms, gs)
-    new_ref[:STATE, :] = jnp.exp(-decay * high_s) * low + high
-    new_ref[STATE:, :] = ms + gs
-    pack_ref[...] = new_ref[...].astype(BF16)
-
-
-def merge(bit, decay_t, group, got, ent):
+    total = jnp.exp(-decay * high_s) * low + high
+    pack_ref[:STATE, :] = total.astype(BF16)
+    pack_ref[STATE:, :] = (ms + gs).astype(BF16)
+    if not last:
+        refs[-3][:STATE, :] = total
+        refs[-3][STATE:, :] = ms + gs
+
+
+def merge(bit, decay_t, group, got, ent, last):
     vm = pl.BlockSpec(memory_space=VMEM)
     first = ent is None
     extra = () if first else (ent,)
     return pl.pallas_call(
-        functools.partial(merge_kernel, bit, first),
+        functools.partial(merge_kernel, bit, first, last),
         in_specs=[vm] * (3 + len(extra)),
-        out_specs=[vm] * 3,
-        out_shape=[
-            jax.ShapeDtypeStruct(group.shape, F32),
+        out_specs=[vm] * (2 if last else 3),
+        out_shape=[jax.ShapeDtypeStruct(group.shape, F32)] * (not last)
+        + [
             jax.ShapeDtypeStruct(group.shape, BF16),
             jax.ShapeDtypeStruct(group.shape, F32),
         ],
@@ -531,10 +534,10 @@
     group, ent, bit = end, None, 1
     while bit * 2 < n_ctx:
         got = flip(packet, "ctx", bit)
-        group, packet, ent = merge(bit, decay_t, group, got, ent)
+        *group, packet, ent = merge(bit, decay_t, group, got, ent, bit * 4 >= n_ctx)
+        group = group[0] if group else None
         bit *= 2
-    pairs = [(i, i ^ bit) for i in range(n_ctx) if (i // bit) % 2 == 0]
-    got = lax.ppermute(packet, "ctx", pairs)
+    got = flip(packet, "ctx", bit)
     gated, bound = gating(
         bit, y, cum, bc, end, got, ent, decay_t, conv_x, skip_gain[None, :], gate_acc
     )
@@ -545,7 +548,7 @@
         away_b = out_blocks(gated, out_weight, [11, 1], feat)
         got_b = flip(away_b, "tp", 1)
         near = out_blocks(gated, out_weight, [6, 10], feat)
-        sd, sf = add_pair(near, tie(got, away_b))
+        sd, sf = add_pair(near, got)
         near_b = out_blocks(gated, out_weight, [20, 0], feat)
         ss, so = add_pair(near_b, got_b)
         rd = lax.ppermute(sd, "tp", to_first)

time: 72.5 us -> 70.3 us (0.970)
  starting transfers between devices: 24.1 us -> 22.3 us
    ppermute x1 -> x0, starting transfers between devices: 4.93 us -> none  [on_device(): got = lax.ppermute(packet, 'ctx', pairs)]
    ppermute x12 -> x13, starting transfers between devices: 7.03 us -> 10.1 us  [flip(): return lax.ppermute(value, axis, [(i, i ^ mask) for i in range(peers)])]
    ppermute x12 -> x13, waiting for transfers between devices: 7.78 us -> 9.85 us  [flip(): return lax.ppermute(value, axis, [(i, i ^ mask) for i in range(peers)])]
    ppermute x1 -> x0, waiting for transfers between devices: 1.73 us -> none  [on_device(): got = lax.ppermute(packet, 'ctx', pairs)]
where the time goes in v2:
time: 70.3 us; the launch traced here: 70.2 us
  waiting for transfers between devices  28.6 us (41%)
  starting transfers between devices  22.3 us (32%)
  Pallas kernels  18.3 us (26%)
  between operations  0.95 us (1%)
    ppermute x13, starting transfers between devices, flip(): return lax.ppermute(value, axis, [(i, i ^ mask) for i in range(peers)])  10.1 us
    ppermute x13, waiting for transfers between devices, flip(): return lax.ppermute(value, axis, [(i, i ^ mask) for i in range(peers)])  9.85 us
    pallas_call x3, Pallas kernels, mm(): pl.pallas_call(functools.partial(mm_kernel, roles, len(extra), edge), in_...  4.62 us
    ppermute x1, waiting for transfers between devices, on_device(): vf = lax.ppermute(tie(tokens, inner), 'tp', to_first)  4.46 us
    ppermute x1, starting transfers between devices, on_device(): tail = lax.ppermute(edge_x, 'ctx', shift)  3.65 us
    pallas_call x1, Pallas kernels, scan(): pl.pallas_call(functools.partial(scan_kernel, len(parts) == 2), in_specs=...  3.53 us
    ppermute x1, waiting for transfers between devices, on_device(): rd = lax.ppermute(sd, 'tp', to_first)  3.42 us
    ppermute x1, waiting for transfers between devices, on_device(): rf = lax.ppermute(sf, 'tp', to_first)  3.26 us
  transfers between devices with their start and end apart: 20, of which 16 were waited for; matrix products, arithmetic and copies ran while one was open for 0% of the time, Pallas kernels for 13%

profile of v2, /device:TPU:0, one launch (start us, length us, event | category | flops | bytes accessed | tf_op | source)
XLA Modules:
  0.0 70.2 jit_solution(12841245221188536718)
XLA Ops:
  0.6 3.1 %collective-permute-start = (bf16[128,1024]{1,0:T(8,128)(2,1)}, bf16[128,1024]{1,0:T(8,128)(2,1)S(1)}, u32[]{:S(2)}, u32[]{:S(2)}) collective-permute-start(bf16[128,1024]{1,0:T(8,128)(2,1)} %refs_0_.2), channel_id=1, source_target_pairs={{0,4},{1,3},{2,6},{3,1},{4,0},{5,7},{6,2},{7,5},{8,12},{9,11},{10,... | collective-permute-start | bytes 786440 | tf_op jit(solution)/shard_map/ppermute | solution.py:496
  3.7 2.8 %shard_map.131.refs_6_ = f32[128,1024]{1,0:T(8,128)S(1)} custom-call(bf16[128,1024]{1,0:T(8,128)(2,1)} %refs_0_.2, bf16[8192,1024]{1,0:T(8,128)(2,1)} %refs_2_.1), custom_call_target="tpu_custom_call" | custom-call | flops 268435456 | bytes 2097152 | tf_op jit(solution)/shard_map/pallas_call | solution.py:117
  6.6 1.5 %collective-permute-start.4 = (bf16[128,1024]{1,0:T(8,128)(2,1)S(1)}, bf16[128,1024]{1,0:T(8,128)(2,1)S(1)}, u32[]{:S(2)}, u32[]{:S(2)}) collective-permute-start(bf16[128,1024]{1,0:T(8,128)(2,1)S(1)} %copy-done.2), channel_id=1, source_target_pairs={{0,2},{1,5},{2,0},{3,7},{4,6},{5,1},{6,4},{7,3},{8,10},{9,13},{10,... | collective-permute-start | bytes 786440 | tf_op jit(solution)/shard_map/ppermute | solution.py:498
  8.1 0.2 collective-permute-done.refs_1_.refs_2_
  8.3 0.3 collective-permute-start.3
  8.6 4.5 %collective-permute-done.4.refs_3_.refs_4_ = bf16[128,1024]{1,0:T(8,128)(2,1)S(1)} collective-permute-done((bf16[128,1024]{1,0:T(8,128)(2,1)S(1)}, bf16[128,1024]{1,0:T(8,128)(2,1)S(1)}, u32[]{:S(2)}, u32[]{:S(2)}) %collective-permute-start.4) | collective-permute-done | bytes 262176 | tf_op jit(solution)/shard_map/ppermute | solution.py:498
  13.1 1.4 %collective-permute-start.1 = (bf16[128,1024]{1,0:T(8,128)(2,1)S(1)}, bf16[128,1024]{1,0:T(8,128)(2,1)S(1)}, u32[]{:S(2)}, u32[]{:S(2)}) collective-permute-start(bf16[128,1024]{1,0:T(8,128)(2,1)S(1)} %collective-permute-done.refs_1_.refs_2_), channel_id=1, source_target_pairs={{0,2},{1,5},{2,0},{3,7},{4,6},{5,1},{6,4},{7,3},{8,10},{9,13},{10,... | collective-permute-start | bytes 786440 | tf_op jit(solution)/shard_map/ppermute | solution.py:500
  14.5 0.1 collective-permute-done.5.refs_4_.refs_5_
  14.6 1.5 %shard_map.132.refs_3_ = f32[128,1024]{1,0:T(8,128)S(1)} custom-call(bf16[128,1024]{1,0:T(8,128)(2,1)S(1)} %collective-permute-done.2.refs_0_.refs_1_, bf16[128,1024]{1,0:T(8,128)(2,1)S(1)} %collective-permute-done.refs_1_.refs_2_, bf16[128,1024]{1,0:T(8,128)(2,1)S(1)} %collective-permute-done.3.refs_2_.refs_3_, ...), custom_call_target="tpu_custom_call" | custom-call | flops 1342177280 | bytes 10485760 | tf_op jit(solution)/shard_map/pallas_call | solution.py:162
  16.2 3.2 %collective-permute-done.1.refs_0_.refs_6_ = bf16[128,1024]{1,0:T(8,128)(2,1)S(1)} collective-permute-done((bf16[128,1024]{1,0:T(8,128)(2,1)S(1)}, bf16[128,1024]{1,0:T(8,128)(2,1)S(1)}, u32[]{:S(2)}, u32[]{:S(2)}) %collective-permute-start.1) | collective-permute-done | bytes 262176 | tf_op jit(solution)/shard_map/ppermute | solution.py:500
  19.4 1.5 %collective-permute-done.6.refs_1_.refs_7_ = bf16[128,1024]{1,0:T(8,128)(2,1)S(1)} collective-permute-done((bf16[128,1024]{1,0:T(8,128)(2,1)S(1)}, bf16[128,1024]{1,0:T(8,128)(2,1)S(1)}, u32[]{:S(2)}, u32[]{:S(2)}) %collective-permute-start.6) | collective-permute-done | bytes 262176 | tf_op jit(solution)/shard_map/ppermute | solution.py:24
  21.0 0.7 %shard_map.133 = (bf16[128,1024]{1,0:T(8,128)(2,1)S(1)}, bf16[8,1024]{1,0:T(8,128)(2,1)S(1)}) custom-call(bf16[128,1024]{1,0:T(8,128)(2,1)S(1)} %collective-permute-done.1.refs_0_.refs_6_, bf16[128,1024]{1,0:T(8,128)(2,1)S(1)} %collective-permute-done.6.refs_1_.refs_7_, bf16[8192,1024]{1,0:T(8,128)(2,1)S(1)} %copy-done, f32[128,1024]{1,0:T(8,128)S(1)} %shard_map.132.refs_3_), custom_call_target="tpu_custom_call" | custom-call | flops 536870912 | bytes 4194304 | tf_op jit(solution)/shard_map/pallas_call | solution.py:162
  21.7 3.7 %collective-permute-start.7 = (bf16[8,1024]{1,0:T(8,128)(2,1)S(1)}, bf16[8,1024]{1,0:T(8,128)(2,1)S(1)}, u32[]{:S(2)}, u32[]{:S(2)}) collective-permute-start(bf16[8,1024]{1,0:T(8,128)(2,1)S(1)} %get-tuple-element.31), channel_id=1, source_target_pairs={{0,8},{8,16},{16,24},{1,9},{9,17},{17,25},{2,10},{10,18},{18,26},{... | collective-permute-start | bytes 49160 | tf_op jit(solution)/shard_map/ppermute | solution.py:514
  25.4 1.4 %collective-permute-done.7.tail_ref = bf16[8,1024]{1,0:T(8,128)(2,1)S(1)} collective-permute-done((bf16[8,1024]{1,0:T(8,128)(2,1)S(1)}, bf16[8,1024]{1,0:T(8,128)(2,1)S(1)}, u32[]{:S(2)}, u32[]{:S(2)}) %collective-permute-start.7) | collective-permute-done | bytes 16416 | tf_op jit(solution)/shard_map/ppermute | solution.py:514
  26.8 0.9 %shard_map.134 = (bf16[128,1024]{1,0:T(8,128)(2,1)S(1)}, bf16[64,544]{1,0:T(8,128)(2,1)S(1)}, f32[64,544]{1,0:T(8,128)S(1)}) custom-call(bf16[128,1024]{1,0:T(8,128)(2,1)S(1)} %get-tuple-element.30.x_ref, bf16[8,1024]{1,0:T(8,128)(2,1)S(1)} %collective-permute-done.7.tail_ref, f32[4,1024]{1,0:T(4,128)S(1)} %copy-done.4, f32[1,1024]{1,0:T(1,128)S(1)} %bitcast.17, ...), custom_call_target="tpu_custom_call" | custom-call | flops 142606336 | bytes 1114112 | tf_op jit(solution)/shard_map/pallas_call | solution.py:200
  27.7 0.1 collective-permute-start.8
  27.8 1.3 %collective-permute-done.8.refs_1_ = bf16[64,544]{1,0:T(8,128)(2,1)S(1)} collective-permute-done((bf16[64,544]{1,0:T(8,128)(2,1)S(1)}, bf16[64,544]{1,0:T(8,128)(2,1)S(1)}, u32[]{:S(2)}, u32[]{:S(2)}) %collective-permute-start.8) | collective-permute-done | bytes 69664 | tf_op jit(solution)/shard_map/ppermute | solution.py:24
  29.1 1.2 %collective-permute-start.11 = (bf16[64,544]{1,0:T(8,128)(2,1)S(1)}, bf16[64,544]{1,0:T(8,128)(2,1)S(1)}, u32[]{:S(2)}, u32[]{:S(2)}) collective-permute-start(bf16[64,544]{1,0:T(8,128)(2,1)S(1)} %shard_map.135.refs_0_), channel_id=1, source_target_pairs={{0,6},{1,7},{2,4},{3,5},{4,2},{5,3},{6,0},{7,1},{8,14},{9,15},{10,... | collective-permute-start | bytes 208904 | tf_op jit(solution)/shard_map/ppermute | solution.py:24
  30.3 1.8 %collective-permute-start.10 = (bf16[64,544]{1,0:T(8,128)(2,1)S(1)}, bf16[64,544]{1,0:T(8,128)(2,1)S(1)}, u32[]{:S(2)}, u32[]{:S(2)}) collective-permute-start(bf16[64,544]{1,0:T(8,128)(2,1)S(1)} %shard_map.135.refs_0_), channel_id=1, source_target_pairs={{0,4},{1,5},{2,6},{3,7},{4,0},{5,1},{6,2},{7,3},{8,12},{9,13},{10,... | collective-permute-start | bytes 208904 | tf_op jit(solution)/shard_map/ppermute | solution.py:24
  32.1 0.5 collective-permute-start.9
  32.7 2.4 %shard_map.136.gate_ref = f32[128,1024]{1,0:T(8,128)S(1)} custom-call(bf16[128,1024]{1,0:T(8,128)(2,1)S(1)} %copy-done.2, bf16[128,1024]{1,0:T(8,128)(2,1)S(1)} %collective-permute-done.2.refs_0_.refs_1_, bf16[128,1024]{1,0:T(8,128)(2,1)S(1)} %collective-permute-done.refs_1_.refs_2_, bf16[128,1024]{1,0:T(8,128)(2,1)S(1)} %collective-permute-done.3.refs_2_.refs_3_, ...), custom_call_target="tpu_custom_call" | custom-call | flops 2147483648 | bytes 16777216 | tf_op jit(solution)/shard_map/pallas_call | solution.py:162
  35.0 0.1 collective-permute-done.11.refs_3_
  35.1 1.2 %collective-permute-done.10.refs_2_ = bf16[64,544]{1,0:T(8,128)(2,1)S(1)} collective-permute-done((bf16[64,544]{1,0:T(8,128)(2,1)S(1)}, bf16[64,544]{1,0:T(8,128)(2,1)S(1)}, u32[]{:S(2)}, u32[]{:S(2)}) %collective-permute-start.10) | collective-permute-done | bytes 69664 | tf_op jit(solution)/shard_map/ppermute | solution.py:24
  36.3 0.2 collective-permute-done.9.refs_1_
  36.6 0.1 collective-permute-start.12
  36.7 1.3 %collective-permute-done.12.refs_1_ = bf16[64,544]{1,0:T(8,128)(2,1)S(1)} collective-permute-done((bf16[64,544]{1,0:T(8,128)(2,1)S(1)}, bf16[64,544]{1,0:T(8,128)(2,1)S(1)}, u32[]{:S(2)}, u32[]{:S(2)}) %collective-permute-start.12) | collective-permute-done | bytes 69664 | tf_op jit(solution)/shard_map/ppermute | solution.py:24
  38.0 3.5 %shard_map.138 = (f32[17,1024]{1,0:T(8,128)S(1)}, bf16[17,1024]{1,0:T(8,128)(2,1)S(1)}, f32[1024,128]{1,0:T(8,128)S(1)}, f32[1024,128]{1,0:T(8,128)S(1)}, f32[2048,128]{1,0:T(8,128)S(1)}) custom-call(bf16[64,544]{1,0:T(8,128)(2,1)S(1)} %shard_map.137.refs_0_, bf16[64,544]{1,0:T(8,128)(2,1)S(1)} %collective-permute-done.12.refs_1_, ...), custom_call_target="tpu_custom_call" | custom-call | flops 16777216 | bytes 1048576 | tf_op jit(solution)/shard_map/pallas_call | solution.py:293
  41.5 2.4 %collective-permute-start.13 = (bf16[17,1024]{1,0:T(8,128)(2,1)S(1)}, bf16[17,1024]{1,0:T(8,128)(2,1)S(1)}, u32[]{:S(2)}, u32[]{:S(2)}) collective-permute-start(bf16[17,1024]{1,0:T(8,128)(2,1)S(1)} %get-tuple-element.43), channel_id=1, source_target_pairs={{0,8},{8,0},{16,24},{24,16},{1,9},{9,1},{17,25},{25,17},{2,10},{10... | collective-permute-start | bytes 104456 | tf_op jit(solution)/shard_map/ppermute | solution.py:24
  43.9 2.1 %collective-permute-done.13.got_ref = bf16[17,1024]{1,0:T(8,128)(2,1)S(1)} collective-permute-done((bf16[17,1024]{1,0:T(8,128)(2,1)S(1)}, bf16[17,1024]{1,0:T(8,128)(2,1)S(1)}, u32[]{:S(2)}, u32[]{:S(2)}) %collective-permute-start.13) | collective-permute-done | bytes 34848 | tf_op jit(solution)/shard_map/ppermute | solution.py:24
  46.0 3.1 %collective-permute-start.14 = (bf16[17,1024]{1,0:T(8,128)(2,1)S(1)}, bf16[17,1024]{1,0:T(8,128)(2,1)S(1)}, u32[]{:S(2)}, u32[]{:S(2)}) collective-permute-start(bf16[17,1024]{1,0:T(8,128)(2,1)S(1)} %get-tuple-element.44), channel_id=1, source_target_pairs={{0,16},{8,24},{16,0},{24,8},{1,17},{9,25},{17,1},{25,9},{2,18},{10... | collective-permute-start | bytes 104456 | tf_op jit(solution)/shard_map/ppermute | solution.py:24
  49.1 2.1 %collective-permute-done.14.got_ref = bf16[17,1024]{1,0:T(8,128)(2,1)S(1)} collective-permute-done((bf16[17,1024]{1,0:T(8,128)(2,1)S(1)}, bf16[17,1024]{1,0:T(8,128)(2,1)S(1)}, u32[]{:S(2)}, u32[]{:S(2)}) %collective-permute-start.14) | collective-permute-done | bytes 34848 | tf_op jit(solution)/shard_map/ppermute | solution.py:24
  51.2 2.3 %shard_map.140 = (bf16[128,1024]{1,0:T(8,128)(2,1)S(1)}, f32[16,1024]{1,0:T(8,128)}) custom-call(f32[1024,128]{1,0:T(8,128)S(1)} %get-tuple-element.39.y_ref, f32[1024,128]{1,0:T(8,128)S(1)} %get-tuple-element.40.cum_ref, f32[2048,128]{1,0:T(8,128)S(1)} %get-tuple-element.41.c_ref, f32[17,1024]{1,0:T(8,128)S(1)} %get-tuple-element.42.group_ref.end_ref, ...), custom_call_target="tpu_custom_call" | custom-call | flops 12582912 | bytes 1048576 | tf_op jit(solution)/shard_map/pallas_call | solution.py:440
  53.4 0.7 %shard_map.145 = bf16[2,128,1024]{2,1,0:T(8,128)(2,1)S(1)} custom-call(bf16[128,1024]{1,0:T(8,128)(2,1)S(1)} %get-tuple-element.46.g_ref, bf16[1024,8192]{1,0:T(8,128)(2,1)S(1)} %bitcast.10), custom_call_target="tpu_custom_call" | custom-call | flops 536870912 | bytes 4194304 | tf_op jit(solution)/shard_map/pallas_call | solution.py:469
  54.2 0.1 collective-permute-start.16
  54.3 0.7 %shard_map.142 = bf16[2,128,1024]{2,1,0:T(8,128)(2,1)S(1)} custom-call(bf16[128,1024]{1,0:T(8,128)(2,1)S(1)} %get-tuple-element.46.g_ref, bf16[1024,8192]{1,0:T(8,128)(2,1)S(1)} %bitcast.10), custom_call_target="tpu_custom_call" | custom-call | flops 536870912 | bytes 4194304 | tf_op jit(solution)/shard_map/pallas_call | solution.py:469
  55.0 0.5 collective-permute-start.15
  55.6 0.7 %shard_map.144.a_ref = bf16[2,128,1024]{2,1,0:T(8,128)(2,1)S(1)} custom-call(bf16[128,1024]{1,0:T(8,128)(2,1)S(1)} %get-tuple-element.46.g_ref, bf16[1024,8192]{1,0:T(8,128)(2,1)S(1)} %bitcast.10), custom_call_target="tpu_custom_call" | custom-call | flops 536870912 | bytes 4194304 | tf_op jit(solution)/shard_map/pallas_call | solution.py:469
  56.3 0.1 shard_map.146
  56.4 0.6 collective-permute-start.18
  57.0 0.7 %shard_map.141.a_ref = bf16[2,128,1024]{2,1,0:T(8,128)(2,1)S(1)} custom-call(bf16[128,1024]{1,0:T(8,128)(2,1)S(1)} %get-tuple-element.46.g_ref, bf16[1024,8192]{1,0:T(8,128)(2,1)S(1)} %bitcast.10), custom_call_target="tpu_custom_call" | custom-call | flops 536870912 | bytes 4194304 | tf_op jit(solution)/shard_map/pallas_call | solution.py:469
  57.7 1.6 %collective-permute-start.17 = (bf16[128,1024]{1,0:T(8,128)(2,1)S(1)}, bf16[128,1024]{1,0:T(8,128)(2,1)S(1)}, u32[]{:S(2)}, u32[]{:S(2)}) collective-permute-start(bf16[128,1024]{1,0:T(8,128)(2,1)S(1)} %get-tuple-element.48), channel_id=1, source_target_pairs={{0,2},{1,5},{2,0},{3,7},{4,6},{5,1},{6,4},{7,3},{8,10},{9,13},{10,... | collective-permute-start | bytes 786440 | tf_op jit(solution)/shard_map/ppermute | solution.py:555
  59.3 0.1 shard_map.143
  59.4 3.4 %collective-permute-done.18.refs_1_ = bf16[128,1024]{1,0:T(8,128)(2,1)S(1)} collective-permute-done((bf16[128,1024]{1,0:T(8,128)(2,1)S(1)}, bf16[128,1024]{1,0:T(8,128)(2,1)S(1)}, u32[]{:S(2)}, u32[]{:S(2)}) %collective-permute-start.18) | collective-permute-done | bytes 262176 | tf_op jit(solution)/shard_map/ppermute | solution.py:554
  62.9 0.1 shard_map.147
  62.9 0.4 collective-permute-start.19
  63.3 3.3 %collective-permute-done.17.refs_1_ = bf16[128,1024]{1,0:T(8,128)(2,1)S(1)} collective-permute-done((bf16[128,1024]{1,0:T(8,128)(2,1)S(1)}, bf16[128,1024]{1,0:T(8,128)(2,1)S(1)}, u32[]{:S(2)}, u32[]{:S(2)}) %collective-permute-start.17) | collective-permute-done | bytes 262176 | tf_op jit(solution)/shard_map/ppermute | solution.py:555
  66.6 2.8 %collective-permute-done.19.refs_2_ = bf16[128,1024]{1,0:T(8,128)(2,1)S(1)} collective-permute-done((bf16[128,1024]{1,0:T(8,128)(2,1)S(1)}, bf16[128,1024]{1,0:T(8,128)(2,1)S(1)}, u32[]{:S(2)}, u32[]{:S(2)}) %collective-permute-start.19) | collective-permute-done | bytes 262176 | tf_op jit(solution)/shard_map/ppermute | solution.py:556
  69.4 0.8 %shard_map.148 = bf16[128,1024]{1,0:T(8,128)(2,1)} custom-call(bf16[128,1024]{1,0:T(8,128)(2,1)S(1)} %get-tuple-element.47.refs_0_, bf16[128,1024]{1,0:T(8,128)(2,1)S(1)} %collective-permute-done.17.refs_1_, bf16[128,1024]{1,0:T(8,128)(2,1)S(1)} %collective-permute-done.19.refs_2_), custom_call_target="tpu_custom_call" | custom-call | flops 393216 | bytes 786432 | tf_op jit(solution)/shard_map/pallas_call | solution.py:328
  (48 shorter events, 0.2 us)
Async XLA Ops:
  0.6 5.9 %copy-start.2 = (bf16[128,1024]{1,0:T(8,128)(2,1)S(1)}, bf16[128,1024]{1,0:T(8,128)(2,1)}, u32[]{:S(2)}) copy-start(bf16[128,1024]{1,0:T(8,128)(2,1)} %refs_0_.2) | copy-start | bytes 786436
  0.6 14.0 %copy-start = (bf16[8192,1024]{1,0:T(8,128)(2,1)S(1)}, bf16[8192,1024]{1,0:T(8,128)(2,1)}, u32[]{:S(2)}) copy-start(bf16[8192,1024]{1,0:T(8,128)(2,1)} %refs_2_.1) | copy-start | bytes 50331652
  0.6 7.6 %collective-permute-start = (bf16[128,1024]{1,0:T(8,128)(2,1)}, bf16[128,1024]{1,0:T(8,128)(2,1)S(1)}, u32[]{:S(2)}, u32[]{:S(2)}) collective-permute-start(bf16[128,1024]{1,0:T(8,128)(2,1)} %refs_0_.2), channel_id=1, source_target_pairs={{0,4},{1,3},{2,6},{3,1},{4,0},{5,7},{6,2},{7,5},{8,12},{9,11},{10,... | collective-permute-start | bytes 786440 | tf_op jit(solution)/shard_map/ppermute | solution.py:496
  6.6 20.2 %copy-start.1 = (bf16[1024,544]{0,1:T(8,128)(2,1)S(1)}, bf16[1024,544]{0,1:T(8,128)(2,1)}, u32[]{:S(2)}) copy-start(bf16[1024,544]{0,1:T(8,128)(2,1)} %param.17) | copy-start | bytes 3342340
  6.6 20.2 %copy-start.4 = (f32[4,1024]{1,0:T(4,128)S(1)}, f32[4,1024]{1,0:T(4,128)}, u32[]{:S(2)}) copy-start(f32[4,1024]{1,0:T(4,128)} %w_ref.5) | copy-start | bytes 49156
  6.6 20.2 %copy-start.5 = (f32[1024]{0:T(1024)S(1)}, f32[1024]{0:T(1024)}, u32[]{:S(2)}) copy-start(f32[1024]{0:T(1024)} %param.16) | copy-start | bytes 12292
  6.6 26.1 %slice-start.4 = ((s8[16777216]{0:T(1024)(128)(4,1)}), s8[4194304]{0:T(1024)(128)(4,1)S(1)}, s32[]{:S(2)}) async-start(s8[16777216]{0:T(1024)(128)(4,1)} %bitcast.11), calls=%async_computation.4 | async-start | bytes 8388608
  6.6 26.0 %slice-start.5 = ((s8[16777216]{0:T(1024)(128)(4,1)}), s8[4194304]{0:T(1024)(128)(4,1)S(1)}, s32[]{:S(2)}) async-start(s8[16777216]{0:T(1024)(128)(4,1)} %bitcast.11), calls=%async_computation.5 | async-start | bytes 8388608
  6.6 6.4 %collective-permute-start.4 = (bf16[128,1024]{1,0:T(8,128)(2,1)S(1)}, bf16[128,1024]{1,0:T(8,128)(2,1)S(1)}, u32[]{:S(2)}, u32[]{:S(2)}) collective-permute-start(bf16[128,1024]{1,0:T(8,128)(2,1)S(1)} %copy-done.2), channel_id=1, source_target_pairs={{0,2},{1,5},{2,0},{3,7},{4,6},{5,1},{6,4},{7,3},{8,10},{9,13},{10,... | collective-permute-start | bytes 786440 | tf_op jit(solution)/shard_map/ppermute | solution.py:498
  8.1 6.4 %collective-permute-start.2 = (bf16[128,1024]{1,0:T(8,128)(2,1)S(1)}, bf16[128,1024]{1,0:T(8,128)(2,1)S(1)}, u32[]{:S(2)}, u32[]{:S(2)}) collective-permute-start(bf16[128,1024]{1,0:T(8,128)(2,1)S(1)} %copy-done.2), channel_id=1, source_target_pairs={{0,1},{1,0},{2,3},{3,2},{4,5},{5,4},{6,7},{7,6},{8,9},{9,8},{10,11... | collective-permute-start | bytes 786440 | tf_op jit(solution)/shard_map/ppermute | solution.py:24
  8.3 6.2 %collective-permute-start.3 = (bf16[128,1024]{1,0:T(8,128)(2,1)S(1)}, bf16[128,1024]{1,0:T(8,128)(2,1)S(1)}, u32[]{:S(2)}, u32[]{:S(2)}) collective-permute-start(bf16[128,1024]{1,0:T(8,128)(2,1)S(1)} %collective-permute-done.refs_1_.refs_2_), channel_id=1, source_target_pairs={{0,1},{1,0},{2,3},{3,2},{4,5},{5,4},{6,7},{7,6},{8,9},{9,8},{10,11... | collective-permute-start | bytes 786440 | tf_op jit(solution)/shard_map/ppermute | solution.py:24
  13.1 1.5 %collective-permute-start.5 = (bf16[128,1024]{1,0:T(8,128)(2,1)S(1)}, bf16[128,1024]{1,0:T(8,128)(2,1)S(1)}, u32[]{:S(2)}, u32[]{:S(2)}) collective-permute-start(bf16[128,1024]{1,0:T(8,128)(2,1)S(1)} %collective-permute-done.4.refs_3_.refs_4_), channel_id=1, source_target_pairs={{0,1},{1,0},{2,3},{3,2},{4,5},{5,4},{6,7},{7,6},{8,9},{9,8},{10,11... | collective-permute-start | bytes 786440 | tf_op jit(solution)/shard_map/ppermute | solution.py:24
  13.1 6.4 %collective-permute-start.1 = (bf16[128,1024]{1,0:T(8,128)(2,1)S(1)}, bf16[128,1024]{1,0:T(8,128)(2,1)S(1)}, u32[]{:S(2)}, u32[]{:S(2)}) collective-permute-start(bf16[128,1024]{1,0:T(8,128)(2,1)S(1)} %collective-permute-done.refs_1_.refs_2_), channel_id=1, source_target_pairs={{0,2},{1,5},{2,0},{3,7},{4,6},{5,1},{6,4},{7,3},{8,10},{9,13},{10,... | collective-permute-start | bytes 786440 | tf_op jit(solution)/shard_map/ppermute | solution.py:500
  16.2 16.5 %slice-start.6 = ((s8[16777216]{0:T(1024)(128)(4,1)}), s8[4194304]{0:T(1024)(128)(4,1)S(1)}, s32[]{:S(2)}) async-start(s8[16777216]{0:T(1024)(128)(4,1)} %bitcast.11), calls=%async_computation.6 | async-start | bytes 8388608
  16.2 16.5 %slice-start.7 = ((s8[16777216]{0:T(1024)(128)(4,1)}), s8[4194304]{0:T(1024)(128)(4,1)S(1)}, s32[]{:S(2)}) async-start(s8[16777216]{0:T(1024)(128)(4,1)} %bitcast.11), calls=%async_computation.7 | async-start | bytes 8388608
  16.2 21.8 %copy-start.3 = (f32[1024,16]{0,1:T(8,128)S(1)}, f32[1024,16]{0,1:T(8,128)}, u32[]{:S(2)}) copy-start(f32[1024,16]{0,1:T(8,128)} %param.20) | copy-start | bytes 196612
  16.2 21.8 %copy-start.6 = (bf16[512,1024]{1,0:T(8,128)(2,1)S(1)}, bf16[512,1024]{1,0:T(8,128)(2,1)}, u32[]{:S(2)}) copy-start(bf16[512,1024]{1,0:T(8,128)(2,1)} %refs_3_.1) | copy-start | bytes 3145732
  16.2 21.8 %copy-start.7 = (f32[1024,16]{0,1:T(8,128)S(1)}, f32[1024,16]{0,1:T(8,128)}, u32[]{:S(2)}) copy-start(f32[1024,16]{0,1:T(8,128)} %param.23) | copy-start | bytes 196612
  16.2 21.8 %copy-start.8 = (f32[1024]{0:T(1024)S(1)}, f32[1024]{0:T(1024)}, u32[]{:S(2)}) copy-start(f32[1024]{0:T(1024)} %param.19) | copy-start | bytes 12292
  19.4 1.5 %collective-permute-start.6 = (bf16[128,1024]{1,0:T(8,128)(2,1)S(1)}, bf16[128,1024]{1,0:T(8,128)(2,1)S(1)}, u32[]{:S(2)}, u32[]{:S(2)}) collective-permute-start(bf16[128,1024]{1,0:T(8,128)(2,1)S(1)} %collective-permute-done.1.refs_0_.refs_6_), channel_id=1, source_target_pairs={{0,1},{1,0},{2,3},{3,2},{4,5},{5,4},{6,7},{7,6},{8,9},{9,8},{10,11... | collective-permute-start | bytes 786440 | tf_op jit(solution)/shard_map/ppermute | solution.py:24
  21.0 32.4 %slice-start = ((s8[16777216]{0:T(1024)(128)(4,1)}), s8[4194304]{0:T(1024)(128)(4,1)S(1)}, s32[]{:S(2)}) async-start(s8[16777216]{0:T(1024)(128)(4,1)} %bitcast.9), calls=%async_computation | async-start | bytes 8388608
  21.0 32.4 %slice-start.1 = ((s8[16777216]{0:T(1024)(128)(4,1)}), s8[4194304]{0:T(1024)(128)(4,1)S(1)}, s32[]{:S(2)}) async-start(s8[16777216]{0:T(1024)(128)(4,1)} %bitcast.9), calls=%async_computation.1 | async-start | bytes 8388608
  21.7 29.4 %copy-start.9 = (f32[1024]{0:T(1024)S(1)}, f32[1024]{0:T(1024)}, u32[]{:S(2)}) copy-start(f32[1024]{0:T(1024)} %param.21) | copy-start | bytes 12292
  21.7 5.1 %collective-permute-start.7 = (bf16[8,1024]{1,0:T(8,128)(2,1)S(1)}, bf16[8,1024]{1,0:T(8,128)(2,1)S(1)}, u32[]{:S(2)}, u32[]{:S(2)}) collective-permute-start(bf16[8,1024]{1,0:T(8,128)(2,1)S(1)} %get-tuple-element.31), channel_id=1, source_target_pairs={{0,8},{8,16},{16,24},{1,9},{9,17},{17,25},{2,10},{10,18},{18,26},{... | collective-permute-start | bytes 49160 | tf_op jit(solution)/shard_map/ppermute | solution.py:514
  27.7 1.3 %collective-permute-start.8 = (bf16[64,544]{1,0:T(8,128)(2,1)S(1)}, bf16[64,544]{1,0:T(8,128)(2,1)S(1)}, u32[]{:S(2)}, u32[]{:S(2)}) collective-permute-start(bf16[64,544]{1,0:T(8,128)(2,1)S(1)} %get-tuple-element.33), channel_id=1, source_target_pairs={{0,1},{1,0},{2,3},{3,2},{4,5},{5,4},{6,7},{7,6},{8,9},{9,8},{10,11... | collective-permute-start | bytes 208904 | tf_op jit(solution)/shard_map/ppermute | solution.py:24
  29.1 24.4 %slice-start.2 = ((s8[16777216]{0:T(1024)(128)(4,1)}), s8[4194304]{0:T(1024)(128)(4,1)S(1)}, s32[]{:S(2)}) async-start(s8[16777216]{0:T(1024)(128)(4,1)} %bitcast.9), calls=%async_computation.2 | async-start | bytes 8388608
  29.1 24.3 %slice-start.3 = ((s8[16777216]{0:T(1024)(128)(4,1)}), s8[4194304]{0:T(1024)(128)(4,1)S(1)}, s32[]{:S(2)}) async-start(s8[16777216]{0:T(1024)(128)(4,1)} %bitcast.9), calls=%async_computation.3 | async-start | bytes 8388608
  29.1 6.0 %collective-permute-start.11 = (bf16[64,544]{1,0:T(8,128)(2,1)S(1)}, bf16[64,544]{1,0:T(8,128)(2,1)S(1)}, u32[]{:S(2)}, u32[]{:S(2)}) collective-permute-start(bf16[64,544]{1,0:T(8,128)(2,1)S(1)} %shard_map.135.refs_0_), channel_id=1, source_target_pairs={{0,6},{1,7},{2,4},{3,5},{4,2},{5,3},{6,0},{7,1},{8,14},{9,15},{10,... | collective-permute-start | bytes 208904 | tf_op jit(solution)/shard_map/ppermute | solution.py:24
  30.3 6.0 %collective-permute-start.10 = (bf16[64,544]{1,0:T(8,128)(2,1)S(1)}, bf16[64,544]{1,0:T(8,128)(2,1)S(1)}, u32[]{:S(2)}, u32[]{:S(2)}) collective-permute-start(bf16[64,544]{1,0:T(8,128)(2,1)S(1)} %shard_map.135.refs_0_), channel_id=1, source_target_pairs={{0,4},{1,5},{2,6},{3,7},{4,0},{5,1},{6,2},{7,3},{8,12},{9,13},{10,... | collective-permute-start | bytes 208904 | tf_op jit(solution)/shard_map/ppermute | solution.py:24
  32.1 4.4 %collective-permute-start.9 = (bf16[64,544]{1,0:T(8,128)(2,1)S(1)}, bf16[64,544]{1,0:T(8,128)(2,1)S(1)}, u32[]{:S(2)}, u32[]{:S(2)}) collective-permute-start(bf16[64,544]{1,0:T(8,128)(2,1)S(1)} %shard_map.135.refs_0_), channel_id=1, source_target_pairs={{0,2},{1,3},{2,0},{3,1},{4,6},{5,7},{6,4},{7,5},{8,10},{9,11},{10,... | collective-permute-start | bytes 208904 | tf_op jit(solution)/shard_map/ppermute | solution.py:24
  36.6 1.3 %collective-permute-start.12 = (bf16[64,544]{1,0:T(8,128)(2,1)S(1)}, bf16[64,544]{1,0:T(8,128)(2,1)S(1)}, u32[]{:S(2)}, u32[]{:S(2)}) collective-permute-start(bf16[64,544]{1,0:T(8,128)(2,1)S(1)} %shard_map.137.refs_0_), channel_id=1, source_target_pairs={{0,1},{1,0},{2,3},{3,2},{4,5},{5,4},{6,7},{7,6},{8,9},{9,8},{10,11... | collective-permute-start | bytes 208904 | tf_op jit(solution)/shard_map/ppermute | solution.py:24
  41.5 4.4 %collective-permute-start.13 = (bf16[17,1024]{1,0:T(8,128)(2,1)S(1)}, bf16[17,1024]{1,0:T(8,128)(2,1)S(1)}, u32[]{:S(2)}, u32[]{:S(2)}) collective-permute-start(bf16[17,1024]{1,0:T(8,128)(2,1)S(1)} %get-tuple-element.43), channel_id=1, source_target_pairs={{0,8},{8,0},{16,24},{24,16},{1,9},{9,1},{17,25},{25,17},{2,10},{10... | collective-permute-start | bytes 104456 | tf_op jit(solution)/shard_map/ppermute | solution.py:24
  46.0 5.2 %collective-permute-start.14 = (bf16[17,1024]{1,0:T(8,128)(2,1)S(1)}, bf16[17,1024]{1,0:T(8,128)(2,1)S(1)}, u32[]{:S(2)}, u32[]{:S(2)}) collective-permute-start(bf16[17,1024]{1,0:T(8,128)(2,1)S(1)} %get-tuple-element.44), channel_id=1, source_target_pairs={{0,16},{8,24},{16,0},{24,8},{1,17},{9,25},{17,1},{25,9},{2,18},{10... | collective-permute-start | bytes 104456 | tf_op jit(solution)/shard_map/ppermute | solution.py:24
  54.2 2.1 %collective-permute-start.16 = (bf16[2,128,1024]{2,1,0:T(8,128)(2,1)S(1)}, bf16[2,128,1024]{2,1,0:T(8,128)(2,1)S(1)}, u32[]{:S(2)}, u32[]{:S(2)}) collective-permute-start(bf16[2,128,1024]{2,1,0:T(8,128)(2,1)S(1)} %shard_map.145), channel_id=1, source_target_pairs={{0,1},{1,0},{2,3},{3,2},{4,5},{5,4},{6,7},{7,6},{8,9},{9,8},{10,11... | collective-permute-start | bytes 1572872 | tf_op jit(solution)/shard_map/ppermute | solution.py:24
  55.0 4.3 %collective-permute-start.15 = (bf16[2,128,1024]{2,1,0:T(8,128)(2,1)S(1)}, bf16[2,128,1024]{2,1,0:T(8,128)(2,1)S(1)}, u32[]{:S(2)}, u32[]{:S(2)}) collective-permute-start(bf16[2,128,1024]{2,1,0:T(8,128)(2,1)S(1)} %shard_map.142), channel_id=1, source_target_pairs={{0,1},{1,0},{2,3},{3,2},{4,5},{5,4},{6,7},{7,6},{8,9},{9,8},{10,11... | collective-permute-start | bytes 1572872 | tf_op jit(solution)/shard_map/ppermute | solution.py:24
  56.4 6.4 %collective-permute-start.18 = (bf16[128,1024]{1,0:T(8,128)(2,1)S(1)}, bf16[128,1024]{1,0:T(8,128)(2,1)S(1)}, u32[]{:S(2)}, u32[]{:S(2)}) collective-permute-start(bf16[128,1024]{1,0:T(8,128)(2,1)S(1)} %get-tuple-element.50), channel_id=1, source_target_pairs={{0,2},{1,5},{2,0},{3,7},{4,6},{5,1},{6,4},{7,3},{8,10},{9,13},{10,... | collective-permute-start | bytes 786440 | tf_op jit(solution)/shard_map/ppermute | solution.py:554
  57.7 8.8 %collective-permute-start.17 = (bf16[128,1024]{1,0:T(8,128)(2,1)S(1)}, bf16[128,1024]{1,0:T(8,128)(2,1)S(1)}, u32[]{:S(2)}, u32[]{:S(2)}) collective-permute-start(bf16[128,1024]{1,0:T(8,128)(2,1)S(1)} %get-tuple-element.48), channel_id=1, source_target_pairs={{0,2},{1,5},{2,0},{3,7},{4,6},{5,1},{6,4},{7,3},{8,10},{9,13},{10,... | collective-permute-start | bytes 786440 | tf_op jit(solution)/shard_map/ppermute | solution.py:555
  62.9 6.4 %collective-permute-start.19 = (bf16[128,1024]{1,0:T(8,128)(2,1)S(1)}, bf16[128,1024]{1,0:T(8,128)(2,1)S(1)}, u32[]{:S(2)}, u32[]{:S(2)}) collective-permute-start(bf16[128,1024]{1,0:T(8,128)(2,1)S(1)} %shard_map.147), channel_id=1, source_target_pairs={{0,4},{1,3},{2,6},{3,1},{4,0},{5,7},{6,2},{7,5},{8,12},{9,11},{10,... | collective-permute-start | bytes 786440 | tf_op jit(solution)/shard_map/ppermute | solution.py:556

commit v3 on v2

--- a/solution.py
+++ b/solution.py
@@ -169,47 +169,85 @@
     )(*blocks, weight, *extra)
 
 
-def conv_kernel(split, x_ref, tail_ref, w_ref, b_ref, pw_ref, conv_ref, send_ref, keep_ref, pad, acc):
+def convolve(pad, w_ref, b_ref, edge, rows):
+    taps = w_ref.shape[0]
+    total = jnp.broadcast_to(b_ref[...], (rows, b_ref.shape[1]))
+    for k in range(taps):
+        at = edge - taps + 1 + k
+        total = total + w_ref[k : k + 1, :] * pad[at : at + rows, :]
+    return (total * jax.nn.sigmoid(total)).astype(BF16)
+
+
+def project(conv, pw_ref):
+    return lax.dot_general(conv, pw_ref[...], (((1,), (1,)), ((), ())), preferred_element_type=F32)
+
+
+def conv_kernel(x_ref, w_ref, b_ref, pw_ref, conv_ref, proj_ref, pad):
     rows, ch = x_ref.shape
-    taps = w_ref.shape[0]
-    edge = tail_ref.shape[0]
-    pad[0:edge, :] = tail_ref[...].astype(F32)
-    pad[edge : edge + rows, :] = x_ref[...].astype(F32)
-    total = jnp.broadcast_to(b_ref[...], (rows, ch))
-    for k in range(taps):
-        total = total + w_ref[k : k + 1, :] * pad[edge - taps + 1 + k : edge - taps + 1 + k + rows, :]
-    conv = (total * jax.nn.sigmoid(total)).astype(BF16)
+    pad[0:EDGE, :] = jnp.zeros((EDGE, ch), F32)
+    pad[EDGE : EDGE + rows, :] = x_ref[...].astype(F32)
+    conv = convolve(pad, w_ref, b_ref, EDGE, rows)
     conv_ref[...] = conv
-    proj = lax.dot_general(conv, pw_ref[...], (((1,), (1,)), ((), ())), preferred_element_type=F32)
+    proj_ref[...] = project(conv, pw_ref)
+
+
+def head_kernel(split, x_ref, tail_ref, w_ref, b_ref, pw_ref, conv0_ref, proj0_ref, conv_ref, send_ref, keep_ref, pad, acc):
+    rows = x_ref.shape[0]
+    head = pad.shape[0] - EDGE
+    pad[0:EDGE, :] = tail_ref[...].astype(F32)
+    pad[EDGE:, :] = x_ref[0:head, :].astype(F32)
+    conv = convolve(pad, w_ref, b_ref, EDGE, head)
+    conv_ref[...] = conv0_ref[...]
+    conv_ref[0:head, :] = conv
+    acc[...] = proj0_ref[...]
+    acc[0:head, :] = project(conv, pw_ref)
     if split:
         half = rows // 2
         core = lax.axis_index("tp") % 2
-        acc[...] = proj
         send_ref[...] = acc[pl.ds(pl.multiple_of((1 - core) * half, half), half), :].astype(BF16)
         keep_ref[...] = acc[pl.ds(pl.multiple_of(core * half, half), half), :]
     else:
-        keep_ref[...] = proj.astype(keep_ref.dtype)
+        keep_ref[...] = acc[...].astype(keep_ref.dtype)
         send_ref[...] = jnp.zeros(send_ref.shape, send_ref.dtype)
 
 
-def conv_proj(x, tail, conv_w, conv_b, proj_wt, split):
+def conv_proj(x, conv_w, conv_b, proj_wt):
     rows, ch = x.shape
     wide = proj_wt.shape[0]
-    half = rows // 2 if split else rows
-    shalf = half if split else 8
-    return pl.pallas_call(
-        functools.partial(conv_kernel, split),
-        in_specs=[pl.BlockSpec(memory_space=VMEM)] * 5,
-        out_specs=[pl.BlockSpec(memory_space=VMEM)] * 3,
+    vm = pl.BlockSpec(memory_space=VMEM)
+    return pl.pallas_call(
+        conv_kernel,
+        in_specs=[vm] * 4,
+        out_specs=[vm] * 2,
         out_shape=[
             jax.ShapeDtypeStruct((rows, ch), BF16),
-            jax.ShapeDtypeStruct((shalf, wide), BF16),
+            jax.ShapeDtypeStruct((rows, wide), F32),
+        ],
+        scratch_shapes=[VMEM((EDGE + rows, ch), F32)],
+        compiler_params=params(6),
+        cost_estimate=cost(2 * rows * ch * wide, 2 * ch * wide),
+    )(x, conv_w, conv_b, proj_wt)
+
+
+def conv_head(x, tail, conv_w, conv_b, proj_wt, conv0, proj0, split):
+    rows, ch = x.shape
+    wide = proj_wt.shape[0]
+    head = min(2 * EDGE, rows)
+    half = rows // 2 if split else rows
+    vm = pl.BlockSpec(memory_space=VMEM)
+    return pl.pallas_call(
+        functools.partial(head_kernel, split),
+        in_specs=[vm] * 7,
+        out_specs=[vm] * 3,
+        out_shape=[
+            jax.ShapeDtypeStruct((rows, ch), BF16),
+            jax.ShapeDtypeStruct((half if split else EDGE, wide), BF16),
             jax.ShapeDtypeStruct((half, wide), F32 if split else BF16),
         ],
-        scratch_shapes=[VMEM((tail.shape[0] + rows, ch), F32), VMEM((rows, wide), F32)],
-        compiler_params=params(6),
-        cost_estimate=cost(2 * rows * ch * wide, 2 * ch * wide),
-    )(x, tail, conv_w, conv_b, proj_wt)
+        scratch_shapes=[VMEM((EDGE + head, ch), F32), VMEM((rows, wide), F32)],
+        compiler_params=params(4),
+        cost_estimate=cost(2 * head * ch * wide, 2 * ch * wide),
+    )(x, tail, conv_w, conv_b, proj_wt, conv0, proj0)
 
 
 def spread(ref, value, groups):
@@ -220,6 +258,14 @@
 
 def collect(ref, count, groups):
     return jnp.concatenate([ref[pl.ds(j, count, stride=groups), :] for j in range(groups)], axis=1)
+
+
+def across(ref, bc_ref, first):
+    rows = bc_ref.shape[0]
+    for n in range(STATE):
+        ref[pl.ds(n, rows, stride=STATE), :] = jnp.broadcast_to(
+            bc_ref[:, first + n : first + n + 1], (rows, LANES)
+        )
 
 
 def line(ref, at, groups):
@@ -232,8 +278,8 @@
     n_p = 2 if split else 1
     parts = refs[:n_p]
     (conv_ref, sw_ref, sb_ref, decay_ref, carried_ref,
-     end_ref, pack_ref, y_ref, cum_ref, c_ref,
-     proj_s, step_s, drive_s, nd_s, h_s, b_ref) = refs[n_p:]
+     end_ref, pack_ref, step_s, drive_s, b_ref, bc_ref,
+     proj_s, nd_s, h_s) = refs[n_p:]
     rows, ch = conv_ref.shape
     groups = ch // LANES
     if split:
@@ -243,11 +289,8 @@
         proj_s[pl.ds(pl.multiple_of((1 - core) * half, half), half), :] = parts[1][...].astype(F32)
     else:
         proj_s[...] = parts[0][...].astype(F32)
-    for n in range(STATE):
-        for ref, at in ((b_ref, DT_RANK + n), (c_ref, DT_RANK + STATE + n)):
-            ref[pl.ds(n, rows, stride=STATE), :] = jnp.broadcast_to(
-                proj_s[:, at : at + 1], (rows, LANES)
-            )
+    bc_ref[...] = proj_s[:, DT_RANK:]
+    across(b_ref, bc_ref, 0)
     low = proj_s[:, :DT_RANK].astype(BF16)
     pre = jnp.dot(low, sw_ref[...], preferred_element_type=F32) + sb_ref[...]
     step = jnp.maximum(pre, 0.0) + jnp.log1p(jnp.exp(-jnp.abs(pre)))
@@ -264,18 +307,11 @@
         at = pl.ds(pl.multiple_of(t * groups, groups), groups)
         dt = step_s[at, :]
         u = drive_s[at, :]
-        total = total + dt
-        cum_ref[at, :] = total
-        y = None
-        new = []
-        for n in range(STATE):
-            a = jnp.exp2(dt * nd[n])
-            v = a * h[n] + u * line(b_ref, t * STATE + n, groups)
-            new.append(v)
-            term = v * line(c_ref, t * STATE + n, groups)
-            y = term if y is None else y + term
-        y_ref[at, :] = y
-        return tuple(new), total
+        new = tuple(
+            jnp.exp2(dt * nd[n]) * h[n] + u * line(b_ref, t * STATE + n, groups)
+            for n in range(STATE)
+        )
+        return new, total + dt
 
     h, total = lax.fori_loop(0, rows, body, (h0, jnp.zeros((groups, LANES), F32)), unroll=8)
     for n in range(STATE):
@@ -293,25 +329,98 @@
     return pl.pallas_call(
         functools.partial(scan_kernel, len(parts) == 2),
         in_specs=[vm] * (5 + len(parts)),
-        out_specs=[vm] * 5,
+        out_specs=[vm] * 6,
         out_shape=[
             jax.ShapeDtypeStruct((STATE + 1, ch), F32),
             jax.ShapeDtypeStruct((STATE + 1, ch), BF16),
             jax.ShapeDtypeStruct((rows * groups, LANES), F32),
             jax.ShapeDtypeStruct((rows * groups, LANES), F32),
             jax.ShapeDtypeStruct((rows * STATE, LANES), F32),
+            jax.ShapeDtypeStruct((rows, 2 * STATE), F32),
         ],
         scratch_shapes=[
             VMEM((rows, parts[0].shape[1]), F32),
-            VMEM((rows * groups, LANES), F32),
-            VMEM((rows * groups, LANES), F32),
             VMEM((STATE * groups, LANES), F32),
             VMEM((STATE * groups, LANES), F32),
-            VMEM((rows * STATE, LANES), F32),
         ],
         compiler_params=params(8),
         cost_estimate=cost(rows * ch * STATE * 8, rows * ch * 8, rows * ch * STATE),
     )(*parts, conv_x, step_w, step_b, decay_t, carried_t)
+
+
+def local_kernel(step_ref, drive_ref, b_ref, bc_ref, decay_ref, carried_ref, y_ref, cum_ref, c_ref, nd_s, h_s):
+    across(c_ref, bc_ref, STATE)
+    groups = decay_ref.shape[1] // LANES
+    rows = step_ref.shape[0] // groups
+    spread(nd_s, decay_ref[...] * -LOG2E, groups)
+    lead = jnp.where(lax.axis_index("ctx") == 0, 1.0, 0.0)
+    spread(h_s, carried_ref[...] * lead, groups)
+    nd = [nd_s[n * groups : (n + 1) * groups, :] for n in range(STATE)]
+    h0 = tuple(h_s[n * groups : (n + 1) * groups, :] for n in range(STATE))
+
+    def body(t, carry):
+        h, total = carry
+        at = pl.ds(pl.multiple_of(t * groups, groups), groups)
+        dt = step_ref[at, :]
+        u = drive_ref[at, :]
+        total = total + dt
+        cum_ref[at, :] = total
+        y = None
+        new = []
+        for n in range(STATE):
+            v = jnp.exp2(dt * nd[n]) * h[n] + u * line(b_ref, t * STATE + n, groups)
+            new.append(v)
+            term = v * line(c_ref, t * STATE + n, groups)
+            y = term if y is None else y + term
+        y_ref[at, :] = y
+        return tuple(new), total
+
+    lax.fori_loop(0, rows, body, (h0, jnp.zeros((groups, LANES), F32)), unroll=8)
+
+
+def local_readout(step, drive, b, bc, decay_t, carried_t):
+    groups = decay_t.shape[1] // LANES
+    vm = pl.BlockSpec(memory_space=VMEM)
+    return pl.pallas_call(
+        local_kernel,
+        in_specs=[vm] * 6,
+        out_specs=[vm] * 3,
+        out_shape=[jax.ShapeDtypeStruct(step.shape, F32)] * 2
+        + [jax.ShapeDtypeStruct(b.shape, F32)],
+        scratch_shapes=[VMEM((STATE * groups, LANES), F32)] * 2,
+        compiler_params=params(4),
+        cost_estimate=cost(step.size * STATE * 8, step.size * 16, step.size * STATE),
+    )(step, drive, b, bc, decay_t, carried_t)
+
+
+def weight_kernel(cum_ref, c_ref, decay_ref, q_ref, nd_s):
+    groups = decay_ref.shape[1] // LANES
+    rows = cum_ref.shape[0] // groups
+    spread(nd_s, decay_ref[...] * -LOG2E, groups)
+    nd = [nd_s[n * groups : (n + 1) * groups, :] for n in range(STATE)]
+
+    def body(t, carry):
+        total = cum_ref[pl.ds(pl.multiple_of(t * groups, groups), groups), :]
+        for n in range(STATE):
+            at = pl.ds(pl.multiple_of((t * STATE + n) * groups, groups), groups)
+            q_ref[at, :] = jnp.exp2(total * nd[n]) * line(c_ref, t * STATE + n, groups)
+        return carry
+
+    lax.fori_loop(0, rows, body, 0, unroll=4)
+
+
+def weights(cum, c, decay_t):
+    groups = decay_t.shape[1] // LANES
+    vm = pl.BlockSpec(memory_space=VMEM)
+    return pl.pallas_call(
+        weight_kernel,
+        in_specs=[vm] * 3,
+        out_specs=vm,
+        out_shape=jax.ShapeDtypeStruct((cum.shape[0] * STATE, LANES), F32),
+        scratch_shapes=[VMEM((STATE * groups, LANES), F32)],
+        compiler_params=params(2),
+        cost_estimate=cost(cum.size * STATE * 3, cum.size * 4, cum.size * STATE),
+    )(cum, c, decay_t)
 
 
 def add_kernel(*refs):
@@ -396,9 +505,9 @@
     )(decay_t, group, got, *extra)
 
 
-def gate_kernel(bit, first, y_ref, cum_ref, c_ref, end_ref, got_ref, decay_ref, conv_ref, skip_ref, gate_ref, *refs):
+def gate_kernel(bit, first, y_ref, q_ref, end_ref, got_ref, decay_ref, conv_ref, skip_ref, gate_ref, *refs):
     ent_ref = None if first else refs[0]
-    out_ref, bound_ref, nd_s, e_s, y_s = refs[-5:]
+    out_ref, bound_ref, e_s, y_s = refs[-4:]
     rows, ch = conv_ref.shape
     groups = ch // LANES
     decay = decay_ref[...]
@@ -410,17 +519,14 @@
         kept = ent_ref[:STATE, :]
         entering = jnp.where(upper, jnp.exp(-decay * ent_ref[STATE:, :]) * got + kept, kept)
     bound_ref[...] = jnp.exp(-decay * end_ref[STATE:, :]) * entering + end_ref[:STATE, :]
-    spread(nd_s, decay * -LOG2E, groups)
     spread(e_s, entering, groups)
-    nd = [nd_s[n * groups : (n + 1) * groups, :] for n in range(STATE)]
     ent = [e_s[n * groups : (n + 1) * groups, :] for n in range(STATE)]
 
     def body(t, carry):
         at = pl.ds(pl.multiple_of(t * groups, groups), groups)
-        total = cum_ref[at, :]
         y = y_ref[at, :]
         for n in range(STATE):
-            y = y + jnp.exp2(total * nd[n]) * ent[n] * line(c_ref, t * STATE + n, groups)
+            y = y + q_ref[pl.ds(pl.multiple_of((t * STATE + n) * groups, groups), groups), :] * ent[n]
         y_s[at, :] = y
         return carry
 
@@ -431,7 +537,7 @@
     out_ref[...] = out.astype(BF16)
 
 
-def gating(bit, y, cum, bc, end, got, ent, decay_t, conv_x, skip, gate):
+def gating(bit, y, q, end, got, ent, decay_t, conv_x, skip, gate):
     rows, ch = conv_x.shape
     groups = ch // LANES
     vm = pl.BlockSpec(memory_space=VMEM)
@@ -439,7 +545,7 @@
     extra = () if first else (ent,)
     return pl.pallas_call(
         functools.partial(gate_kernel, bit, first),
-        in_specs=[vm] * (9 + len(extra)),
+        in_specs=[vm] * (8 + len(extra)),
         out_specs=[vm, vm],
         out_shape=[
             jax.ShapeDtypeStruct((rows, ch), BF16),
@@ -447,12 +553,11 @@
         ],
         scratch_shapes=[
             VMEM((STATE * groups, LANES), F32),
-            VMEM((STATE * groups, LANES), F32),
             VMEM((rows * groups, LANES), F32),
         ],
         compiler_params=params(8),
         cost_estimate=cost(rows * ch * STATE * 6, rows * ch * 8, rows * ch * STATE),
-    )(y, cum, bc, end, got, decay_t, conv_x, skip, gate, *extra)
+    )(y, q, end, got, decay_t, conv_x, skip, gate, *extra)
 
 
 def out_stack_kernel(masks, g_ref, w_ref, out):
@@ -504,7 +609,9 @@
         inner, = mm([p1, vs, qs, vf, qf], [1, 20, 11, 10, 21], inner_w, inner)
         vd = tie(vd, inner)
         qd = flip(vd, "tp", 1)
-        inner_x, edge_x = mm([vd, qd], [6, 7], inner_w, inner, EDGE)
+        inner, = mm([vd], [6], inner_w, inner)
+        qd = tie(qd, inner)
+        inner_x, edge_x = mm([qd], [7], inner_w, inner, EDGE)
     else:
         piece = lax.all_gather(tokens, "tp", axis=1, tiled=True)
         inner_x = jnp.dot(piece, inner_weight, preferred_element_type=F32).astype(BF16)
@@ -512,8 +619,10 @@
         edge_x = inner_x[rows - EDGE :]
 
     tail = lax.ppermute(edge_x, "ctx", shift)
-    conv_x, send, keep = conv_proj(
-        inner_x, tail, conv_weight, conv_bias[None, :], proj_wt, square
+    conv_b = conv_bias[None, :]
+    conv0, proj0 = conv_proj(inner_x, conv_weight, conv_b, proj_wt)
+    conv_x, send, keep = conv_head(
+        inner_x, tie(tail, proj0), conv_weight, conv_b, proj_wt, conv0, proj0, square
     )
     if square:
         part = add(keep, flip(send, "tp", 1))
@@ -527,19 +636,24 @@
         parts = (mine, flip(mine, "tp", 1))
     else:
         parts = (lax.psum(keep, "tp"),)
-    end, packet, y, cum, bc = scan(
+    end, packet, step, drive, b_rows, bc = scan(
         parts, conv_x, step_weight, step_bias[None, :], decay_t, carried_t
     )
 
+    y, cum, c_rows = local_readout(step, drive, b_rows, bc, decay_t, carried_t)
     group, ent, bit = end, None, 1
     while bit * 2 < n_ctx:
         got = flip(packet, "ctx", bit)
+        if bit == 1:
+            got = tie(got, y)
         *group, packet, ent = merge(bit, decay_t, group, got, ent, bit * 4 >= n_ctx)
         group = group[0] if group else None
         bit *= 2
     got = flip(packet, "ctx", bit)
+    q = weights(cum, c_rows, tie(decay_t, packet))
+    got = tie(got, q)
     gated, bound = gating(
-        bit, y, cum, bc, end, got, ent, decay_t, conv_x, skip_gain[None, :], gate_acc
+        bit, y, q, end, got, ent, decay_t, conv_x, skip_gain[None, :], gate_acc
     )
     if square:
         out_weight = pltpu.with_memory_space_constraint(out_weight, VMEM)

time: 70.3 us -> 68.1 us (0.969)
  waiting for transfers between devices: 28.6 us -> 23.9 us
  Pallas kernels: 18.3 us -> 20.9 us
    pallas_call x1 -> x4, Pallas kernels: 0.88 us -> 5.29 us  [the longest x1 2.64 us: local_readout(): pl.pallas_call(local_kernel, in_specs=[vm] * 6, out_specs=[vm] * 3, out_s...]
    ppermute x13, waiting for transfers between devices: 9.85 us -> 6.16 us  [flip(): return lax.ppermute(value, axis, [(i, i ^ mask) for i in range(peers)])]
    pallas_call x1, Pallas kernels: 3.53 us -> 2.48 us  [scan(): pl.pallas_call(functools.partial(scan_kernel, len(parts) == 2), in_specs=...]
    ppermute x1, waiting for transfers between devices: 1.43 us -> 0.38 us  [on_device(): tail = lax.ppermute(edge_x, 'ctx', shift)]
    pallas_call x1, Pallas kernels: 2.25 us -> 1.37 us  [gating(): pl.pallas_call(functools.partial(gate_kernel, bit, first), in_specs=[vm]...]
    pallas_call x3 -> x4, Pallas kernels: 4.62 us -> 4.8 us  [mm(): pl.pallas_call(functools.partial(mm_kernel, roles, len(extra), edge), in_...]
  transfers between devices with their start and end apart: 20 -> 20, of which waited for: 16 -> 14; matrix products, arithmetic and copies ran while one was open for 0% -> 0% of each run, Pallas kernels for 13% -> 21%
where the time goes in v3:
time: 68.1 us; the launch traced here: 67.9 us
  waiting for transfers between devices  23.9 us (35%)
  starting transfers between devices  21.9 us (32%)
  Pallas kernels  20.9 us (31%)
  between operations  1.01 us (1%)
    ppermute x13, starting transfers between devices, flip(): return lax.ppermute(value, axis, [(i, i ^ mask) for i in range(peers)])  9.6 us
    ppermute x13, waiting for transfers between devices, flip(): return lax.ppermute(value, axis, [(i, i ^ mask) for i in range(peers)])  6.16 us
    pallas_call x4, Pallas kernels, mm(): pl.pallas_call(functools.partial(mm_kernel, roles, len(extra), edge), in_...  4.8 us
    ppermute x1, waiting for transfers between devices, on_device(): vf = lax.ppermute(tie(tokens, inner), 'tp', to_first)  4.45 us
    ppermute x1, starting transfers between devices, on_device(): tail = lax.ppermute(edge_x, 'ctx', shift)  3.83 us
    ppermute x1, waiting for transfers between devices, on_device(): rd = lax.ppermute(sd, 'tp', to_first)  3.42 us
    ppermute x1, waiting for transfers between devices, on_device(): rf = lax.ppermute(sf, 'tp', to_first)  3.26 us
    ppermute x1, waiting for transfers between devices, on_device(): vd = lax.ppermute(vs, 'tp', to_first)  3.24 us
  transfers between devices with their start and end apart: 20, of which 14 were waited for; matrix products, arithmetic and copies ran while one was open for 0% of the time, Pallas kernels for 21%

profile of v3, /device:TPU:0, one launch (start us, length us, event | category | flops | bytes accessed | tf_op | source)
XLA Modules:
  0.0 67.9 jit_solution(9908762726963607695)
XLA Ops:
  0.6 3.1 %collective-permute-start = (bf16[128,1024]{1,0:T(8,128)(2,1)}, bf16[128,1024]{1,0:T(8,128)(2,1)S(1)}, u32[]{:S(2)}, u32[]{:S(2)}) collective-permute-start(bf16[128,1024]{1,0:T(8,128)(2,1)} %refs_0_.2), channel_id=1, source_target_pairs={{0,4},{1,3},{2,6},{3,1},{4,0},{5,7},{6,2},{7,5},{8,12},{9,11},{10,... | collective-permute-start | bytes 786440 | tf_op jit(solution)/shard_map/ppermute | solution.py:601
  3.7 2.8 %shard_map.131.refs_6_ = f32[128,1024]{1,0:T(8,128)S(1)} custom-call(bf16[128,1024]{1,0:T(8,128)(2,1)} %refs_0_.2, bf16[8192,1024]{1,0:T(8,128)(2,1)} %refs_1_.5), custom_call_target="tpu_custom_call" | custom-call | flops 268435456 | bytes 2097152 | tf_op jit(solution)/shard_map/pallas_call | solution.py:117
  6.6 1.5 %collective-permute-start.4 = (bf16[128,1024]{1,0:T(8,128)(2,1)S(1)}, bf16[128,1024]{1,0:T(8,128)(2,1)S(1)}, u32[]{:S(2)}, u32[]{:S(2)}) collective-permute-start(bf16[128,1024]{1,0:T(8,128)(2,1)S(1)} %copy-done.2), channel_id=1, source_target_pairs={{0,2},{1,5},{2,0},{3,7},{4,6},{5,1},{6,4},{7,3},{8,10},{9,13},{10,... | collective-permute-start | bytes 786440 | tf_op jit(solution)/shard_map/ppermute | solution.py:603
  8.0 0.2 collective-permute-done.refs_1_.refs_2_
  8.3 0.3 collective-permute-start.3
  8.6 4.5 %collective-permute-done.4.refs_3_.refs_4_ = bf16[128,1024]{1,0:T(8,128)(2,1)S(1)} collective-permute-done((bf16[128,1024]{1,0:T(8,128)(2,1)S(1)}, bf16[128,1024]{1,0:T(8,128)(2,1)S(1)}, u32[]{:S(2)}, u32[]{:S(2)}) %collective-permute-start.4) | collective-permute-done | bytes 262176 | tf_op jit(solution)/shard_map/ppermute | solution.py:603
  13.0 1.4 %collective-permute-start.1 = (bf16[128,1024]{1,0:T(8,128)(2,1)S(1)}, bf16[128,1024]{1,0:T(8,128)(2,1)S(1)}, u32[]{:S(2)}, u32[]{:S(2)}) collective-permute-start(bf16[128,1024]{1,0:T(8,128)(2,1)S(1)} %collective-permute-done.refs_1_.refs_2_), channel_id=1, source_target_pairs={{0,2},{1,5},{2,0},{3,7},{4,6},{5,1},{6,4},{7,3},{8,10},{9,13},{10,... | collective-permute-start | bytes 786440 | tf_op jit(solution)/shard_map/ppermute | solution.py:605
  14.4 0.1 collective-permute-done.5.refs_4_.refs_5_
  14.5 1.5 %shard_map.132.refs_2_ = f32[128,1024]{1,0:T(8,128)S(1)} custom-call(bf16[128,1024]{1,0:T(8,128)(2,1)S(1)} %collective-permute-done.2.refs_0_.refs_1_, bf16[128,1024]{1,0:T(8,128)(2,1)S(1)} %collective-permute-done.refs_1_.refs_2_, bf16[128,1024]{1,0:T(8,128)(2,1)S(1)} %collective-permute-done.3.refs_2_.refs_3_, ...), custom_call_target="tpu_custom_call" | custom-call | flops 1342177280 | bytes 10485760 | tf_op jit(solution)/shard_map/pallas_call | solution.py:162
  16.1 3.2 %collective-permute-done.1.refs_0_.refs_6_ = bf16[128,1024]{1,0:T(8,128)(2,1)S(1)} collective-permute-done((bf16[128,1024]{1,0:T(8,128)(2,1)S(1)}, bf16[128,1024]{1,0:T(8,128)(2,1)S(1)}, u32[]{:S(2)}, u32[]{:S(2)}) %collective-permute-start.1) | collective-permute-done | bytes 262176 | tf_op jit(solution)/shard_map/ppermute | solution.py:605
  19.4 0.5 shard_map.133.refs_2_
  19.9 1.0 %collective-permute-done.6.refs_0_.refs_7_ = bf16[128,1024]{1,0:T(8,128)(2,1)S(1)} collective-permute-done((bf16[128,1024]{1,0:T(8,128)(2,1)S(1)}, bf16[128,1024]{1,0:T(8,128)(2,1)S(1)}, u32[]{:S(2)}, u32[]{:S(2)}) %collective-permute-start.6) | collective-permute-done | bytes 262176 | tf_op jit(solution)/shard_map/ppermute | solution.py:24
  20.9 0.5 shard_map.134
  21.4 3.8 %collective-permute-start.7 = (bf16[8,1024]{1,0:T(8,128)(2,1)S(1)}, bf16[8,1024]{1,0:T(8,128)(2,1)S(1)}, u32[]{:S(2)}, u32[]{:S(2)}) collective-permute-start(bf16[8,1024]{1,0:T(8,128)(2,1)S(1)} %get-tuple-element.43), channel_id=1, source_target_pairs={{0,8},{8,16},{16,24},{1,9},{9,17},{17,25},{2,10},{10,18},{18,26},{... | collective-permute-start | bytes 49160 | tf_op jit(solution)/shard_map/ppermute | solution.py:621
  25.3 0.8 %shard_map.135 = (bf16[128,1024]{1,0:T(8,128)(2,1)S(1)}, f32[128,544]{1,0:T(8,128)S(1)}) custom-call(bf16[128,1024]{1,0:T(8,128)(2,1)S(1)} %get-tuple-element.42.x_ref, f32[4,1024]{1,0:T(4,128)S(1)} %copy-done.4, f32[1,1024]{1,0:T(1,128)S(1)} %bitcast.20, bf16[544,1024]{1,0:T(8,128)(2,1)S(1)} %bitcast.13), custom_call_target="tpu_custom_call" | custom-call | flops 142606336 | bytes 1114112 | tf_op jit(solution)/shard_map/pallas_call | solution.py:218
  26.1 0.4 collective-permute-done.7.tail_ref
  26.5 0.4 shard_map.136
  27.0 1.3 %collective-permute-done.8.refs_1_ = bf16[64,544]{1,0:T(8,128)(2,1)S(1)} collective-permute-done((bf16[64,544]{1,0:T(8,128)(2,1)S(1)}, bf16[64,544]{1,0:T(8,128)(2,1)S(1)}, u32[]{:S(2)}, u32[]{:S(2)}) %collective-permute-start.8) | collective-permute-done | bytes 69664 | tf_op jit(solution)/shard_map/ppermute | solution.py:24
  28.3 1.2 %collective-permute-start.11 = (bf16[64,544]{1,0:T(8,128)(2,1)S(1)}, bf16[64,544]{1,0:T(8,128)(2,1)S(1)}, u32[]{:S(2)}, u32[]{:S(2)}) collective-permute-start(bf16[64,544]{1,0:T(8,128)(2,1)S(1)} %shard_map.137.refs_0_), channel_id=1, source_target_pairs={{0,6},{1,7},{2,4},{3,5},{4,2},{5,3},{6,0},{7,1},{8,14},{9,15},{10,... | collective-permute-start | bytes 208904 | tf_op jit(solution)/shard_map/ppermute | solution.py:24
  29.5 1.8 %collective-permute-start.10 = (bf16[64,544]{1,0:T(8,128)(2,1)S(1)}, bf16[64,544]{1,0:T(8,128)(2,1)S(1)}, u32[]{:S(2)}, u32[]{:S(2)}) collective-permute-start(bf16[64,544]{1,0:T(8,128)(2,1)S(1)} %shard_map.137.refs_0_), channel_id=1, source_target_pairs={{0,4},{1,5},{2,6},{3,7},{4,0},{5,1},{6,2},{7,3},{8,12},{9,13},{10,... | collective-permute-start | bytes 208904 | tf_op jit(solution)/shard_map/ppermute | solution.py:24
  31.3 0.5 collective-permute-start.9
  31.9 2.4 %shard_map.138.gate_ref = f32[128,1024]{1,0:T(8,128)S(1)} custom-call(bf16[128,1024]{1,0:T(8,128)(2,1)S(1)} %copy-done.2, bf16[128,1024]{1,0:T(8,128)(2,1)S(1)} %collective-permute-done.2.refs_0_.refs_1_, bf16[128,1024]{1,0:T(8,128)(2,1)S(1)} %collective-permute-done.refs_1_.refs_2_, bf16[128,1024]{1,0:T(8,128)(2,1)S(1)} %collective-permute-done.3.refs_2_.refs_3_, ...), custom_call_target="tpu_custom_call" | custom-call | flops 2147483648 | bytes 16777216 | tf_op jit(solution)/shard_map/pallas_call | solution.py:162
  34.3 1.2 %collective-permute-done.10.refs_2_ = bf16[64,544]{1,0:T(8,128)(2,1)S(1)} collective-permute-done((bf16[64,544]{1,0:T(8,128)(2,1)S(1)}, bf16[64,544]{1,0:T(8,128)(2,1)S(1)}, u32[]{:S(2)}, u32[]{:S(2)}) %collective-permute-start.10) | collective-permute-done | bytes 69664 | tf_op jit(solution)/shard_map/ppermute | solution.py:24
  35.5 0.2 collective-permute-done.9.refs_1_
  35.8 0.1 collective-permute-start.12
  35.9 1.3 %collective-permute-done.12.refs_1_ = bf16[64,544]{1,0:T(8,128)(2,1)S(1)} collective-permute-done((bf16[64,544]{1,0:T(8,128)(2,1)S(1)}, bf16[64,544]{1,0:T(8,128)(2,1)S(1)}, u32[]{:S(2)}, u32[]{:S(2)}) %collective-permute-start.12) | collective-permute-done | bytes 69664 | tf_op jit(solution)/shard_map/ppermute | solution.py:24
  37.1 2.5 %shard_map.140 = (f32[17,1024]{1,0:T(8,128)S(1)}, bf16[17,1024]{1,0:T(8,128)(2,1)S(1)}, f32[1024,128]{1,0:T(8,128)S(1)}, f32[1024,128]{1,0:T(8,128)S(1)}, f32[20...) custom-call(bf16[64,544]{1,0:T(8,128)(2,1)S(1)} %shard_map.139.refs_0_, bf16[64,544]{1,0:T(8,128)(2,1)S(1)} %collective-permute-done.12.refs_1_, ...), custom_call_target="tpu_custom_call" | custom-call | flops 16777216 | bytes 1048576 | tf_op jit(solution)/shard_map/pallas_call | solution.py:329
  39.6 2.4 %collective-permute-start.13 = (bf16[17,1024]{1,0:T(8,128)(2,1)S(1)}, bf16[17,1024]{1,0:T(8,128)(2,1)S(1)}, u32[]{:S(2)}, u32[]{:S(2)}) collective-permute-start(bf16[17,1024]{1,0:T(8,128)(2,1)S(1)} %get-tuple-element.62), channel_id=1, source_target_pairs={{0,8},{8,0},{16,24},{24,16},{1,9},{9,1},{17,25},{25,17},{2,10},{10... | collective-permute-start | bytes 104456 | tf_op jit(solution)/shard_map/ppermute | solution.py:24
  42.0 2.6 %shard_map.141 = (f32[1024,128]{1,0:T(8,128)S(1)}, f32[1024,128]{1,0:T(8,128)S(1)}, f32[2048,128]{1,0:T(8,128)S(1)}) custom-call(f32[1024,128]{1,0:T(8,128)S(1)} %get-tuple-element.54.step_ref, f32[1024,128]{1,0:T(8,128)S(1)} %get-tuple-element.55.drive_ref, f32[2048,128]{1,0:T(8,128)S(1)} %get-tuple-element.56.b_ref, ...), custom_call_target="tpu_custom_call" | custom-call | flops 16777216 | bytes 2097152 | tf_op jit(solution)/shard_map/pallas_call | solution.py:384
  44.7 2.6 %collective-permute-start.14 = (bf16[17,1024]{1,0:T(8,128)(2,1)S(1)}, bf16[17,1024]{1,0:T(8,128)(2,1)S(1)}, u32[]{:S(2)}, u32[]{:S(2)}) collective-permute-start(bf16[17,1024]{1,0:T(8,128)(2,1)S(1)} %get-tuple-element.64), channel_id=1, source_target_pairs={{0,16},{8,24},{16,0},{24,8},{1,17},{9,25},{17,1},{25,9},{2,18},{10... | collective-permute-start | bytes 104456 | tf_op jit(solution)/shard_map/ppermute | solution.py:24
  47.4 1.4 %shard_map.143.q_ref = f32[16384,128]{1,0:T(8,128)S(1)} custom-call(f32[1024,128]{1,0:T(8,128)S(1)} %get-tuple-element.59.cum_ref, f32[2048,128]{1,0:T(8,128)S(1)} %get-tuple-element.60.c_ref, f32[16,1024]{1,0:T(8,128)S(1)} %bitcast.18), custom_call_target="tpu_custom_call" | custom-call | flops 6291456 | bytes 524288 | tf_op jit(solution)/shard_map/pallas_call | solution.py:415
  48.8 1.0 %collective-permute-done.14.got_ref = bf16[17,1024]{1,0:T(8,128)(2,1)S(1)} collective-permute-done((bf16[17,1024]{1,0:T(8,128)(2,1)S(1)}, bf16[17,1024]{1,0:T(8,128)(2,1)S(1)}, u32[]{:S(2)}, u32[]{:S(2)}) %collective-permute-start.14) | collective-permute-done | bytes 34848 | tf_op jit(solution)/shard_map/ppermute | solution.py:24
  49.8 1.4 %shard_map.144 = (bf16[128,1024]{1,0:T(8,128)(2,1)S(1)}, f32[16,1024]{1,0:T(8,128)}) custom-call(f32[1024,128]{1,0:T(8,128)S(1)} %get-tuple-element.58.y_ref, f32[16384,128]{1,0:T(8,128)S(1)} %shard_map.143.q_ref, f32[17,1024]{1,0:T(8,128)S(1)} %get-tuple-element.61.group_ref.end_ref, bf16[17,1024]{1,0:T(8,128)(2,1)S(1)} %collective-permute-done.14.got_ref, ...), custom_call_target="tpu_custom_call" | custom-call | flops 12582912 | bytes 1048576 | tf_op jit(solution)/shard_map/pallas_call | solution.py:546
  51.2 0.7 %shard_map.149 = bf16[2,128,1024]{2,1,0:T(8,128)(2,1)S(1)} custom-call(bf16[128,1024]{1,0:T(8,128)(2,1)S(1)} %get-tuple-element.68.g_ref, bf16[1024,8192]{1,0:T(8,128)(2,1)S(1)} %bitcast.10), custom_call_target="tpu_custom_call" | custom-call | flops 536870912 | bytes 4194304 | tf_op jit(solution)/shard_map/pallas_call | solution.py:574
  51.9 0.1 collective-permute-start.16
  52.0 0.7 %shard_map.146 = bf16[2,128,1024]{2,1,0:T(8,128)(2,1)S(1)} custom-call(bf16[128,1024]{1,0:T(8,128)(2,1)S(1)} %get-tuple-element.68.g_ref, bf16[1024,8192]{1,0:T(8,128)(2,1)S(1)} %bitcast.10), custom_call_target="tpu_custom_call" | custom-call | flops 536870912 | bytes 4194304 | tf_op jit(solution)/shard_map/pallas_call | solution.py:574
  52.7 0.5 collective-permute-start.15
  53.3 0.7 %shard_map.148.a_ref = bf16[2,128,1024]{2,1,0:T(8,128)(2,1)S(1)} custom-call(bf16[128,1024]{1,0:T(8,128)(2,1)S(1)} %get-tuple-element.68.g_ref, bf16[1024,8192]{1,0:T(8,128)(2,1)S(1)} %bitcast.10), custom_call_target="tpu_custom_call" | custom-call | flops 536870912 | bytes 4194304 | tf_op jit(solution)/shard_map/pallas_call | solution.py:574
  54.0 0.1 shard_map.150
  54.1 0.6 collective-permute-start.18
  54.7 0.7 %shard_map.145.a_ref = bf16[2,128,1024]{2,1,0:T(8,128)(2,1)S(1)} custom-call(bf16[128,1024]{1,0:T(8,128)(2,1)S(1)} %get-tuple-element.68.g_ref, bf16[1024,8192]{1,0:T(8,128)(2,1)S(1)} %bitcast.10), custom_call_target="tpu_custom_call" | custom-call | flops 536870912 | bytes 4194304 | tf_op jit(solution)/shard_map/pallas_call | solution.py:574
  55.5 1.6 %collective-permute-start.17 = (bf16[128,1024]{1,0:T(8,128)(2,1)S(1)}, bf16[128,1024]{1,0:T(8,128)(2,1)S(1)}, u32[]{:S(2)}, u32[]{:S(2)}) collective-permute-start(bf16[128,1024]{1,0:T(8,128)(2,1)S(1)} %get-tuple-element.70), channel_id=1, source_target_pairs={{0,2},{1,5},{2,0},{3,7},{4,6},{5,1},{6,4},{7,3},{8,10},{9,13},{10,... | collective-permute-start | bytes 786440 | tf_op jit(solution)/shard_map/ppermute | solution.py:669
  57.0 0.1 shard_map.147
  57.2 3.4 %collective-permute-done.18.refs_1_ = bf16[128,1024]{1,0:T(8,128)(2,1)S(1)} collective-permute-done((bf16[128,1024]{1,0:T(8,128)(2,1)S(1)}, bf16[128,1024]{1,0:T(8,128)(2,1)S(1)}, u32[]{:S(2)}, u32[]{:S(2)}) %collective-permute-start.18) | collective-permute-done | bytes 262176 | tf_op jit(solution)/shard_map/ppermute | solution.py:668
  60.6 0.4 collective-permute-start.19
  61.0 3.3 %collective-permute-done.17.refs_1_ = bf16[128,1024]{1,0:T(8,128)(2,1)S(1)} collective-permute-done((bf16[128,1024]{1,0:T(8,128)(2,1)S(1)}, bf16[128,1024]{1,0:T(8,128)(2,1)S(1)}, u32[]{:S(2)}, u32[]{:S(2)}) %collective-permute-start.17) | collective-permute-done | bytes 262176 | tf_op jit(solution)/shard_map/ppermute | solution.py:669
  64.3 2.8 %collective-permute-done.19.refs_2_ = bf16[128,1024]{1,0:T(8,128)(2,1)S(1)} collective-permute-done((bf16[128,1024]{1,0:T(8,128)(2,1)S(1)}, bf16[128,1024]{1,0:T(8,128)(2,1)S(1)}, u32[]{:S(2)}, u32[]{:S(2)}) %collective-permute-start.19) | collective-permute-done | bytes 262176 | tf_op jit(solution)/shard_map/ppermute | solution.py:670
  67.1 0.8 %shard_map.152 = bf16[128,1024]{1,0:T(8,128)(2,1)} custom-call(bf16[128,1024]{1,0:T(8,128)(2,1)S(1)} %get-tuple-element.69.refs_0_, bf16[128,1024]{1,0:T(8,128)(2,1)S(1)} %collective-permute-done.17.refs_1_, bf16[128,1024]{1,0:T(8,128)(2,1)S(1)} %collective-permute-done.19.refs_2_), custom_call_target="tpu_custom_call" | custom-call | flops 393216 | bytes 786432 | tf_op jit(solution)/shard_map/pallas_call | solution.py:437
  (52 shorter events, 0.4 us)
Async XLA Ops:
  0.6 5.9 %copy-start.2 = (bf16[128,1024]{1,0:T(8,128)(2,1)S(1)}, bf16[128,1024]{1,0:T(8,128)(2,1)}, u32[]{:S(2)}) copy-start(bf16[128,1024]{1,0:T(8,128)(2,1)} %refs_0_.2) | copy-start | bytes 786436
  0.6 13.9 %copy-start = (bf16[8192,1024]{1,0:T(8,128)(2,1)S(1)}, bf16[8192,1024]{1,0:T(8,128)(2,1)}, u32[]{:S(2)}) copy-start(bf16[8192,1024]{1,0:T(8,128)(2,1)} %refs_1_.5) | copy-start | bytes 50331652
  0.6 7.6 %collective-permute-start = (bf16[128,1024]{1,0:T(8,128)(2,1)}, bf16[128,1024]{1,0:T(8,128)(2,1)S(1)}, u32[]{:S(2)}, u32[]{:S(2)}) collective-permute-start(bf16[128,1024]{1,0:T(8,128)(2,1)} %refs_0_.2), channel_id=1, source_target_pairs={{0,4},{1,3},{2,6},{3,1},{4,0},{5,7},{6,2},{7,5},{8,12},{9,11},{10,... | collective-permute-start | bytes 786440 | tf_op jit(solution)/shard_map/ppermute | solution.py:601
  6.6 6.4 %collective-permute-start.4 = (bf16[128,1024]{1,0:T(8,128)(2,1)S(1)}, bf16[128,1024]{1,0:T(8,128)(2,1)S(1)}, u32[]{:S(2)}, u32[]{:S(2)}) collective-permute-start(bf16[128,1024]{1,0:T(8,128)(2,1)S(1)} %copy-done.2), channel_id=1, source_target_pairs={{0,2},{1,5},{2,0},{3,7},{4,6},{5,1},{6,4},{7,3},{8,10},{9,13},{10,... | collective-permute-start | bytes 786440 | tf_op jit(solution)/shard_map/ppermute | solution.py:603
  8.0 6.4 %collective-permute-start.2 = (bf16[128,1024]{1,0:T(8,128)(2,1)S(1)}, bf16[128,1024]{1,0:T(8,128)(2,1)S(1)}, u32[]{:S(2)}, u32[]{:S(2)}) collective-permute-start(bf16[128,1024]{1,0:T(8,128)(2,1)S(1)} %copy-done.2), channel_id=1, source_target_pairs={{0,1},{1,0},{2,3},{3,2},{4,5},{5,4},{6,7},{7,6},{8,9},{9,8},{10,11... | collective-permute-start | bytes 786440 | tf_op jit(solution)/shard_map/ppermute | solution.py:24
  8.3 6.2 %collective-permute-start.3 = (bf16[128,1024]{1,0:T(8,128)(2,1)S(1)}, bf16[128,1024]{1,0:T(8,128)(2,1)S(1)}, u32[]{:S(2)}, u32[]{:S(2)}) collective-permute-start(bf16[128,1024]{1,0:T(8,128)(2,1)S(1)} %collective-permute-done.refs_1_.refs_2_), channel_id=1, source_target_pairs={{0,1},{1,0},{2,3},{3,2},{4,5},{5,4},{6,7},{7,6},{8,9},{9,8},{10,11... | collective-permute-start | bytes 786440 | tf_op jit(solution)/shard_map/ppermute | solution.py:24
  13.0 1.5 %collective-permute-start.5 = (bf16[128,1024]{1,0:T(8,128)(2,1)S(1)}, bf16[128,1024]{1,0:T(8,128)(2,1)S(1)}, u32[]{:S(2)}, u32[]{:S(2)}) collective-permute-start(bf16[128,1024]{1,0:T(8,128)(2,1)S(1)} %collective-permute-done.4.refs_3_.refs_4_), channel_id=1, source_target_pairs={{0,1},{1,0},{2,3},{3,2},{4,5},{5,4},{6,7},{7,6},{8,9},{9,8},{10,11... | collective-permute-start | bytes 786440 | tf_op jit(solution)/shard_map/ppermute | solution.py:24
  13.0 6.4 %collective-permute-start.1 = (bf16[128,1024]{1,0:T(8,128)(2,1)S(1)}, bf16[128,1024]{1,0:T(8,128)(2,1)S(1)}, u32[]{:S(2)}, u32[]{:S(2)}) collective-permute-start(bf16[128,1024]{1,0:T(8,128)(2,1)S(1)} %collective-permute-done.refs_1_.refs_2_), channel_id=1, source_target_pairs={{0,2},{1,5},{2,0},{3,7},{4,6},{5,1},{6,4},{7,3},{8,10},{9,13},{10,... | collective-permute-start | bytes 786440 | tf_op jit(solution)/shard_map/ppermute | solution.py:605
  16.1 9.1 %copy-start.1 = (bf16[1024,544]{0,1:T(8,128)(2,1)S(1)}, bf16[1024,544]{0,1:T(8,128)(2,1)}, u32[]{:S(2)}) copy-start(bf16[1024,544]{0,1:T(8,128)(2,1)} %param.17) | copy-start | bytes 3342340
  16.1 9.1 %copy-start.4 = (f32[4,1024]{1,0:T(4,128)S(1)}, f32[4,1024]{1,0:T(4,128)}, u32[]{:S(2)}) copy-start(f32[4,1024]{1,0:T(4,128)} %w_ref.7) | copy-start | bytes 49156
  16.1 9.1 %copy-start.5 = (f32[1024]{0:T(1024)S(1)}, f32[1024]{0:T(1024)}, u32[]{:S(2)}) copy-start(f32[1024]{0:T(1024)} %param.16) | copy-start | bytes 12292
  16.1 15.7 %slice-start.4 = ((s8[16777216]{0:T(1024)(128)(4,1)}), s8[4194304]{0:T(1024)(128)(4,1)S(1)}, s32[]{:S(2)}) async-start(s8[16777216]{0:T(1024)(128)(4,1)} %bitcast.11), calls=%async_computation.4 | async-start | bytes 8388608
  16.1 15.7 %slice-start.5 = ((s8[16777216]{0:T(1024)(128)(4,1)}), s8[4194304]{0:T(1024)(128)(4,1)S(1)}, s32[]{:S(2)}) async-start(s8[16777216]{0:T(1024)(128)(4,1)} %bitcast.11), calls=%async_computation.5 | async-start | bytes 8388608
  19.4 1.5 %collective-permute-start.6 = (bf16[128,1024]{1,0:T(8,128)(2,1)S(1)}, bf16[128,1024]{1,0:T(8,128)(2,1)S(1)}, u32[]{:S(2)}, u32[]{:S(2)}) collective-permute-start(bf16[128,1024]{1,0:T(8,128)(2,1)S(1)} %collective-permute-done.1.refs_0_.refs_6_), channel_id=1, source_target_pairs={{0,1},{1,0},{2,3},{3,2},{4,5},{5,4},{6,7},{7,6},{8,9},{9,8},{10,11... | collective-permute-start | bytes 786440 | tf_op jit(solution)/shard_map/ppermute | solution.py:24
  19.8 12.0 %slice-start.6 = ((s8[16777216]{0:T(1024)(128)(4,1)}), s8[4194304]{0:T(1024)(128)(4,1)S(1)}, s32[]{:S(2)}) async-start(s8[16777216]{0:T(1024)(128)(4,1)} %bitcast.11), calls=%async_computation.6 | async-start | bytes 8388608
  19.9 12.0 %slice-start.7 = ((s8[16777216]{0:T(1024)(128)(4,1)}), s8[4194304]{0:T(1024)(128)(4,1)S(1)}, s32[]{:S(2)}) async-start(s8[16777216]{0:T(1024)(128)(4,1)} %bitcast.11), calls=%async_computation.7 | async-start | bytes 8388608
  19.9 17.3 %copy-start.3 = (f32[1024,16]{0,1:T(8,128)S(1)}, f32[1024,16]{0,1:T(8,128)}, u32[]{:S(2)}) copy-start(f32[1024,16]{0,1:T(8,128)} %param.20) | copy-start | bytes 196612
  19.9 17.3 %copy-start.7 = (bf16[512,1024]{1,0:T(8,128)(2,1)S(1)}, bf16[512,1024]{1,0:T(8,128)(2,1)}, u32[]{:S(2)}) copy-start(bf16[512,1024]{1,0:T(8,128)(2,1)} %refs_3_.1) | copy-start | bytes 3145732
  19.9 17.2 %copy-start.8 = (f32[1024,16]{0,1:T(8,128)S(1)}, f32[1024,16]{0,1:T(8,128)}, u32[]{:S(2)}) copy-start(f32[1024,16]{0,1:T(8,128)} %param.23) | copy-start | bytes 196612
  19.9 17.2 %copy-start.9 = (f32[1024]{0:T(1024)S(1)}, f32[1024]{0:T(1024)}, u32[]{:S(2)}) copy-start(f32[1024]{0:T(1024)} %param.19) | copy-start | bytes 12292
  21.4 5.1 %collective-permute-start.7 = (bf16[8,1024]{1,0:T(8,128)(2,1)S(1)}, bf16[8,1024]{1,0:T(8,128)(2,1)S(1)}, u32[]{:S(2)}, u32[]{:S(2)}) collective-permute-start(bf16[8,1024]{1,0:T(8,128)(2,1)S(1)} %get-tuple-element.43), channel_id=1, source_target_pairs={{0,8},{8,16},{16,24},{1,9},{9,17},{17,25},{2,10},{10,18},{18,26},{... | collective-permute-start | bytes 49160 | tf_op jit(solution)/shard_map/ppermute | solution.py:621
  26.9 1.3 %collective-permute-start.8 = (bf16[64,544]{1,0:T(8,128)(2,1)S(1)}, bf16[64,544]{1,0:T(8,128)(2,1)S(1)}, u32[]{:S(2)}, u32[]{:S(2)}) collective-permute-start(bf16[64,544]{1,0:T(8,128)(2,1)S(1)} %get-tuple-element.48), channel_id=1, source_target_pairs={{0,1},{1,0},{2,3},{3,2},{4,5},{5,4},{6,7},{7,6},{8,9},{9,8},{10,11... | collective-permute-start | bytes 208904 | tf_op jit(solution)/shard_map/ppermute | solution.py:24
  28.3 21.5 %copy-start.6 = (f32[1024]{0:T(1024)S(1)}, f32[1024]{0:T(1024)}, u32[]{:S(2)}) copy-start(f32[1024]{0:T(1024)} %param.21) | copy-start | bytes 12292
  28.3 6.0 %collective-permute-start.11 = (bf16[64,544]{1,0:T(8,128)(2,1)S(1)}, bf16[64,544]{1,0:T(8,128)(2,1)S(1)}, u32[]{:S(2)}, u32[]{:S(2)}) collective-permute-start(bf16[64,544]{1,0:T(8,128)(2,1)S(1)} %shard_map.137.refs_0_), channel_id=1, source_target_pairs={{0,6},{1,7},{2,4},{3,5},{4,2},{5,3},{6,0},{7,1},{8,14},{9,15},{10,... | collective-permute-start | bytes 208904 | tf_op jit(solution)/shard_map/ppermute | solution.py:24
  29.5 6.0 %collective-permute-start.10 = (bf16[64,544]{1,0:T(8,128)(2,1)S(1)}, bf16[64,544]{1,0:T(8,128)(2,1)S(1)}, u32[]{:S(2)}, u32[]{:S(2)}) collective-permute-start(bf16[64,544]{1,0:T(8,128)(2,1)S(1)} %shard_map.137.refs_0_), channel_id=1, source_target_pairs={{0,4},{1,5},{2,6},{3,7},{4,0},{5,1},{6,2},{7,3},{8,12},{9,13},{10,... | collective-permute-start | bytes 208904 | tf_op jit(solution)/shard_map/ppermute | solution.py:24
  31.3 4.4 %collective-permute-start.9 = (bf16[64,544]{1,0:T(8,128)(2,1)S(1)}, bf16[64,544]{1,0:T(8,128)(2,1)S(1)}, u32[]{:S(2)}, u32[]{:S(2)}) collective-permute-start(bf16[64,544]{1,0:T(8,128)(2,1)S(1)} %shard_map.137.refs_0_), channel_id=1, source_target_pairs={{0,2},{1,3},{2,0},{3,1},{4,6},{5,7},{6,4},{7,5},{8,10},{9,11},{10,... | collective-permute-start | bytes 208904 | tf_op jit(solution)/shard_map/ppermute | solution.py:24
  31.8 19.3 %slice-start = ((s8[16777216]{0:T(1024)(128)(4,1)}), s8[4194304]{0:T(1024)(128)(4,1)S(1)}, s32[]{:S(2)}) async-start(s8[16777216]{0:T(1024)(128)(4,1)} %bitcast.9), calls=%async_computation | async-start | bytes 8388608
  31.9 19.3 %slice-start.1 = ((s8[16777216]{0:T(1024)(128)(4,1)}), s8[4194304]{0:T(1024)(128)(4,1)S(1)}, s32[]{:S(2)}) async-start(s8[16777216]{0:T(1024)(128)(4,1)} %bitcast.9), calls=%async_computation.1 | async-start | bytes 8388608
  35.8 1.3 %collective-permute-start.12 = (bf16[64,544]{1,0:T(8,128)(2,1)S(1)}, bf16[64,544]{1,0:T(8,128)(2,1)S(1)}, u32[]{:S(2)}, u32[]{:S(2)}) collective-permute-start(bf16[64,544]{1,0:T(8,128)(2,1)S(1)} %shard_map.139.refs_0_), channel_id=1, source_target_pairs={{0,1},{1,0},{2,3},{3,2},{4,5},{5,4},{6,7},{7,6},{8,9},{9,8},{10,11... | collective-permute-start | bytes 208904 | tf_op jit(solution)/shard_map/ppermute | solution.py:24
  39.6 5.0 %collective-permute-start.13 = (bf16[17,1024]{1,0:T(8,128)(2,1)S(1)}, bf16[17,1024]{1,0:T(8,128)(2,1)S(1)}, u32[]{:S(2)}, u32[]{:S(2)}) collective-permute-start(bf16[17,1024]{1,0:T(8,128)(2,1)S(1)} %get-tuple-element.62), channel_id=1, source_target_pairs={{0,8},{8,0},{16,24},{24,16},{1,9},{9,1},{17,25},{25,17},{2,10},{10... | collective-permute-start | bytes 104456 | tf_op jit(solution)/shard_map/ppermute | solution.py:24
  42.0 9.2 %slice-start.2 = ((s8[16777216]{0:T(1024)(128)(4,1)}), s8[4194304]{0:T(1024)(128)(4,1)S(1)}, s32[]{:S(2)}) async-start(s8[16777216]{0:T(1024)(128)(4,1)} %bitcast.9), calls=%async_computation.2 | async-start | bytes 8388608
  44.7 5.1 %collective-permute-start.14 = (bf16[17,1024]{1,0:T(8,128)(2,1)S(1)}, bf16[17,1024]{1,0:T(8,128)(2,1)S(1)}, u32[]{:S(2)}, u32[]{:S(2)}) collective-permute-start(bf16[17,1024]{1,0:T(8,128)(2,1)S(1)} %get-tuple-element.64), channel_id=1, source_target_pairs={{0,16},{8,24},{16,0},{24,8},{1,17},{9,25},{17,1},{25,9},{2,18},{10... | collective-permute-start | bytes 104456 | tf_op jit(solution)/shard_map/ppermute | solution.py:24
  47.4 3.8 %slice-start.3 = ((s8[16777216]{0:T(1024)(128)(4,1)}), s8[4194304]{0:T(1024)(128)(4,1)S(1)}, s32[]{:S(2)}) async-start(s8[16777216]{0:T(1024)(128)(4,1)} %bitcast.9), calls=%async_computation.3 | async-start | bytes 8388608
  51.9 2.1 %collective-permute-start.16 = (bf16[2,128,1024]{2,1,0:T(8,128)(2,1)S(1)}, bf16[2,128,1024]{2,1,0:T(8,128)(2,1)S(1)}, u32[]{:S(2)}, u32[]{:S(2)}) collective-permute-start(bf16[2,128,1024]{2,1,0:T(8,128)(2,1)S(1)} %shard_map.149), channel_id=1, source_target_pairs={{0,1},{1,0},{2,3},{3,2},{4,5},{5,4},{6,7},{7,6},{8,9},{9,8},{10,11... | collective-permute-start | bytes 1572872 | tf_op jit(solution)/shard_map/ppermute | solution.py:24
  52.7 4.3 %collective-permute-start.15 = (bf16[2,128,1024]{2,1,0:T(8,128)(2,1)S(1)}, bf16[2,128,1024]{2,1,0:T(8,128)(2,1)S(1)}, u32[]{:S(2)}, u32[]{:S(2)}) collective-permute-start(bf16[2,128,1024]{2,1,0:T(8,128)(2,1)S(1)} %shard_map.146), channel_id=1, source_target_pairs={{0,1},{1,0},{2,3},{3,2},{4,5},{5,4},{6,7},{7,6},{8,9},{9,8},{10,11... | collective-permute-start | bytes 1572872 | tf_op jit(solution)/shard_map/ppermute | solution.py:24
  54.1 6.4 %collective-permute-start.18 = (bf16[128,1024]{1,0:T(8,128)(2,1)S(1)}, bf16[128,1024]{1,0:T(8,128)(2,1)S(1)}, u32[]{:S(2)}, u32[]{:S(2)}) collective-permute-start(bf16[128,1024]{1,0:T(8,128)(2,1)S(1)} %get-tuple-element.72), channel_id=1, source_target_pairs={{0,2},{1,5},{2,0},{3,7},{4,6},{5,1},{6,4},{7,3},{8,10},{9,13},{10,... | collective-permute-start | bytes 786440 | tf_op jit(solution)/shard_map/ppermute | solution.py:668
  55.5 8.8 %collective-permute-start.17 = (bf16[128,1024]{1,0:T(8,128)(2,1)S(1)}, bf16[128,1024]{1,0:T(8,128)(2,1)S(1)}, u32[]{:S(2)}, u32[]{:S(2)}) collective-permute-start(bf16[128,1024]{1,0:T(8,128)(2,1)S(1)} %get-tuple-element.70), channel_id=1, source_target_pairs={{0,2},{1,5},{2,0},{3,7},{4,6},{5,1},{6,4},{7,3},{8,10},{9,13},{10,... | collective-permute-start | bytes 786440 | tf_op jit(solution)/shard_map/ppermute | solution.py:669
  60.6 6.4 %collective-permute-start.19 = (bf16[128,1024]{1,0:T(8,128)(2,1)S(1)}, bf16[128,1024]{1,0:T(8,128)(2,1)S(1)}, u32[]{:S(2)}, u32[]{:S(2)}) collective-permute-start(bf16[128,1024]{1,0:T(8,128)(2,1)S(1)} %shard_map.151), channel_id=1, source_target_pairs={{0,4},{1,3},{2,6},{3,1},{4,0},{5,7},{6,2},{7,5},{8,12},{9,11},{10,... | collective-permute-start | bytes 786440 | tf_op jit(solution)/shard_map/ppermute | solution.py:670

commit v4 on v3

--- a/solution.py
+++ b/solution.py
@@ -150,6 +150,27 @@
         outs[1][...] = total[total.shape[0] - edge :].astype(BF16)
 
 
+def edge_kernel(role, x_ref, w_ref, acc_ref, out_ref):
+    rows, feat = x_ref.shape
+    start = rows - out_ref.shape[0]
+    at = pl.ds(pl.multiple_of(peer(role) * feat, feat), feat)
+    part = jnp.dot(x_ref[start:, :], w_ref[at, :], preferred_element_type=F32)
+    out_ref[...] = (acc_ref[start:, :] + part).astype(BF16)
+
+
+def mm_edge(x, role, weight, acc):
+    vm = pl.BlockSpec(memory_space=VMEM)
+    feat, ch = x.shape[1], weight.shape[1]
+    return pl.pallas_call(
+        functools.partial(edge_kernel, role),
+        in_specs=[vm] * 3,
+        out_specs=vm,
+        out_shape=jax.ShapeDtypeStruct((EDGE, ch), BF16),
+        compiler_params=params(4),
+        cost_estimate=cost(2 * EDGE * feat * ch, 2 * feat * ch),
+    )(x, weight, acc)
+
+
 def mm(blocks, roles, weight, acc, edge=0):
     rows, feat = blocks[0].shape
     ch = weight.shape[1]
@@ -481,8 +502,8 @@
     high_s = jnp.where(upper, ms, gs)
     total = jnp.exp(-decay * high_s) * low + high
     pack_ref[:STATE, :] = total.astype(BF16)
-    pack_ref[STATE:, :] = (ms + gs).astype(BF16)
     if not last:
+        pack_ref[STATE:, :] = (ms + gs).astype(BF16)
         refs[-3][:STATE, :] = total
         refs[-3][STATE:, :] = ms + gs
 
@@ -497,7 +518,7 @@
         out_specs=[vm] * (2 if last else 3),
         out_shape=[jax.ShapeDtypeStruct(group.shape, F32)] * (not last)
         + [
-            jax.ShapeDtypeStruct(group.shape, BF16),
+            jax.ShapeDtypeStruct((STATE + (not last), group.shape[1]), BF16),
             jax.ShapeDtypeStruct(group.shape, F32),
         ],
         compiler_params=params(3),
@@ -611,7 +632,8 @@
         qd = flip(vd, "tp", 1)
         inner, = mm([vd], [6], inner_w, inner)
         qd = tie(qd, inner)
-        inner_x, edge_x = mm([qd], [7], inner_w, inner, EDGE)
+        edge_x = mm_edge(qd, 7, inner_w, inner)
+        inner_x, _ = mm([qd], [7], inner_w, inner, EDGE)
     else:
         piece = lax.all_gather(tokens, "tp", axis=1, tiled=True)
         inner_x = jnp.dot(piece, inner_weight, preferred_element_type=F32).astype(BF16)

time: 68.1 us -> 68 us (level)
  Pallas kernels: 20.9 us -> 21.9 us
    ppermute x13, starting transfers between devices: 9.6 us -> 8.91 us  [flip(): return lax.ppermute(value, axis, [(i, i ^ mask) for i in range(peers)])]
  transfers between devices with their start and end apart: 20 -> 20, of which waited for: 14 -> 13; matrix products, arithmetic and copies ran while one was open for 0% -> 0% of each run, Pallas kernels for 21% -> 23%
where the time goes in v4:
time: 68 us; the launch traced here: 67.8 us
  waiting for transfers between devices  23.5 us (35%)
  Pallas kernels  21.9 us (32%)
  starting transfers between devices  21.4 us (31%)
  between operations  0.97 us (1%)
    ppermute x13, starting transfers between devices, flip(): return lax.ppermute(value, axis, [(i, i ^ mask) for i in range(peers)])  8.91 us
    ppermute x13, waiting for transfers between devices, flip(): return lax.ppermute(value, axis, [(i, i ^ mask) for i in range(peers)])  6.01 us
    pallas_call x4, Pallas kernels, mm(): pl.pallas_call(functools.partial(mm_kernel, roles, len(extra), edge), in_...  5.4 us
    ppermute x1, waiting for transfers between devices, on_device(): vf = lax.ppermute(tie(tokens, inner), 'tp', to_first)  4.45 us
    ppermute x1, starting transfers between devices, on_device(): tail = lax.ppermute(edge_x, 'ctx', shift)  3.97 us
    ppermute x1, waiting for transfers between devices, on_device(): rd = lax.ppermute(sd, 'tp', to_first)  3.42 us
    ppermute x1, waiting for transfers between devices, on_device(): vd = lax.ppermute(vs, 'tp', to_first)  3.3 us
    ppermute x1, waiting for transfers between devices, on_device(): rf = lax.ppermute(sf, 'tp', to_first)  3.25 us
  transfers between devices with their start and end apart: 20, of which 13 were waited for; matrix products, arithmetic and copies ran while one was open for 0% of the time, Pallas kernels for 23%

profile of v4, /device:TPU:0, one launch (start us, length us, event | category | flops | bytes accessed | tf_op | source)
XLA Modules:
  0.0 67.8 jit_solution(10723342569625666910)
XLA Ops:
  0.6 3.1 %collective-permute-start = (bf16[128,1024]{1,0:T(8,128)(2,1)}, bf16[128,1024]{1,0:T(8,128)(2,1)S(1)}, u32[]{:S(2)}, u32[]{:S(2)}) collective-permute-start(bf16[128,1024]{1,0:T(8,128)(2,1)} %refs_0_.2), channel_id=1, source_target_pairs={{0,4},{1,3},{2,6},{3,1},{4,0},{5,7},{6,2},{7,5},{8,12},{9,11},{10,... | collective-permute-start | bytes 786440 | tf_op jit(solution)/shard_map/ppermute | solution.py:622
  3.7 2.8 %shard_map.131.refs_6_ = f32[128,1024]{1,0:T(8,128)S(1)} custom-call(bf16[128,1024]{1,0:T(8,128)(2,1)} %refs_0_.2, bf16[8192,1024]{1,0:T(8,128)(2,1)} %w_ref.7), custom_call_target="tpu_custom_call" | custom-call | flops 268435456 | bytes 2097152 | tf_op jit(solution)/shard_map/pallas_call | solution.py:117
  6.6 1.5 %collective-permute-start.4 = (bf16[128,1024]{1,0:T(8,128)(2,1)S(1)}, bf16[128,1024]{1,0:T(8,128)(2,1)S(1)}, u32[]{:S(2)}, u32[]{:S(2)}) collective-permute-start(bf16[128,1024]{1,0:T(8,128)(2,1)S(1)} %copy-done.2), channel_id=1, source_target_pairs={{0,2},{1,5},{2,0},{3,7},{4,6},{5,1},{6,4},{7,3},{8,10},{9,13},{10,... | collective-permute-start | bytes 786440 | tf_op jit(solution)/shard_map/ppermute | solution.py:624
  8.0 0.2 collective-permute-done.refs_1_.refs_2_
  8.3 0.3 collective-permute-start.3
  8.6 4.5 %collective-permute-done.4.refs_3_.refs_4_ = bf16[128,1024]{1,0:T(8,128)(2,1)S(1)} collective-permute-done((bf16[128,1024]{1,0:T(8,128)(2,1)S(1)}, bf16[128,1024]{1,0:T(8,128)(2,1)S(1)}, u32[]{:S(2)}, u32[]{:S(2)}) %collective-permute-start.4) | collective-permute-done | bytes 262176 | tf_op jit(solution)/shard_map/ppermute | solution.py:624
  13.0 1.4 %collective-permute-start.1 = (bf16[128,1024]{1,0:T(8,128)(2,1)S(1)}, bf16[128,1024]{1,0:T(8,128)(2,1)S(1)}, u32[]{:S(2)}, u32[]{:S(2)}) collective-permute-start(bf16[128,1024]{1,0:T(8,128)(2,1)S(1)} %collective-permute-done.refs_1_.refs_2_), channel_id=1, source_target_pairs={{0,2},{1,5},{2,0},{3,7},{4,6},{5,1},{6,4},{7,3},{8,10},{9,13},{10,... | collective-permute-start | bytes 786440 | tf_op jit(solution)/shard_map/ppermute | solution.py:626
  14.4 0.1 collective-permute-done.5.refs_4_.refs_5_
  14.5 1.5 %shard_map.132.refs_2_ = f32[128,1024]{1,0:T(8,128)S(1)} custom-call(bf16[128,1024]{1,0:T(8,128)(2,1)S(1)} %collective-permute-done.2.refs_0_.refs_1_, bf16[128,1024]{1,0:T(8,128)(2,1)S(1)} %collective-permute-done.refs_1_.refs_2_, bf16[128,1024]{1,0:T(8,128)(2,1)S(1)} %collective-permute-done.3.refs_2_.refs_3_, ...), custom_call_target="tpu_custom_call" | custom-call | flops 1342177280 | bytes 10485760 | tf_op jit(solution)/shard_map/pallas_call | solution.py:183
  16.1 3.3 %collective-permute-done.1.refs_0_.refs_6_ = bf16[128,1024]{1,0:T(8,128)(2,1)S(1)} collective-permute-done((bf16[128,1024]{1,0:T(8,128)(2,1)S(1)}, bf16[128,1024]{1,0:T(8,128)(2,1)S(1)}, u32[]{:S(2)}, u32[]{:S(2)}) %collective-permute-start.1) | collective-permute-done | bytes 262176 | tf_op jit(solution)/shard_map/ppermute | solution.py:626
  19.4 0.5 shard_map.133.refs_2_.acc_ref
  19.9 1.0 %collective-permute-done.6.refs_0_.x_ref.refs_7_ = bf16[128,1024]{1,0:T(8,128)(2,1)S(1)} collective-permute-done((bf16[128,1024]{1,0:T(8,128)(2,1)S(1)}, bf16[128,1024]{1,0:T(8,128)(2,1)S(1)}, u32[]{:S(2)}, u32[]{:S(2)}) %collective-permute-start.6) | collective-permute-done | bytes 262176 | tf_op jit(solution)/shard_map/ppermute | solution.py:24
  20.9 0.4 shard_map.135
  21.4 4.0 %collective-permute-start.7 = (bf16[8,1024]{1,0:T(8,128)(2,1)S(1)}, bf16[8,1024]{1,0:T(8,128)(2,1)S(1)}, u32[]{:S(2)}, u32[]{:S(2)}) collective-permute-start(bf16[8,1024]{1,0:T(8,128)(2,1)S(1)} %shard_map.135), channel_id=1, source_target_pairs={{0,8},{8,16},{16,24},{1,9},{9,17},{17,25},{2,10},{10,18},{18,26},{... | collective-permute-start | bytes 49160 | tf_op jit(solution)/shard_map/ppermute | solution.py:643
  25.3 1.1 %shard_map.134 = (bf16[128,1024]{1,0:T(8,128)(2,1)S(1)}, bf16[8,1024]{1,0:T(8,128)(2,1)}) custom-call(bf16[128,1024]{1,0:T(8,128)(2,1)S(1)} %collective-permute-done.6.refs_0_.x_ref.refs_7_, bf16[8192,1024]{1,0:T(8,128)(2,1)S(1)} %copy-done, f32[128,1024]{1,0:T(8,128)S(1)} %shard_map.133.refs_2_.acc_ref), custom_call_target="tpu_custom_call" | custom-call | flops 268435456 | bytes 2097152 | tf_op jit(solution)/shard_map/pallas_call | solution.py:183
  26.4 0.8 %shard_map.136 = (bf16[128,1024]{1,0:T(8,128)(2,1)S(1)}, f32[128,544]{1,0:T(8,128)S(1)}) custom-call(bf16[128,1024]{1,0:T(8,128)(2,1)S(1)} %get-tuple-element.41.x_ref, f32[4,1024]{1,0:T(4,128)S(1)} %copy-done.4, f32[1,1024]{1,0:T(1,128)S(1)} %bitcast.20, bf16[544,1024]{1,0:T(8,128)(2,1)S(1)} %bitcast.13), custom_call_target="tpu_custom_call" | custom-call | flops 142606336 | bytes 1114112 | tf_op jit(solution)/shard_map/pallas_call | solution.py:239
  27.3 0.4 shard_map.137
  27.8 1.3 %collective-permute-done.8.refs_1_ = bf16[64,544]{1,0:T(8,128)(2,1)S(1)} collective-permute-done((bf16[64,544]{1,0:T(8,128)(2,1)S(1)}, bf16[64,544]{1,0:T(8,128)(2,1)S(1)}, u32[]{:S(2)}, u32[]{:S(2)}) %collective-permute-start.8) | collective-permute-done | bytes 69664 | tf_op jit(solution)/shard_map/ppermute | solution.py:24
  29.1 1.2 %collective-permute-start.11 = (bf16[64,544]{1,0:T(8,128)(2,1)S(1)}, bf16[64,544]{1,0:T(8,128)(2,1)S(1)}, u32[]{:S(2)}, u32[]{:S(2)}) collective-permute-start(bf16[64,544]{1,0:T(8,128)(2,1)S(1)} %shard_map.138.refs_0_), channel_id=1, source_target_pairs={{0,6},{1,7},{2,4},{3,5},{4,2},{5,3},{6,0},{7,1},{8,14},{9,15},{10,... | collective-permute-start | bytes 208904 | tf_op jit(solution)/shard_map/ppermute | solution.py:24
  30.3 1.8 %collective-permute-start.10 = (bf16[64,544]{1,0:T(8,128)(2,1)S(1)}, bf16[64,544]{1,0:T(8,128)(2,1)S(1)}, u32[]{:S(2)}, u32[]{:S(2)}) collective-permute-start(bf16[64,544]{1,0:T(8,128)(2,1)S(1)} %shard_map.138.refs_0_), channel_id=1, source_target_pairs={{0,4},{1,5},{2,6},{3,7},{4,0},{5,1},{6,2},{7,3},{8,12},{9,13},{10,... | collective-permute-start | bytes 208904 | tf_op jit(solution)/shard_map/ppermute | solution.py:24
  32.1 0.5 collective-permute-start.9
  32.7 2.4 %shard_map.139.gate_ref = f32[128,1024]{1,0:T(8,128)S(1)} custom-call(bf16[128,1024]{1,0:T(8,128)(2,1)S(1)} %copy-done.2, bf16[128,1024]{1,0:T(8,128)(2,1)S(1)} %collective-permute-done.2.refs_0_.refs_1_, bf16[128,1024]{1,0:T(8,128)(2,1)S(1)} %collective-permute-done.refs_1_.refs_2_, bf16[128,1024]{1,0:T(8,128)(2,1)S(1)} %collective-permute-done.3.refs_2_.refs_3_, ...), custom_call_target="tpu_custom_call" | custom-call | flops 2147483648 | bytes 16777216 | tf_op jit(solution)/shard_map/pallas_call | solution.py:183
  35.1 1.2 %collective-permute-done.10.refs_2_ = bf16[64,544]{1,0:T(8,128)(2,1)S(1)} collective-permute-done((bf16[64,544]{1,0:T(8,128)(2,1)S(1)}, bf16[64,544]{1,0:T(8,128)(2,1)S(1)}, u32[]{:S(2)}, u32[]{:S(2)}) %collective-permute-start.10) | collective-permute-done | bytes 69664 | tf_op jit(solution)/shard_map/ppermute | solution.py:24
  36.3 0.3 collective-permute-done.9.refs_1_
  36.6 0.1 collective-permute-start.12
  36.7 1.3 %collective-permute-done.12.refs_1_ = bf16[64,544]{1,0:T(8,128)(2,1)S(1)} collective-permute-done((bf16[64,544]{1,0:T(8,128)(2,1)S(1)}, bf16[64,544]{1,0:T(8,128)(2,1)S(1)}, u32[]{:S(2)}, u32[]{:S(2)}) %collective-permute-start.12) | collective-permute-done | bytes 69664 | tf_op jit(solution)/shard_map/ppermute | solution.py:24
  38.0 2.5 %shard_map.141 = (f32[17,1024]{1,0:T(8,128)S(1)}, bf16[17,1024]{1,0:T(8,128)(2,1)S(1)}, f32[1024,128]{1,0:T(8,128)S(1)}, f32[1024,128]{1,0:T(8,128)S(1)}, f32[20...) custom-call(bf16[64,544]{1,0:T(8,128)(2,1)S(1)} %shard_map.140.refs_0_, bf16[64,544]{1,0:T(8,128)(2,1)S(1)} %collective-permute-done.12.refs_1_, ...), custom_call_target="tpu_custom_call" | custom-call | flops 16777216 | bytes 1048576 | tf_op jit(solution)/shard_map/pallas_call | solution.py:350
  40.4 1.7 %collective-permute-start.13 = (bf16[17,1024]{1,0:T(8,128)(2,1)S(1)}, bf16[17,1024]{1,0:T(8,128)(2,1)S(1)}, u32[]{:S(2)}, u32[]{:S(2)}) collective-permute-start(bf16[17,1024]{1,0:T(8,128)(2,1)S(1)} %get-tuple-element.60), channel_id=1, source_target_pairs={{0,8},{8,0},{16,24},{24,16},{1,9},{9,1},{17,25},{25,17},{2,10},{10... | collective-permute-start | bytes 104456 | tf_op jit(solution)/shard_map/ppermute | solution.py:24
  42.1 2.6 %shard_map.142 = (f32[1024,128]{1,0:T(8,128)S(1)}, f32[1024,128]{1,0:T(8,128)S(1)}, f32[2048,128]{1,0:T(8,128)S(1)}) custom-call(f32[1024,128]{1,0:T(8,128)S(1)} %get-tuple-element.52.step_ref, f32[1024,128]{1,0:T(8,128)S(1)} %get-tuple-element.53.drive_ref, f32[2048,128]{1,0:T(8,128)S(1)} %get-tuple-element.54.b_ref, ...), custom_call_target="tpu_custom_call" | custom-call | flops 16777216 | bytes 2097152 | tf_op jit(solution)/shard_map/pallas_call | solution.py:405
  44.8 2.6 %collective-permute-start.14 = (bf16[16,1024]{1,0:T(8,128)(2,1)S(1)}, bf16[16,1024]{1,0:T(8,128)(2,1)S(1)}, u32[]{:S(2)}, u32[]{:S(2)}) collective-permute-start(bf16[16,1024]{1,0:T(8,128)(2,1)S(1)} %get-tuple-element.62), channel_id=1, source_target_pairs={{0,16},{8,24},{16,0},{24,8},{1,17},{9,25},{17,1},{25,9},{2,18},{10... | collective-permute-start | bytes 98312 | tf_op jit(solution)/shard_map/ppermute | solution.py:24
  47.5 1.4 %shard_map.144.q_ref = f32[16384,128]{1,0:T(8,128)S(1)} custom-call(f32[1024,128]{1,0:T(8,128)S(1)} %get-tuple-element.57.cum_ref, f32[2048,128]{1,0:T(8,128)S(1)} %get-tuple-element.58.c_ref, f32[16,1024]{1,0:T(8,128)S(1)} %bitcast.18), custom_call_target="tpu_custom_call" | custom-call | flops 6291456 | bytes 524288 | tf_op jit(solution)/shard_map/pallas_call | solution.py:436
  48.9 0.8 %collective-permute-done.14.got_ref = bf16[16,1024]{1,0:T(8,128)(2,1)S(1)} collective-permute-done((bf16[16,1024]{1,0:T(8,128)(2,1)S(1)}, bf16[16,1024]{1,0:T(8,128)(2,1)S(1)}, u32[]{:S(2)}, u32[]{:S(2)}) %collective-permute-start.14) | collective-permute-done | bytes 32800 | tf_op jit(solution)/shard_map/ppermute | solution.py:24
  49.7 1.4 %shard_map.145 = (bf16[128,1024]{1,0:T(8,128)(2,1)S(1)}, f32[16,1024]{1,0:T(8,128)}) custom-call(f32[1024,128]{1,0:T(8,128)S(1)} %get-tuple-element.56.y_ref, f32[16384,128]{1,0:T(8,128)S(1)} %shard_map.144.q_ref, f32[17,1024]{1,0:T(8,128)S(1)} %get-tuple-element.59.group_ref.end_ref, bf16[16,1024]{1,0:T(8,128)(2,1)S(1)} %collective-permute-done.14.got_ref, ...), custom_call_target="tpu_custom_call" | custom-call | flops 12582912 | bytes 1048576 | tf_op jit(solution)/shard_map/pallas_call | solution.py:567
  51.1 0.7 %shard_map.150 = bf16[2,128,1024]{2,1,0:T(8,128)(2,1)S(1)} custom-call(bf16[128,1024]{1,0:T(8,128)(2,1)S(1)} %get-tuple-element.66.g_ref, bf16[1024,8192]{1,0:T(8,128)(2,1)S(1)} %bitcast.10), custom_call_target="tpu_custom_call" | custom-call | flops 536870912 | bytes 4194304 | tf_op jit(solution)/shard_map/pallas_call | solution.py:595
  51.8 0.1 collective-permute-start.16
  51.9 0.7 %shard_map.147 = bf16[2,128,1024]{2,1,0:T(8,128)(2,1)S(1)} custom-call(bf16[128,1024]{1,0:T(8,128)(2,1)S(1)} %get-tuple-element.66.g_ref, bf16[1024,8192]{1,0:T(8,128)(2,1)S(1)} %bitcast.10), custom_call_target="tpu_custom_call" | custom-call | flops 536870912 | bytes 4194304 | tf_op jit(solution)/shard_map/pallas_call | solution.py:595
  52.7 0.5 collective-permute-start.15
  53.2 0.7 %shard_map.149.a_ref = bf16[2,128,1024]{2,1,0:T(8,128)(2,1)S(1)} custom-call(bf16[128,1024]{1,0:T(8,128)(2,1)S(1)} %get-tuple-element.66.g_ref, bf16[1024,8192]{1,0:T(8,128)(2,1)S(1)} %bitcast.10), custom_call_target="tpu_custom_call" | custom-call | flops 536870912 | bytes 4194304 | tf_op jit(solution)/shard_map/pallas_call | solution.py:595
  53.9 0.1 shard_map.151
  54.1 0.6 collective-permute-start.18
  54.7 0.7 %shard_map.146.a_ref = bf16[2,128,1024]{2,1,0:T(8,128)(2,1)S(1)} custom-call(bf16[128,1024]{1,0:T(8,128)(2,1)S(1)} %get-tuple-element.66.g_ref, bf16[1024,8192]{1,0:T(8,128)(2,1)S(1)} %bitcast.10), custom_call_target="tpu_custom_call" | custom-call | flops 536870912 | bytes 4194304 | tf_op jit(solution)/shard_map/pallas_call | solution.py:595
  55.4 1.6 %collective-permute-start.17 = (bf16[128,1024]{1,0:T(8,128)(2,1)S(1)}, bf16[128,1024]{1,0:T(8,128)(2,1)S(1)}, u32[]{:S(2)}, u32[]{:S(2)}) collective-permute-start(bf16[128,1024]{1,0:T(8,128)(2,1)S(1)} %get-tuple-element.68), channel_id=1, source_target_pairs={{0,2},{1,5},{2,0},{3,7},{4,6},{5,1},{6,4},{7,3},{8,10},{9,13},{10,... | collective-permute-start | bytes 786440 | tf_op jit(solution)/shard_map/ppermute | solution.py:691
  57.0 0.1 shard_map.148
  57.1 3.4 %collective-permute-done.18.refs_1_ = bf16[128,1024]{1,0:T(8,128)(2,1)S(1)} collective-permute-done((bf16[128,1024]{1,0:T(8,128)(2,1)S(1)}, bf16[128,1024]{1,0:T(8,128)(2,1)S(1)}, u32[]{:S(2)}, u32[]{:S(2)}) %collective-permute-start.18) | collective-permute-done | bytes 262176 | tf_op jit(solution)/shard_map/ppermute | solution.py:690
  60.6 0.4 collective-permute-start.19
  61.0 3.2 %collective-permute-done.17.refs_1_ = bf16[128,1024]{1,0:T(8,128)(2,1)S(1)} collective-permute-done((bf16[128,1024]{1,0:T(8,128)(2,1)S(1)}, bf16[128,1024]{1,0:T(8,128)(2,1)S(1)}, u32[]{:S(2)}, u32[]{:S(2)}) %collective-permute-start.17) | collective-permute-done | bytes 262176 | tf_op jit(solution)/shard_map/ppermute | solution.py:691
  64.2 2.8 %collective-permute-done.19.refs_2_ = bf16[128,1024]{1,0:T(8,128)(2,1)S(1)} collective-permute-done((bf16[128,1024]{1,0:T(8,128)(2,1)S(1)}, bf16[128,1024]{1,0:T(8,128)(2,1)S(1)}, u32[]{:S(2)}, u32[]{:S(2)}) %collective-permute-start.19) | collective-permute-done | bytes 262176 | tf_op jit(solution)/shard_map/ppermute | solution.py:692
  67.0 0.8 %shard_map.153 = bf16[128,1024]{1,0:T(8,128)(2,1)} custom-call(bf16[128,1024]{1,0:T(8,128)(2,1)S(1)} %get-tuple-element.67.refs_0_, bf16[128,1024]{1,0:T(8,128)(2,1)S(1)} %collective-permute-done.17.refs_1_, bf16[128,1024]{1,0:T(8,128)(2,1)S(1)} %collective-permute-done.19.refs_2_), custom_call_target="tpu_custom_call" | custom-call | flops 393216 | bytes 786432 | tf_op jit(solution)/shard_map/pallas_call | solution.py:458
  (53 shorter events, 0.4 us)
Async XLA Ops:
  0.6 5.9 %copy-start.2 = (bf16[128,1024]{1,0:T(8,128)(2,1)S(1)}, bf16[128,1024]{1,0:T(8,128)(2,1)}, u32[]{:S(2)}) copy-start(bf16[128,1024]{1,0:T(8,128)(2,1)} %refs_0_.2) | copy-start | bytes 786436
  0.6 13.9 %copy-start = (bf16[8192,1024]{1,0:T(8,128)(2,1)S(1)}, bf16[8192,1024]{1,0:T(8,128)(2,1)}, u32[]{:S(2)}) copy-start(bf16[8192,1024]{1,0:T(8,128)(2,1)} %w_ref.7) | copy-start | bytes 50331652
  0.6 7.6 %collective-permute-start = (bf16[128,1024]{1,0:T(8,128)(2,1)}, bf16[128,1024]{1,0:T(8,128)(2,1)S(1)}, u32[]{:S(2)}, u32[]{:S(2)}) collective-permute-start(bf16[128,1024]{1,0:T(8,128)(2,1)} %refs_0_.2), channel_id=1, source_target_pairs={{0,4},{1,3},{2,6},{3,1},{4,0},{5,7},{6,2},{7,5},{8,12},{9,11},{10,... | collective-permute-start | bytes 786440 | tf_op jit(solution)/shard_map/ppermute | solution.py:622
  6.6 6.4 %collective-permute-start.4 = (bf16[128,1024]{1,0:T(8,128)(2,1)S(1)}, bf16[128,1024]{1,0:T(8,128)(2,1)S(1)}, u32[]{:S(2)}, u32[]{:S(2)}) collective-permute-start(bf16[128,1024]{1,0:T(8,128)(2,1)S(1)} %copy-done.2), channel_id=1, source_target_pairs={{0,2},{1,5},{2,0},{3,7},{4,6},{5,1},{6,4},{7,3},{8,10},{9,13},{10,... | collective-permute-start | bytes 786440 | tf_op jit(solution)/shard_map/ppermute | solution.py:624
  8.0 6.4 %collective-permute-start.2 = (bf16[128,1024]{1,0:T(8,128)(2,1)S(1)}, bf16[128,1024]{1,0:T(8,128)(2,1)S(1)}, u32[]{:S(2)}, u32[]{:S(2)}) collective-permute-start(bf16[128,1024]{1,0:T(8,128)(2,1)S(1)} %copy-done.2), channel_id=1, source_target_pairs={{0,1},{1,0},{2,3},{3,2},{4,5},{5,4},{6,7},{7,6},{8,9},{9,8},{10,11... | collective-permute-start | bytes 786440 | tf_op jit(solution)/shard_map/ppermute | solution.py:24
  8.3 6.2 %collective-permute-start.3 = (bf16[128,1024]{1,0:T(8,128)(2,1)S(1)}, bf16[128,1024]{1,0:T(8,128)(2,1)S(1)}, u32[]{:S(2)}, u32[]{:S(2)}) collective-permute-start(bf16[128,1024]{1,0:T(8,128)(2,1)S(1)} %collective-permute-done.refs_1_.refs_2_), channel_id=1, source_target_pairs={{0,1},{1,0},{2,3},{3,2},{4,5},{5,4},{6,7},{7,6},{8,9},{9,8},{10,11... | collective-permute-start | bytes 786440 | tf_op jit(solution)/shard_map/ppermute | solution.py:24
  13.0 1.5 %collective-permute-start.5 = (bf16[128,1024]{1,0:T(8,128)(2,1)S(1)}, bf16[128,1024]{1,0:T(8,128)(2,1)S(1)}, u32[]{:S(2)}, u32[]{:S(2)}) collective-permute-start(bf16[128,1024]{1,0:T(8,128)(2,1)S(1)} %collective-permute-done.4.refs_3_.refs_4_), channel_id=1, source_target_pairs={{0,1},{1,0},{2,3},{3,2},{4,5},{5,4},{6,7},{7,6},{8,9},{9,8},{10,11... | collective-permute-start | bytes 786440 | tf_op jit(solution)/shard_map/ppermute | solution.py:24
  13.0 6.4 %collective-permute-start.1 = (bf16[128,1024]{1,0:T(8,128)(2,1)S(1)}, bf16[128,1024]{1,0:T(8,128)(2,1)S(1)}, u32[]{:S(2)}, u32[]{:S(2)}) collective-permute-start(bf16[128,1024]{1,0:T(8,128)(2,1)S(1)} %collective-permute-done.refs_1_.refs_2_), channel_id=1, source_target_pairs={{0,2},{1,5},{2,0},{3,7},{4,6},{5,1},{6,4},{7,3},{8,10},{9,13},{10,... | collective-permute-start | bytes 786440 | tf_op jit(solution)/shard_map/ppermute | solution.py:626
  19.4 1.5 %collective-permute-start.6 = (bf16[128,1024]{1,0:T(8,128)(2,1)S(1)}, bf16[128,1024]{1,0:T(8,128)(2,1)S(1)}, u32[]{:S(2)}, u32[]{:S(2)}) collective-permute-start(bf16[128,1024]{1,0:T(8,128)(2,1)S(1)} %collective-permute-done.1.refs_0_.refs_6_), channel_id=1, source_target_pairs={{0,1},{1,0},{2,3},{3,2},{4,5},{5,4},{6,7},{7,6},{8,9},{9,8},{10,11... | collective-permute-start | bytes 786440 | tf_op jit(solution)/shard_map/ppermute | solution.py:24
  19.8 6.6 %copy-start.1 = (bf16[1024,544]{0,1:T(8,128)(2,1)S(1)}, bf16[1024,544]{0,1:T(8,128)(2,1)}, u32[]{:S(2)}) copy-start(bf16[1024,544]{0,1:T(8,128)(2,1)} %param.17) | copy-start | bytes 3342340
  19.9 6.6 %copy-start.4 = (f32[4,1024]{1,0:T(4,128)S(1)}, f32[4,1024]{1,0:T(4,128)}, u32[]{:S(2)}) copy-start(f32[4,1024]{1,0:T(4,128)} %w_ref.9) | copy-start | bytes 49156
  19.9 6.6 %copy-start.5 = (f32[1024]{0:T(1024)S(1)}, f32[1024]{0:T(1024)}, u32[]{:S(2)}) copy-start(f32[1024]{0:T(1024)} %param.16) | copy-start | bytes 12292
  19.9 12.7 %slice-start.4 = ((s8[16777216]{0:T(1024)(128)(4,1)}), s8[4194304]{0:T(1024)(128)(4,1)S(1)}, s32[]{:S(2)}) async-start(s8[16777216]{0:T(1024)(128)(4,1)} %bitcast.11), calls=%async_computation.4 | async-start | bytes 8388608
  19.9 12.7 %slice-start.5 = ((s8[16777216]{0:T(1024)(128)(4,1)}), s8[4194304]{0:T(1024)(128)(4,1)S(1)}, s32[]{:S(2)}) async-start(s8[16777216]{0:T(1024)(128)(4,1)} %bitcast.11), calls=%async_computation.5 | async-start | bytes 8388608
  21.3 11.3 %slice-start.6 = ((s8[16777216]{0:T(1024)(128)(4,1)}), s8[4194304]{0:T(1024)(128)(4,1)S(1)}, s32[]{:S(2)}) async-start(s8[16777216]{0:T(1024)(128)(4,1)} %bitcast.11), calls=%async_computation.6 | async-start | bytes 8388608
  21.3 11.3 %slice-start.7 = ((s8[16777216]{0:T(1024)(128)(4,1)}), s8[4194304]{0:T(1024)(128)(4,1)S(1)}, s32[]{:S(2)}) async-start(s8[16777216]{0:T(1024)(128)(4,1)} %bitcast.11), calls=%async_computation.7 | async-start | bytes 8388608
  21.3 16.6 %copy-start.3 = (f32[1024,16]{0,1:T(8,128)S(1)}, f32[1024,16]{0,1:T(8,128)}, u32[]{:S(2)}) copy-start(f32[1024,16]{0,1:T(8,128)} %param.20) | copy-start | bytes 196612
  21.3 16.6 %copy-start.7 = (bf16[512,1024]{1,0:T(8,128)(2,1)S(1)}, bf16[512,1024]{1,0:T(8,128)(2,1)}, u32[]{:S(2)}) copy-start(bf16[512,1024]{1,0:T(8,128)(2,1)} %refs_3_.1) | copy-start | bytes 3145732
  21.3 16.6 %copy-start.8 = (f32[1024,16]{0,1:T(8,128)S(1)}, f32[1024,16]{0,1:T(8,128)}, u32[]{:S(2)}) copy-start(f32[1024,16]{0,1:T(8,128)} %param.23) | copy-start | bytes 196612
  21.4 16.6 %copy-start.9 = (f32[1024]{0:T(1024)S(1)}, f32[1024]{0:T(1024)}, u32[]{:S(2)}) copy-start(f32[1024]{0:T(1024)} %param.19) | copy-start | bytes 12292
  21.4 5.9 %collective-permute-start.7 = (bf16[8,1024]{1,0:T(8,128)(2,1)S(1)}, bf16[8,1024]{1,0:T(8,128)(2,1)S(1)}, u32[]{:S(2)}, u32[]{:S(2)}) collective-permute-start(bf16[8,1024]{1,0:T(8,128)(2,1)S(1)} %shard_map.135), channel_id=1, source_target_pairs={{0,8},{8,16},{16,24},{1,9},{9,17},{17,25},{2,10},{10,18},{18,26},{... | collective-permute-start | bytes 49160 | tf_op jit(solution)/shard_map/ppermute | solution.py:643
  27.7 1.3 %collective-permute-start.8 = (bf16[64,544]{1,0:T(8,128)(2,1)S(1)}, bf16[64,544]{1,0:T(8,128)(2,1)S(1)}, u32[]{:S(2)}, u32[]{:S(2)}) collective-permute-start(bf16[64,544]{1,0:T(8,128)(2,1)S(1)} %get-tuple-element.46), channel_id=1, source_target_pairs={{0,1},{1,0},{2,3},{3,2},{4,5},{5,4},{6,7},{7,6},{8,9},{9,8},{10,11... | collective-permute-start | bytes 208904 | tf_op jit(solution)/shard_map/ppermute | solution.py:24
  29.1 20.6 %copy-start.6 = (f32[1024]{0:T(1024)S(1)}, f32[1024]{0:T(1024)}, u32[]{:S(2)}) copy-start(f32[1024]{0:T(1024)} %param.21) | copy-start | bytes 12292
  29.1 6.0 %collective-permute-start.11 = (bf16[64,544]{1,0:T(8,128)(2,1)S(1)}, bf16[64,544]{1,0:T(8,128)(2,1)S(1)}, u32[]{:S(2)}, u32[]{:S(2)}) collective-permute-start(bf16[64,544]{1,0:T(8,128)(2,1)S(1)} %shard_map.138.refs_0_), channel_id=1, source_target_pairs={{0,6},{1,7},{2,4},{3,5},{4,2},{5,3},{6,0},{7,1},{8,14},{9,15},{10,... | collective-permute-start | bytes 208904 | tf_op jit(solution)/shard_map/ppermute | solution.py:24
  30.3 6.0 %collective-permute-start.10 = (bf16[64,544]{1,0:T(8,128)(2,1)S(1)}, bf16[64,544]{1,0:T(8,128)(2,1)S(1)}, u32[]{:S(2)}, u32[]{:S(2)}) collective-permute-start(bf16[64,544]{1,0:T(8,128)(2,1)S(1)} %shard_map.138.refs_0_), channel_id=1, source_target_pairs={{0,4},{1,5},{2,6},{3,7},{4,0},{5,1},{6,2},{7,3},{8,12},{9,13},{10,... | collective-permute-start | bytes 208904 | tf_op jit(solution)/shard_map/ppermute | solution.py:24
  32.1 4.4 %collective-permute-start.9 = (bf16[64,544]{1,0:T(8,128)(2,1)S(1)}, bf16[64,544]{1,0:T(8,128)(2,1)S(1)}, u32[]{:S(2)}, u32[]{:S(2)}) collective-permute-start(bf16[64,544]{1,0:T(8,128)(2,1)S(1)} %shard_map.138.refs_0_), channel_id=1, source_target_pairs={{0,2},{1,3},{2,0},{3,1},{4,6},{5,7},{6,4},{7,5},{8,10},{9,11},{10,... | collective-permute-start | bytes 208904 | tf_op jit(solution)/shard_map/ppermute | solution.py:24
  32.6 18.4 %slice-start = ((s8[16777216]{0:T(1024)(128)(4,1)}), s8[4194304]{0:T(1024)(128)(4,1)S(1)}, s32[]{:S(2)}) async-start(s8[16777216]{0:T(1024)(128)(4,1)} %bitcast.9), calls=%async_computation | async-start | bytes 8388608
  32.7 18.4 %slice-start.1 = ((s8[16777216]{0:T(1024)(128)(4,1)}), s8[4194304]{0:T(1024)(128)(4,1)S(1)}, s32[]{:S(2)}) async-start(s8[16777216]{0:T(1024)(128)(4,1)} %bitcast.9), calls=%async_computation.1 | async-start | bytes 8388608
  36.6 1.3 %collective-permute-start.12 = (bf16[64,544]{1,0:T(8,128)(2,1)S(1)}, bf16[64,544]{1,0:T(8,128)(2,1)S(1)}, u32[]{:S(2)}, u32[]{:S(2)}) collective-permute-start(bf16[64,544]{1,0:T(8,128)(2,1)S(1)} %shard_map.140.refs_0_), channel_id=1, source_target_pairs={{0,1},{1,0},{2,3},{3,2},{4,5},{5,4},{6,7},{7,6},{8,9},{9,8},{10,11... | collective-permute-start | bytes 208904 | tf_op jit(solution)/shard_map/ppermute | solution.py:24
  40.4 4.3 %collective-permute-start.13 = (bf16[17,1024]{1,0:T(8,128)(2,1)S(1)}, bf16[17,1024]{1,0:T(8,128)(2,1)S(1)}, u32[]{:S(2)}, u32[]{:S(2)}) collective-permute-start(bf16[17,1024]{1,0:T(8,128)(2,1)S(1)} %get-tuple-element.60), channel_id=1, source_target_pairs={{0,8},{8,0},{16,24},{24,16},{1,9},{9,1},{17,25},{25,17},{2,10},{10... | collective-permute-start | bytes 104456 | tf_op jit(solution)/shard_map/ppermute | solution.py:24
  42.1 9.0 %slice-start.2 = ((s8[16777216]{0:T(1024)(128)(4,1)}), s8[4194304]{0:T(1024)(128)(4,1)S(1)}, s32[]{:S(2)}) async-start(s8[16777216]{0:T(1024)(128)(4,1)} %bitcast.9), calls=%async_computation.2 | async-start | bytes 8388608
  44.8 4.9 %collective-permute-start.14 = (bf16[16,1024]{1,0:T(8,128)(2,1)S(1)}, bf16[16,1024]{1,0:T(8,128)(2,1)S(1)}, u32[]{:S(2)}, u32[]{:S(2)}) collective-permute-start(bf16[16,1024]{1,0:T(8,128)(2,1)S(1)} %get-tuple-element.62), channel_id=1, source_target_pairs={{0,16},{8,24},{16,0},{24,8},{1,17},{9,25},{17,1},{25,9},{2,18},{10... | collective-permute-start | bytes 98312 | tf_op jit(solution)/shard_map/ppermute | solution.py:24
  47.5 3.6 %slice-start.3 = ((s8[16777216]{0:T(1024)(128)(4,1)}), s8[4194304]{0:T(1024)(128)(4,1)S(1)}, s32[]{:S(2)}) async-start(s8[16777216]{0:T(1024)(128)(4,1)} %bitcast.9), calls=%async_computation.3 | async-start | bytes 8388608
  51.8 2.1 %collective-permute-start.16 = (bf16[2,128,1024]{2,1,0:T(8,128)(2,1)S(1)}, bf16[2,128,1024]{2,1,0:T(8,128)(2,1)S(1)}, u32[]{:S(2)}, u32[]{:S(2)}) collective-permute-start(bf16[2,128,1024]{2,1,0:T(8,128)(2,1)S(1)} %shard_map.150), channel_id=1, source_target_pairs={{0,1},{1,0},{2,3},{3,2},{4,5},{5,4},{6,7},{7,6},{8,9},{9,8},{10,11... | collective-permute-start | bytes 1572872 | tf_op jit(solution)/shard_map/ppermute | solution.py:24
  52.7 4.3 %collective-permute-start.15 = (bf16[2,128,1024]{2,1,0:T(8,128)(2,1)S(1)}, bf16[2,128,1024]{2,1,0:T(8,128)(2,1)S(1)}, u32[]{:S(2)}, u32[]{:S(2)}) collective-permute-start(bf16[2,128,1024]{2,1,0:T(8,128)(2,1)S(1)} %shard_map.147), channel_id=1, source_target_pairs={{0,1},{1,0},{2,3},{3,2},{4,5},{5,4},{6,7},{7,6},{8,9},{9,8},{10,11... | collective-permute-start | bytes 1572872 | tf_op jit(solution)/shard_map/ppermute | solution.py:24
  54.1 6.4 %collective-permute-start.18 = (bf16[128,1024]{1,0:T(8,128)(2,1)S(1)}, bf16[128,1024]{1,0:T(8,128)(2,1)S(1)}, u32[]{:S(2)}, u32[]{:S(2)}) collective-permute-start(bf16[128,1024]{1,0:T(8,128)(2,1)S(1)} %get-tuple-element.70), channel_id=1, source_target_pairs={{0,2},{1,5},{2,0},{3,7},{4,6},{5,1},{6,4},{7,3},{8,10},{9,13},{10,... | collective-permute-start | bytes 786440 | tf_op jit(solution)/shard_map/ppermute | solution.py:690
  55.4 8.8 %collective-permute-start.17 = (bf16[128,1024]{1,0:T(8,128)(2,1)S(1)}, bf16[128,1024]{1,0:T(8,128)(2,1)S(1)}, u32[]{:S(2)}, u32[]{:S(2)}) collective-permute-start(bf16[128,1024]{1,0:T(8,128)(2,1)S(1)} %get-tuple-element.68), channel_id=1, source_target_pairs={{0,2},{1,5},{2,0},{3,7},{4,6},{5,1},{6,4},{7,3},{8,10},{9,13},{10,... | collective-permute-start | bytes 786440 | tf_op jit(solution)/shard_map/ppermute | solution.py:691
  60.6 6.4 %collective-permute-start.19 = (bf16[128,1024]{1,0:T(8,128)(2,1)S(1)}, bf16[128,1024]{1,0:T(8,128)(2,1)S(1)}, u32[]{:S(2)}, u32[]{:S(2)}) collective-permute-start(bf16[128,1024]{1,0:T(8,128)(2,1)S(1)} %shard_map.152), channel_id=1, source_target_pairs={{0,4},{1,3},{2,6},{3,1},{4,0},{5,7},{6,2},{7,5},{8,12},{9,11},{10,... | collective-permute-start | bytes 786440 | tf_op jit(solution)/shard_map/ppermute | solution.py:692
